TPU v7x, 512 devices: a whole 4x8x8 slice. The times are simulated.
512 devices in a mesh: table: 64 (over x, y, core), segment: 8 (over z).
Axes of the slice: x: 4, y: 8, z: 8, core: 2. Of those that a mesh axis runs over, the one named last changes fastest.
Arguments:
- hidden: bfloat16 [8, 16384, 1280], P('segment', 'table'), may hold values from -6 to 6
- owner: int32 [8, 16384, 8], P('segment', 'table'), may hold values from 0 to 63, all different within a row; in each aligned block of 256 rows (0 to 255, 256 to 511, ..., all dimensions but the last counted through in order) at most 64 rows name the same one
- slot: int32 [8, 16384, 8], P('segment', 'table'), may hold values from 0 to 127
- memory_table: bfloat16 [8, 8192, 640], P('segment', 'table'), may hold values from -6 to 6
- key_weight: bfloat16 [8, 640, 1280], P('segment'), may hold values from -0.25 to 0.25
- value_weight: bfloat16 [8, 640, 1280], P('segment'), may hold values from -0.25 to 0.25
- conv_weight: float32 [8, 4, 1280], P('segment'), may hold values from -3 to 3
Outputs:
- passed: bfloat16 [8, 16384, 1280], P('segment', 'table')
Inputs may be any that keep to these rules, and one draw needn't show every extreme that they name: `owner`: A token's 8 heads name different shards; among the tokens of one device no shard is named by more than 64 lookups, a bound that some block reaches.
All inputs are finite; a program needn't handle non-finite values.
Results may differ from a plain program's by a relative error of at most 0.0047.
Values may be sent and summed in bfloat16 or wider, within the bound.
No kernel may reach another device: no remote copies, remote signals or barrier semaphores. Data moves between devices by JAX's collectives and lax.ppermute only.
A program may use at most 64 MiB of HBM per device.

v0:
```python
import math

import jax
import jax.numpy as jnp
from jax import lax
from jax.experimental import pallas as pl
from jax.experimental.pallas import tpu as pltpu
from jax.sharding import Mesh, PartitionSpec as P


CONV_DILATION = 3
NX, NY, NC = 4, 8, 2
HALO = 16
TABLE = ("x", "y", "core")


def rotated(value, axis, by):
    count = lax.axis_size(axis)
    return lax.ppermute(value, axis, [(i, (i + by) % count) for i in range(count)])


def rms_scale(values):
    return values * lax.rsqrt(jnp.mean(values * values, axis=-1, keepdims=True) + 1e-06)


def pick_kernel(x_ref, asked_ref, own_ref, other_ref, *, rows_dev):
    lane = lax.broadcasted_iota(jnp.int32, (asked_ref.shape[1], rows_dev), 1)
    for swapped, out_ref in ((0, own_ref), (1, other_ref)):
        for far in range(NY):
            column = swapped * NY + far
            hit = asked_ref[0, :, column : column + 1] == lane
            out_ref[0, :, far * rows_dev : (far + 1) * rows_dev] = hit.astype(jnp.float32).astype(jnp.bfloat16)


def pick_matrices(x, asked, rows_dev):
    groups, rows, columns = asked.shape
    shape = jax.ShapeDtypeStruct((groups, rows, NY * rows_dev), jnp.bfloat16)
    spec = pl.BlockSpec((1, rows, NY * rows_dev), lambda i, x_ref: (i, 0, 0))
    return pl.pallas_call(
        lambda *refs: pick_kernel(*refs, rows_dev=rows_dev),
        grid_spec=pltpu.PrefetchScalarGridSpec(
            num_scalar_prefetch=1,
            grid=(groups,),
            in_specs=[
                pl.BlockSpec((1, rows, columns), lambda i, x_ref: (lax.rem(x_ref[0] - i + groups, groups), 0, 0))
            ],
            out_specs=[spec, spec],
        ),
        out_shape=[shape, shape],
        name="pick_matrices",
    )(x.astype(jnp.int32).reshape(1), asked)


def local(hidden, owner, slot, memory_table, key_weight, value_weight, conv_weight):
    bf16 = jnp.bfloat16
    tok_rows, head_count = owner.shape[1:]
    features = hidden.shape[2]
    rows_dev, row_features = memory_table.shape[1:]
    x, y, core = (lax.axis_index(name) for name in TABLE)
    first = (x == 0) & (y == 0) & (core == 0)

    table = rotated(memory_table[0], "segment", 1)
    numbers = jnp.concatenate([owner[0].T, slot[0].T], axis=0)
    numbers = rotated(numbers, "segment", 1)
    tail = jnp.concatenate(
        [
            hidden[0, tok_rows - HALO :],
            owner[0, tok_rows - HALO :].astype(bf16),
            slot[0, tok_rows - HALO :].astype(bf16),
            jnp.zeros((HALO, 128 - 2 * head_count), bf16),
        ],
        axis=1,
    )
    shards = NX * NY * NC
    sections = lax.axis_size("segment")
    tail = lax.ppermute(
        tail,
        TABLE + ("segment",),
        [
            (i * sections + s, (i + 1) * sections + (s + 1) % sections)
            for i in range(shards - 1)
            for s in range(sections)
        ],
    )
    states = rotated(hidden[0], "segment", 1)
    weight_one = jnp.where(core == 0, key_weight[0], value_weight[0])
    weight_one = rotated(weight_one, "segment", 1)
    weight_two = rotated(weight_one, "core", 1)
    taps = rotated(conv_weight[0], "segment", 1)

    copies = jnp.broadcast_to(table[None], (NY, rows_dev, row_features))
    own_rows = lax.all_to_all(copies, "y", split_axis=0, concat_axis=0, tiled=True)
    own_rows = own_rows.reshape(NY * rows_dev, row_features)
    other_rows = rotated(own_rows, "core", 1)

    head_numbers = tail[:, features : features + 2 * head_count].astype(jnp.int32).T
    numbers = jnp.concatenate([head_numbers, numbers], axis=1)
    place = lax.broadcasted_iota(jnp.int32, (shards, 1), 0)
    ahead, swapped, far = place // (NY * NC), place // NY % NC, place % NY
    shard = (x + ahead) % NX * (NY * NC) + far * NC + (core ^ swapped)
    asked = jnp.full((shards, tok_rows + HALO), -1, jnp.int32)
    for h in range(head_count):
        asked = jnp.maximum(
            asked, jnp.where(numbers[h][None, :] == shard, numbers[head_count + h][None, :], -1)
        )
    asked = asked.reshape(NX, NY * NC, tok_rows + HALO)
    received = [asked[0]]
    for ahead in range(1, NX):
        received.append(rotated(asked[ahead], "x", ahead))
    asked = jnp.stack(received).transpose(0, 2, 1)
    pick_own, pick_other = pick_matrices(x, asked, rows_dev)

    rows = tok_rows + HALO
    other_part = jnp.dot(pick_other.reshape(NX * rows, -1), other_rows, preferred_element_type=jnp.float32)
    own_part = jnp.dot(pick_own.reshape(NX * rows, -1), own_rows, preferred_element_type=jnp.float32)
    partial = (other_part + own_part).astype(bf16).reshape(NX, rows, row_features)
    partial = lax.all_to_all(partial, "x", split_axis=0, concat_axis=0, tiled=True)
    packed = jnp.sum(partial.astype(jnp.float32), axis=0).astype(bf16)

    states_float = jnp.concatenate([tail[:, :features], states], axis=0).astype(jnp.float32)
    one = jnp.dot(packed, weight_one, preferred_element_type=jnp.float32)
    two = jnp.dot(packed, weight_two, preferred_element_type=jnp.float32)
    keys_out = jnp.where(core == 0, one, two)
    values_out = jnp.where(core == 0, two, one)
    affinity = jnp.sum(rms_scale(states_float) * rms_scale(keys_out), axis=-1, keepdims=True) / math.sqrt(features)
    gated = jax.nn.sigmoid(affinity) * values_out
    normed = rms_scale(gated)
    before = lax.broadcasted_iota(jnp.int32, (rows, 1), 0) < HALO
    normed = jnp.where(before & first, 0.0, normed)
    convolved = jnp.zeros((tok_rows, features), jnp.float32)
    for k in range(taps.shape[0]):
        start = HALO - k * CONV_DILATION
        convolved = convolved + taps[k] * normed[start : start + tok_rows]
    branch = jax.nn.silu(convolved) + gated[HALO:]
    return (states_float[HALO:] + branch).astype(bf16)[None]


def solution(mesh):
    grid = Mesh(mesh.devices.reshape(NX, NY, NC, -1), TABLE + ("segment",))
    in_specs = (
        P("segment", TABLE, None),
        P("segment", TABLE, None),
        P("segment", TABLE, None),
        P("segment", TABLE, None),
        P("segment", None, None),
        P("segment", None, None),
        P("segment", None, None),
    )
    out_specs = P("segment", TABLE, None)

    return jax.shard_map(local, mesh=grid, in_specs=in_specs, out_specs=out_specs, check_vma=False)
```

profile of v0, /device:TPU:1, one launch (start us, length us, event | category | flops | bytes accessed | tf_op | source)
XLA Modules:
  0.0 129.3 jit_solution(4723640652744192189)
XLA Ops:
  0.0 4.8 %collective-permute-start.7 = (bf16[128,640]{1,0:T(8,128)(2,1)}, bf16[128,640]{1,0:T(8,128)(2,1)S(1)}, u32[]{:S(2)}, u32[]{:S(2)}) collective-permute-start(bf16[128,640]{1,0:T(8,128)(2,1)} %bitcast.48), channel_id=1, source_target_pairs={{0,1},{1,2},{2,3},{3,4},{4,5},{5,6},{6,7},{7,0},{8,9},{9,10},{10,1... | collective-permute-start | bytes 491528 | tf_op jit(solution)/shard_map/ppermute | solution.py:19
  4.8 10.8 %collective-permute-done.7 = bf16[128,640]{1,0:T(8,128)(2,1)S(1)} collective-permute-done((bf16[128,640]{1,0:T(8,128)(2,1)}, bf16[128,640]{1,0:T(8,128)(2,1)S(1)}, u32[]{:S(2)}, u32[]{:S(2)}) %collective-permute-start.7) | collective-permute-done | bytes 163872 | tf_op jit(solution)/shard_map/ppermute | solution.py:19
  16.8 7.0 %all-to-all-start = ((bf16[8,128,640]{2,1,0:T(8,128)(2,1)}), bf16[8,128,640]{2,1,0:T(8,128)(2,1)}, u32[]{:S(2)}, u32[]{:S(2)}) async-start(bf16[8,128,640]{2,1,0:T(8,128)(2,1)} %broadcast_in_dim.119), calls=%async_computation | async-start | bytes 2621440 | tf_op jit(solution)/shard_map/all_to_all | solution.py:92
  23.7 2.8 %select_bitcast_fusion = bf16[640,1280]{1,0:T(8,128)(2,1)} fusion(bf16[1,640,1280]{2,1,0:T(8,128)(2,1)S(1)} %copy-done.1, bf16[1,640,1280]{2,1,0:T(8,128)(2,1)} %param.12, pred[]{:T(512)S(6)} %eq.62), kind=kLoop, calls=%fused_computation.2 | loop fusion | flops 819200 | bytes 4915201 | tf_op jit(solution)/shard_map/jit(_where)/select_n | solution.py:86
  26.5 1.9 %collective-permute-start.9 = (bf16[640,1280]{1,0:T(8,128)(2,1)}, bf16[640,1280]{1,0:T(8,128)(2,1)}, u32[]{:S(2)}, u32[]{:S(2)}) collective-permute-start(bf16[640,1280]{1,0:T(8,128)(2,1)} %select_bitcast_fusion), channel_id=1, source_target_pairs={{0,1},{1,2},{2,3},{3,4},{4,5},{5,6},{6,7},{7,0},{8,9},{9,10},{10,1... | collective-permute-start | bytes 4915208 | tf_op jit(solution)/shard_map/ppermute | solution.py:19
  29.7 1.9 %collective-permute-start = (bf16[16,1408]{1,0:T(8,128)(2,1)S(1)}, bf16[16,1408]{1,0:T(8,128)(2,1)S(1)}, u32[]{:S(2)}, u32[]{:S(2)}) collective-permute-start(bf16[16,1408]{1,0:T(8,128)(2,1)S(1)} %concatenate.12), channel_id=1, source_target_pairs={{0,9},{1,10},{2,11},{3,12},{4,13},{5,14},{6,15},{7,8},{8,17},{9,18... | collective-permute-start | bytes 135176 | tf_op jit(solution)/shard_map/ppermute | solution.py:76
  31.6 3.8 %collective-permute-start.3 = (s32[16,256]{1,0:T(8,128)S(1)}, s32[16,256]{1,0:T(8,128)S(1)}, u32[]{:S(2)}, u32[]{:S(2)}) collective-permute-start(s32[16,256]{1,0:T(8,128)S(1)} %pad_add_fusion.1), channel_id=1, source_target_pairs={{0,1},{1,2},{2,3},{3,4},{4,5},{5,6},{6,7},{7,0},{8,9},{9,10},{10,1... | collective-permute-start | bytes 49160 | tf_op jit(solution)/shard_map/ppermute | solution.py:19
  35.4 23.2 %all-to-all-done = bf16[8,128,640]{2,1,0:T(8,128)(2,1)} async-done(((bf16[8,128,640]{2,1,0:T(8,128)(2,1)}), bf16[8,128,640]{2,1,0:T(8,128)(2,1)}, u32[]{:S(2)}, u32[]{:S(2)}) %all-to-all-start) | async-done | bytes 1310752 | tf_op jit(solution)/shard_map/all_to_all | solution.py:92
  58.6 2.5 %collective-permute-start.8 = (bf16[1024,640]{1,0:T(8,128)(2,1)}, bf16[1024,640]{1,0:T(8,128)(2,1)S(1)}, u32[]{:S(2)}, u32[]{:S(2)}) collective-permute-start(bf16[1024,640]{1,0:T(8,128)(2,1)} %bitcast.18), channel_id=1, source_target_pairs={{0,8},{8,0},{1,9},{9,1},{2,10},{10,2},{3,11},{11,3},{4,12},{12,4},... | collective-permute-start | bytes 3932168 | tf_op jit(solution)/shard_map/ppermute | solution.py:19
  61.1 7.4 %collective-permute-done = bf16[16,1408]{1,0:T(8,128)(2,1)S(1)} collective-permute-done((bf16[16,1408]{1,0:T(8,128)(2,1)S(1)}, bf16[16,1408]{1,0:T(8,128)(2,1)S(1)}, u32[]{:S(2)}, u32[]{:S(2)}) %collective-permute-start) | collective-permute-done | bytes 45088 | tf_op jit(solution)/shard_map/ppermute | solution.py:76
  69.0 3.1 %collective-permute-start.4 = (s32[16,272]{1,0:T(8,128)S(1)}, s32[16,272]{1,0:T(8,128)S(1)}, u32[]{:S(2)}, u32[]{:S(2)}) collective-permute-start(s32[16,272]{1,0:T(8,128)S(1)} %get-tuple-element.34), channel_id=1, source_target_pairs={{0,128},{128,256},{256,384},{384,0},{1,129},{129,257},{257,385},{3... | collective-permute-start | bytes 52232 | tf_op jit(solution)/shard_map/ppermute | solution.py:19
  72.2 3.9 %collective-permute-start.5 = (s32[16,272]{1,0:T(8,128)S(1)}, s32[16,272]{1,0:T(8,128)S(1)}, u32[]{:S(2)}, u32[]{:S(2)}) collective-permute-start(s32[16,272]{1,0:T(8,128)S(1)} %get-tuple-element.33), channel_id=1, source_target_pairs={{0,256},{128,384},{256,0},{384,128},{1,257},{129,385},{257,1},{385... | collective-permute-start | bytes 52232 | tf_op jit(solution)/shard_map/ppermute | solution.py:19
  76.0 3.5 %collective-permute-start.6 = (s32[16,272]{1,0:T(8,128)S(1)}, s32[16,272]{1,0:T(8,128)S(1)}, u32[]{:S(2)}, u32[]{:S(2)}) collective-permute-start(s32[16,272]{1,0:T(8,128)S(1)} %get-tuple-element.32), channel_id=1, source_target_pairs={{0,384},{128,0},{256,128},{384,256},{1,385},{129,1},{257,129},{385... | collective-permute-start | bytes 52232 | tf_op jit(solution)/shard_map/ppermute | solution.py:19
  79.6 1.9 %collective-permute-start.1 = (bf16[256,1280]{1,0:T(8,128)(2,1)}, bf16[256,1280]{1,0:T(8,128)(2,1)S(1)}, u32[]{:S(2)}, u32[]{:S(2)}) collective-permute-start(bf16[256,1280]{1,0:T(8,128)(2,1)} %bitcast.3), channel_id=1, source_target_pairs={{0,1},{1,2},{2,3},{3,4},{4,5},{5,6},{6,7},{7,0},{8,9},{9,10},{10,1... | collective-permute-start | bytes 1966088 | tf_op jit(solution)/shard_map/ppermute | solution.py:19
  82.6 4.9 %pick_matrices.1 = (bf16[4,272,1024]{2,1,0:T(8,128)(2,1)}, bf16[4,272,1024]{2,1,0:T(8,128)(2,1)}) custom-call(s32[1]{0:T(128)} %bitcast.5.refs_0_, s32[4,272,16]{2,1,0:T(8,128)} %bitcast.40), custom_call_target="tpu_custom_call" | custom-call | tf_op jit(solution)/shard_map/pick_matrices/pallas_call | solution.py:39
  87.5 3.5 %collective-permute-start.10 = (bf16[640,1280]{1,0:T(8,128)(2,1)}, bf16[640,1280]{1,0:T(8,128)(2,1)}, u32[]{:S(2)}, u32[]{:S(2)}) collective-permute-start(bf16[640,1280]{1,0:T(8,128)(2,1)} %collective-permute-done.9), channel_id=1, source_target_pairs={{0,8},{8,0},{1,9},{9,1},{2,10},{10,2},{3,11},{11,3},{4,12},{12,4},... | collective-permute-start | bytes 4915208 | tf_op jit(solution)/shard_map/ppermute | solution.py:19
  91.0 4.0 %fusion.49 = f32[1088,640]{1,0:T(8,128)S(1)} fusion(bf16[1088,1024]{1,0:T(8,128)(2,1)} %bitcast.47, bf16[1024,640]{1,0:T(8,128)(2,1)} %bitcast.18), kind=kOutput, calls=%fused_computation.124 | convolution fusion | flops 1426063360 | bytes 6324224 | tf_op jit(solution)/shard_map/dot_general | solution.py:115
  95.1 3.1 %fusion = bf16[1088,640]{1,0:T(8,128)(2,1)} fusion(f32[1088,640]{1,0:T(8,128)S(1)} %fusion.49, bf16[1088,1024]{1,0:T(8,128)(2,1)S(1)} %bitcast.46, bf16[1024,640]{1,0:T(8,128)(2,1)S(1)} %collective-permute-done.8), kind=kOutput, calls=%fused_computation.1 | convolution fusion | flops 1427456000 | bytes 7716864 | tf_op jit(solution)/shard_map/dot_general | solution.py:114
  98.1 4.2 %all-to-all-start.1 = ((bf16[4,272,640]{2,1,0:T(8,128)(2,1)}), bf16[4,272,640]{2,1,0:T(8,128)(2,1)S(1)}, u32[]{:S(2)}, u32[]{:S(2)}) async-start(bf16[4,272,640]{2,1,0:T(8,128)(2,1)} %bitcast.20), calls=%async_computation.1 | async-start | bytes 2785280 | tf_op jit(solution)/shard_map/all_to_all | solution.py:117
  102.3 1.9 %collective-permute-start.2 = (f32[4,1280]{1,0:T(4,128)S(1)}, f32[4,1280]{1,0:T(4,128)S(1)}, u32[]{:S(2)}, u32[]{:S(2)}) collective-permute-start(f32[4,1280]{1,0:T(4,128)S(1)} %bitcast.49), channel_id=1, source_target_pairs={{0,1},{1,2},{2,3},{3,4},{4,5},{5,6},{6,7},{7,0},{8,9},{9,10},{10,1... | collective-permute-start | bytes 61448 | tf_op jit(solution)/shard_map/ppermute | solution.py:19
  104.2 4.1 %collective-permute-done.2 = f32[4,1280]{1,0:T(4,128)S(1)} collective-permute-done((f32[4,1280]{1,0:T(4,128)S(1)}, f32[4,1280]{1,0:T(4,128)S(1)}, u32[]{:S(2)}, u32[]{:S(2)}) %collective-permute-start.2) | collective-permute-done | bytes 20512 | tf_op jit(solution)/shard_map/ppermute | solution.py:19
  108.7 12.1 %all-to-all-done.1 = bf16[4,272,640]{2,1,0:T(8,128)(2,1)S(1)} async-done(((bf16[4,272,640]{2,1,0:T(8,128)(2,1)}), bf16[4,272,640]{2,1,0:T(8,128)(2,1)S(1)}, u32[]{:S(2)}, u32[]{:S(2)}) %all-to-all-start.1) | async-done | bytes 1392672 | tf_op jit(solution)/shard_map/all_to_all | solution.py:117
  121.9 2.3 %fusion.50 = f32[272,1280]{1,0:T(8,128)S(1)} fusion(bf16[272,640]{1,0:T(8,128)(2,1)} %reduce_sum.49, bf16[640,1280]{1,0:T(8,128)(2,1)} %collective-permute-done.10), kind=kOutput, calls=%fused_computation.125 | convolution fusion | flops 445644800 | bytes 3379200 | tf_op jit(solution)/shard_map/dot_general | solution.py:122
  124.2 2.3 %multiply_reduce_fusion.2 = (f32[272]{0:T(512)S(1)}, f32[272,1280]{1,0:T(8,128)S(1)}) fusion(f32[272,1280]{1,0:T(8,128)S(1)} %fusion.50, pred[]{:T(512)S(6)} %eq.62, bf16[272,640]{1,0:T(8,128)(2,1)S(1)} %copy-done, bf16[640,1280]{1,0:T(8,128)(2,1)} %collective-permute-done.9), kind=kOutput, calls=%fused_computation.7 | convolution fusion | flops 446689024 | bytes 4772929 | tf_op jit(solution)/shard_map/dot_general | solution.py:121
  (52 shorter events, 8.2 us)
Async XLA Ops:
  0.0 15.6 %collective-permute-start.7 = (bf16[128,640]{1,0:T(8,128)(2,1)}, bf16[128,640]{1,0:T(8,128)(2,1)S(1)}, u32[]{:S(2)}, u32[]{:S(2)}) collective-permute-start(bf16[128,640]{1,0:T(8,128)(2,1)} %bitcast.48), channel_id=1, source_target_pairs={{0,1},{1,2},{2,3},{3,4},{4,5},{5,6},{6,7},{7,0},{8,9},{9,10},{10,1... | collective-permute-start | bytes 491528 | tf_op jit(solution)/shard_map/ppermute | solution.py:19
  16.7 7.0 %copy-start.1 = (bf16[1,640,1280]{2,1,0:T(8,128)(2,1)S(1)}, bf16[1,640,1280]{2,1,0:T(8,128)(2,1)}, u32[]{:S(2)}) copy-start(bf16[1,640,1280]{2,1,0:T(8,128)(2,1)} %param.11) | copy-start | bytes 4915204
  16.8 41.9 %all-to-all-start = ((bf16[8,128,640]{2,1,0:T(8,128)(2,1)}), bf16[8,128,640]{2,1,0:T(8,128)(2,1)}, u32[]{:S(2)}, u32[]{:S(2)}) async-start(bf16[8,128,640]{2,1,0:T(8,128)(2,1)} %broadcast_in_dim.119), calls=%async_computation | async-start | bytes 2621440 | tf_op jit(solution)/shard_map/all_to_all | solution.py:92
  23.7 4.8 %copy-start.3 = (s32[1,256,8]{1,2,0:T(8,128)S(1)}, s32[1,256,8]{1,2,0:T(8,128)}, u32[]{:S(2)}) copy-start(s32[1,256,8]{1,2,0:T(8,128)} %param.8) | copy-start | bytes 24580
  23.7 4.9 %copy-start.2 = (s32[1,256,8]{1,2,0:T(8,128)S(1)}, s32[1,256,8]{1,2,0:T(8,128)}, u32[]{:S(2)}) copy-start(s32[1,256,8]{1,2,0:T(8,128)} %param.9) | copy-start | bytes 24580
  26.5 60.9 %collective-permute-start.9 = (bf16[640,1280]{1,0:T(8,128)(2,1)}, bf16[640,1280]{1,0:T(8,128)(2,1)}, u32[]{:S(2)}, u32[]{:S(2)}) collective-permute-start(bf16[640,1280]{1,0:T(8,128)(2,1)} %select_bitcast_fusion), channel_id=1, source_target_pairs={{0,1},{1,2},{2,3},{3,4},{4,5},{5,6},{6,7},{7,0},{8,9},{9,10},{10,1... | collective-permute-start | bytes 4915208 | tf_op jit(solution)/shard_map/ppermute | solution.py:19
  29.7 38.8 %collective-permute-start = (bf16[16,1408]{1,0:T(8,128)(2,1)S(1)}, bf16[16,1408]{1,0:T(8,128)(2,1)S(1)}, u32[]{:S(2)}, u32[]{:S(2)}) collective-permute-start(bf16[16,1408]{1,0:T(8,128)(2,1)S(1)} %concatenate.12), channel_id=1, source_target_pairs={{0,9},{1,10},{2,11},{3,12},{4,13},{5,14},{6,15},{7,8},{8,17},{9,18... | collective-permute-start | bytes 135176 | tf_op jit(solution)/shard_map/ppermute | solution.py:76
  31.6 37.0 %collective-permute-start.3 = (s32[16,256]{1,0:T(8,128)S(1)}, s32[16,256]{1,0:T(8,128)S(1)}, u32[]{:S(2)}, u32[]{:S(2)}) collective-permute-start(s32[16,256]{1,0:T(8,128)S(1)} %pad_add_fusion.1), channel_id=1, source_target_pairs={{0,1},{1,2},{2,3},{3,4},{4,5},{5,6},{6,7},{7,0},{8,9},{9,10},{10,1... | collective-permute-start | bytes 49160 | tf_op jit(solution)/shard_map/ppermute | solution.py:19
  58.6 36.4 %collective-permute-start.8 = (bf16[1024,640]{1,0:T(8,128)(2,1)}, bf16[1024,640]{1,0:T(8,128)(2,1)S(1)}, u32[]{:S(2)}, u32[]{:S(2)}) collective-permute-start(bf16[1024,640]{1,0:T(8,128)(2,1)} %bitcast.18), channel_id=1, source_target_pairs={{0,8},{8,0},{1,9},{9,1},{2,10},{10,2},{3,11},{11,3},{4,12},{12,4},... | collective-permute-start | bytes 3932168 | tf_op jit(solution)/shard_map/ppermute | solution.py:19
  69.0 10.6 %collective-permute-start.4 = (s32[16,272]{1,0:T(8,128)S(1)}, s32[16,272]{1,0:T(8,128)S(1)}, u32[]{:S(2)}, u32[]{:S(2)}) collective-permute-start(s32[16,272]{1,0:T(8,128)S(1)} %get-tuple-element.34), channel_id=1, source_target_pairs={{0,128},{128,256},{256,384},{384,0},{1,129},{129,257},{257,385},{3... | collective-permute-start | bytes 52232 | tf_op jit(solution)/shard_map/ppermute | solution.py:19
  72.2 9.4 %collective-permute-start.5 = (s32[16,272]{1,0:T(8,128)S(1)}, s32[16,272]{1,0:T(8,128)S(1)}, u32[]{:S(2)}, u32[]{:S(2)}) collective-permute-start(s32[16,272]{1,0:T(8,128)S(1)} %get-tuple-element.33), channel_id=1, source_target_pairs={{0,256},{128,384},{256,0},{384,128},{1,257},{129,385},{257,1},{385... | collective-permute-start | bytes 52232 | tf_op jit(solution)/shard_map/ppermute | solution.py:19
  76.0 5.5 %collective-permute-start.6 = (s32[16,272]{1,0:T(8,128)S(1)}, s32[16,272]{1,0:T(8,128)S(1)}, u32[]{:S(2)}, u32[]{:S(2)}) collective-permute-start(s32[16,272]{1,0:T(8,128)S(1)} %get-tuple-element.32), channel_id=1, source_target_pairs={{0,384},{128,0},{256,128},{384,256},{1,385},{129,1},{257,129},{385... | collective-permute-start | bytes 52232 | tf_op jit(solution)/shard_map/ppermute | solution.py:19
  79.6 28.8 %collective-permute-start.1 = (bf16[256,1280]{1,0:T(8,128)(2,1)}, bf16[256,1280]{1,0:T(8,128)(2,1)S(1)}, u32[]{:S(2)}, u32[]{:S(2)}) collective-permute-start(bf16[256,1280]{1,0:T(8,128)(2,1)} %bitcast.3), channel_id=1, source_target_pairs={{0,1},{1,2},{2,3},{3,4},{4,5},{5,6},{6,7},{7,0},{8,9},{9,10},{10,1... | collective-permute-start | bytes 1966088 | tf_op jit(solution)/shard_map/ppermute | solution.py:19
  87.5 34.4 %collective-permute-start.10 = (bf16[640,1280]{1,0:T(8,128)(2,1)}, bf16[640,1280]{1,0:T(8,128)(2,1)}, u32[]{:S(2)}, u32[]{:S(2)}) collective-permute-start(bf16[640,1280]{1,0:T(8,128)(2,1)} %collective-permute-done.9), channel_id=1, source_target_pairs={{0,8},{8,0},{1,9},{9,1},{2,10},{10,2},{3,11},{11,3},{4,12},{12,4},... | collective-permute-start | bytes 4915208 | tf_op jit(solution)/shard_map/ppermute | solution.py:19
  91.0 4.1 %copy-start.4 = (bf16[4,272,1024]{2,1,0:T(8,128)(2,1)S(1)}, bf16[4,272,1024]{2,1,0:T(8,128)(2,1)}, u32[]{:S(2)}) copy-start(bf16[4,272,1024]{2,1,0:T(8,128)(2,1)} %get-tuple-element.7) | copy-start | bytes 6684676
  98.1 4.2 %copy-start.5 = (f32[1,4,1280]{2,1,0:T(4,128)S(1)}, f32[1,4,1280]{2,1,0:T(4,128)}, u32[]{:S(2)}) copy-start(f32[1,4,1280]{2,1,0:T(4,128)} %param.13) | copy-start | bytes 61444
  98.1 22.8 %all-to-all-start.1 = ((bf16[4,272,640]{2,1,0:T(8,128)(2,1)}), bf16[4,272,640]{2,1,0:T(8,128)(2,1)S(1)}, u32[]{:S(2)}, u32[]{:S(2)}) async-start(bf16[4,272,640]{2,1,0:T(8,128)(2,1)} %bitcast.20), calls=%async_computation.1 | async-start | bytes 2785280 | tf_op jit(solution)/shard_map/all_to_all | solution.py:117
  102.3 6.0 %collective-permute-start.2 = (f32[4,1280]{1,0:T(4,128)S(1)}, f32[4,1280]{1,0:T(4,128)S(1)}, u32[]{:S(2)}, u32[]{:S(2)}) collective-permute-start(f32[4,1280]{1,0:T(4,128)S(1)} %bitcast.49), channel_id=1, source_target_pairs={{0,1},{1,2},{2,3},{3,4},{4,5},{5,6},{6,7},{7,0},{8,9},{9,10},{10,1... | collective-permute-start | bytes 61448 | tf_op jit(solution)/shard_map/ppermute | solution.py:19
  121.9 2.3 %copy-start = (bf16[272,640]{1,0:T(8,128)(2,1)S(1)}, bf16[272,640]{1,0:T(8,128)(2,1)}, u32[]{:S(2)}) copy-start(bf16[272,640]{1,0:T(8,128)(2,1)} %reduce_sum.49) | copy-start | bytes 1044484
where the time goes:
time: 130 us; the launch traced here: 129 us
  waiting for transfers between devices  57.6 us (44%)
  starting transfers between devices  43.9 us (34%)
  matrix products  11.7 us (9%)
  other arithmetic  7.54 us (6%)
  Pallas kernels  4.87 us (4%)
  local copies, waits for them, and re-layouts  3.42 us (3%)
    ppermute x10, starting transfers between devices, rotated(): lax.ppermute(value, axis, [(i, (i + by) % count) for i in range(count)])  30.9 us
    all_to_all x1, waiting for transfers between devices, local(): lax.all_to_all(copies, 'y', split_axis=0, concat_axis=0, tiled=True)  23.2 us
    ppermute x10, waiting for transfers between devices, rotated(): lax.ppermute(value, axis, [(i, (i + by) % count) for i in range(count)])  14.9 us
    all_to_all x1, waiting for transfers between devices, local(): lax.all_to_all(partial, 'x', split_axis=0, concat_axis=0, tiled=True)  12.1 us
    ppermute x1, waiting for transfers between devices, local(): lax.ppermute(tail, TABLE + ('segment',), [(i * sections + s, (i + 1) * se...  7.39 us
    all_to_all x1, starting transfers between devices, local(): lax.all_to_all(copies, 'y', split_axis=0, concat_axis=0, tiled=True)  6.95 us
    pallas_call x1, Pallas kernels, pick_matrices(): pl.pallas_call(lambda *refs: pick_kernel(*refs, rows_dev=rows_dev), grid_...  4.87 us
    all_to_all x1, starting transfers between devices, local(): lax.all_to_all(partial, 'x', split_axis=0, concat_axis=0, tiled=True)  4.17 us
  transfers between devices with their start and end apart: 13, of which 5 were waited for; matrix products, arithmetic and copies ran while one was open for 11% of the time, Pallas kernels for 4%

commit v1 on v0

v1 whole, which is shorter than its diff:
```python
import math

import jax
import jax.numpy as jnp
from jax import lax
from jax.experimental import pallas as pl
from jax.experimental.pallas import tpu as pltpu
from jax.sharding import Mesh, PartitionSpec as P


CONV_DILATION = 3
NX, NY, NC = 4, 8, 2
HALO = 16
TABLE = ("x", "y", "core")


def rotated(value, axis, by):
    count = lax.axis_size(axis)
    return lax.ppermute(value, axis, [(i, (i + by) % count) for i in range(count)])


VMEM = pl.BlockSpec(memory_space=pltpu.VMEM)
SMEM = pl.BlockSpec(memory_space=pltpu.SMEM)


def pick_matrices(x, asked, rows_dev):
    groups, rows, _ = asked.shape

    def body(x_ref, asked_ref, own_ref, other_ref):
        lane = lax.broadcasted_iota(jnp.int32, (rows, rows_dev), 1)
        for group in range(groups):
            source = lax.rem(x_ref[0] - group + groups, groups)
            for swapped, out_ref in ((0, own_ref), (1, other_ref)):
                for far in range(NY):
                    column = swapped * NY + far
                    hit = asked_ref[source, :, column : column + 1] == lane
                    hit = hit.astype(jnp.float32).astype(jnp.bfloat16)
                    out_ref[group, :, far * rows_dev : (far + 1) * rows_dev] = hit

    shape = jax.ShapeDtypeStruct((groups, rows, NY * rows_dev), jnp.bfloat16)
    return pl.pallas_call(
        body,
        in_specs=[SMEM, VMEM],
        out_specs=[VMEM, VMEM],
        out_shape=[shape, shape],
        name="pick_matrices",
    )(x, asked)


def dot_own(pick, table_rows):
    groups, rows, _ = pick.shape

    def body(pick_ref, rows_ref, out_ref):
        for group in range(groups):
            out_ref[group] = jnp.dot(pick_ref[group], rows_ref[...], preferred_element_type=jnp.float32)

    return pl.pallas_call(
        body,
        in_specs=[VMEM, VMEM],
        out_specs=VMEM,
        out_shape=jax.ShapeDtypeStruct((groups, rows, table_rows.shape[1]), jnp.float32),
        name="dot_own",
    )(pick, table_rows)


def dot_other(pick, table_rows, own):
    def body(pick_ref, rows_ref, own_ref, out_ref):
        for group in range(own.shape[0]):
            total = jnp.dot(pick_ref[group], rows_ref[...], preferred_element_type=jnp.float32)
            out_ref[group] = (own_ref[group] + total).astype(jnp.bfloat16)

    return pl.pallas_call(
        body,
        in_specs=[VMEM, VMEM, VMEM],
        out_specs=VMEM,
        out_shape=jax.ShapeDtypeStruct(own.shape, jnp.bfloat16),
        name="dot_other",
    )(pick, table_rows, own)


def dense(place, sums, tail, hidden, weight_one, weight_two, taps):
    chunk, features = hidden.shape
    rows = chunk + HALO

    def body(place_ref, sums_ref, tail_ref, hidden_ref, one_ref, two_ref, taps_ref, out_ref, product_ref, normed_ref):
        total = sums_ref[0].astype(jnp.float32)
        for group in range(1, sums_ref.shape[0]):
            total = total + sums_ref[group].astype(jnp.float32)
        packed = total.astype(jnp.bfloat16)
        core = place_ref[1]
        product_ref[core] = jnp.dot(packed, one_ref[...], preferred_element_type=jnp.float32)
        product_ref[1 - core] = jnp.dot(packed, two_ref[...], preferred_element_type=jnp.float32)
        states = jnp.concatenate([tail_ref[:, :features], hidden_ref[...]], axis=0).astype(jnp.float32)
        keys = product_ref[0]
        mean_states = jnp.mean(states * states, axis=-1, keepdims=True)
        mean_keys = jnp.mean(keys * keys, axis=-1, keepdims=True)
        affinity = jnp.sum(states * keys, axis=-1, keepdims=True)
        affinity = affinity * lax.rsqrt(mean_states + 1e-06) * lax.rsqrt(mean_keys + 1e-06) / math.sqrt(features)
        gated = jax.nn.sigmoid(affinity) * product_ref[1]
        product_ref[1] = gated
        scale = lax.rsqrt(jnp.mean(gated * gated, axis=-1, keepdims=True) + 1e-06)
        normed_ref[...] = gated * scale
        normed_ref[:HALO] = jnp.where(place_ref[0] > 0, normed_ref[:HALO], 0.0)
        convolved = taps_ref[0:1] * normed_ref[HALO:]
        for k in range(1, taps_ref.shape[0]):
            at = HALO - k * CONV_DILATION
            convolved = convolved + taps_ref[k : k + 1] * normed_ref[at : at + chunk]
        branch = convolved * jax.nn.sigmoid(convolved) + product_ref[1, HALO:]
        out_ref[...] = (hidden_ref[...].astype(jnp.float32) + branch).astype(jnp.bfloat16)

    return pl.pallas_call(
        body,
        in_specs=[SMEM] + [VMEM] * 6,
        out_specs=VMEM,
        out_shape=jax.ShapeDtypeStruct((chunk, features), jnp.bfloat16),
        scratch_shapes=[
            pltpu.VMEM((2, rows, features), jnp.float32),
            pltpu.VMEM((rows, features), jnp.float32),
        ],
        name="dense",
    )(place, sums, tail, hidden, weight_one, weight_two, taps)


def local(hidden, owner, slot, memory_table, key_weight, value_weight, conv_weight):
    bf16 = jnp.bfloat16
    tok_rows, head_count = owner.shape[1:]
    features = hidden.shape[2]
    rows_dev, row_features = memory_table.shape[1:]
    x, y, core = (lax.axis_index(name) for name in TABLE)

    table = rotated(memory_table[0], "segment", 1)
    numbers = jnp.concatenate([owner[0].T, slot[0].T], axis=0)
    numbers = rotated(numbers, "segment", 1)
    tail = jnp.concatenate(
        [
            hidden[0, tok_rows - HALO :],
            owner[0, tok_rows - HALO :].astype(bf16),
            slot[0, tok_rows - HALO :].astype(bf16),
            jnp.zeros((HALO, 128 - 2 * head_count), bf16),
        ],
        axis=1,
    )
    shards = NX * NY * NC
    sections = lax.axis_size("segment")
    tail = lax.ppermute(
        tail,
        TABLE + ("segment",),
        [
            (i * sections + s, (i + 1) * sections + (s + 1) % sections)
            for i in range(shards - 1)
            for s in range(sections)
        ],
    )
    states = rotated(hidden[0], "segment", 1)
    weight_one = jnp.where(core == 0, key_weight[0], value_weight[0])
    weight_one = rotated(weight_one, "segment", 1)
    weight_two = rotated(weight_one, "core", 1)
    taps = rotated(conv_weight[0], "segment", 1)

    copies = jnp.broadcast_to(table[None], (NY, rows_dev, row_features))
    own_rows = lax.all_to_all(copies, "y", split_axis=0, concat_axis=0, tiled=True)
    own_rows = own_rows.reshape(NY * rows_dev, row_features)
    other_rows = rotated(own_rows, "core", 1)

    head_numbers = tail[:, features : features + 2 * head_count].astype(jnp.int32).T
    numbers = jnp.concatenate([head_numbers, numbers], axis=1)
    place = lax.broadcasted_iota(jnp.int32, (shards, 1), 0)
    ahead, swapped, far = place // (NY * NC), place // NY % NC, place % NY
    shard = (x + ahead) % NX * (NY * NC) + far * NC + (core ^ swapped)
    asked = jnp.full((shards, tok_rows + HALO), -1, jnp.int32)
    for h in range(head_count):
        asked = jnp.maximum(
            asked, jnp.where(numbers[h][None, :] == shard, numbers[head_count + h][None, :], -1)
        )
    asked = asked.reshape(NX, NY * NC, tok_rows + HALO)
    received = [asked[0]]
    for ahead in range(1, NX):
        received.append(rotated(asked[ahead], "x", ahead))
    asked = jnp.stack(received).transpose(0, 2, 1)
    pick_own, pick_other = pick_matrices(x.astype(jnp.int32).reshape(1), asked, rows_dev)

    own_part = dot_own(pick_own, own_rows)
    sums = dot_other(pick_other, other_rows, own_part)
    sums = lax.all_to_all(sums, "x", split_axis=0, concat_axis=0, tiled=True)
    later = (x > 0) | (y > 0) | (core > 0)
    place = jnp.stack([later.astype(jnp.int32), core.astype(jnp.int32)])
    return dense(place, sums, tail, states, weight_one, weight_two, taps)[None]


def solution(mesh):
    grid = Mesh(mesh.devices.reshape(NX, NY, NC, -1), TABLE + ("segment",))
    in_specs = (
        P("segment", TABLE, None),
        P("segment", TABLE, None),
        P("segment", TABLE, None),
        P("segment", TABLE, None),
        P("segment", None, None),
        P("segment", None, None),
        P("segment", None, None),
    )
    out_specs = P("segment", TABLE, None)

    return jax.shard_map(local, mesh=grid, in_specs=in_specs, out_specs=out_specs, check_vma=False)
```

time: 130 us -> 133 us (1.023)
  the two profiles are of different devices: /device:TPU:1 before, /device:TPU:18 now
where the time goes in v1:
time: 133 us; the launch traced here: 132 us
  waiting for transfers between devices  59.7 us (45%)
  starting transfers between devices  41.9 us (32%)
  Pallas kernels  22.9 us (17%)
  local copies, waits for them, and re-layouts  5.03 us (4%)
  other arithmetic  2.57 us (2%)
    ppermute x10, waiting for transfers between devices, rotated(): lax.ppermute(value, axis, [(i, (i + by) % count) for i in range(count)])  32.4 us
    all_to_all x1, waiting for transfers between devices, local(): lax.all_to_all(copies, 'y', split_axis=0, concat_axis=0, tiled=True)  27.3 us
    ppermute x10, starting transfers between devices, rotated(): lax.ppermute(value, axis, [(i, (i + by) % count) for i in range(count)])  26.2 us
    all_to_all x1, starting transfers between devices, local(): lax.all_to_all(copies, 'y', split_axis=0, concat_axis=0, tiled=True)  7.56 us
    pallas_call x1, Pallas kernels, dense(): pl.pallas_call(body, in_specs=[SMEM] + [VMEM] * 6, out_specs=VMEM, out_sh...  6.29 us
    all_to_all x1, starting transfers between devices, local(): sums = lax.all_to_all(sums, 'x', split_axis=0, concat_axis=0, tiled=True)  6.19 us
    pallas_call x1, Pallas kernels, dot_other(): pl.pallas_call(body, in_specs=[VMEM, VMEM, VMEM], out_specs=VMEM, out_sha...  5.87 us
    pallas_call x1, Pallas kernels, dot_own(): pl.pallas_call(body, in_specs=[VMEM, VMEM], out_specs=VMEM, out_shape=jax...  5.44 us
  transfers between devices with their start and end apart: 13, of which 6 were waited for; matrix products, arithmetic and copies ran while one was open for 4% of the time, Pallas kernels for 13%

profile of v1, /device:TPU:18, one launch (start us, length us, event | category | flops | bytes accessed | tf_op | source)
XLA Modules:
  0.0 132.3 jit_solution(11555936301475566292)
XLA Ops:
  0.0 4.3 %collective-permute-start.5 = (bf16[128,640]{1,0:T(8,128)(2,1)}, bf16[128,640]{1,0:T(8,128)(2,1)S(1)}, u32[]{:S(2)}, u32[]{:S(2)}) collective-permute-start(bf16[128,640]{1,0:T(8,128)(2,1)} %bitcast.39), channel_id=1, source_target_pairs={{0,1},{1,2},{2,3},{3,4},{4,5},{5,6},{6,7},{7,0},{8,9},{9,10},{10,1... | collective-permute-start | bytes 491528 | tf_op jit(solution)/shard_map/ppermute | solution.py:19
  4.3 11.1 %collective-permute-done.5 = bf16[128,640]{1,0:T(8,128)(2,1)S(1)} collective-permute-done((bf16[128,640]{1,0:T(8,128)(2,1)}, bf16[128,640]{1,0:T(8,128)(2,1)S(1)}, u32[]{:S(2)}, u32[]{:S(2)}) %collective-permute-start.5) | collective-permute-done | bytes 163872 | tf_op jit(solution)/shard_map/ppermute | solution.py:19
  15.3 1.2 broadcast_in_dim.101
  16.5 7.6 %all-to-all-start = ((bf16[8,128,640]{2,1,0:T(8,128)(2,1)}), bf16[8,128,640]{2,1,0:T(8,128)(2,1)S(1)}, u32[]{:S(2)}, u32[]{:S(2)}) async-start(bf16[8,128,640]{2,1,0:T(8,128)(2,1)} %broadcast_in_dim.101), calls=%async_computation | async-start | bytes 2621440 | tf_op jit(solution)/shard_map/all_to_all | solution.py:161
  24.1 1.4 %select_bitcast_fusion = bf16[640,1280]{1,0:T(8,128)(2,1)} fusion(bf16[1,640,1280]{2,1,0:T(8,128)(2,1)S(1)} %copy-done.2, bf16[1,640,1280]{2,1,0:T(8,128)(2,1)} %param.12, pred[]{:T(512)S(6)} %eq.138), kind=kLoop, calls=%fused_computation | loop fusion | flops 819200 | bytes 4915201 | tf_op jit(solution)/shard_map/jit(_where)/select_n | solution.py:155
  25.5 1.9 %collective-permute-start.8 = (bf16[640,1280]{1,0:T(8,128)(2,1)}, bf16[640,1280]{1,0:T(8,128)(2,1)S(1)}, u32[]{:S(2)}, u32[]{:S(2)}) collective-permute-start(bf16[640,1280]{1,0:T(8,128)(2,1)} %select_bitcast_fusion), channel_id=1, source_target_pairs={{0,1},{1,2},{2,3},{3,4},{4,5},{5,6},{6,7},{7,0},{8,9},{9,10},{10,1... | collective-permute-start | bytes 4915208 | tf_op jit(solution)/shard_map/ppermute | solution.py:19
  27.7 27.3 %all-to-all-done = bf16[8,128,640]{2,1,0:T(8,128)(2,1)S(1)} async-done(((bf16[8,128,640]{2,1,0:T(8,128)(2,1)}), bf16[8,128,640]{2,1,0:T(8,128)(2,1)S(1)}, u32[]{:S(2)}, u32[]{:S(2)}) %all-to-all-start) | async-done | bytes 1310752 | tf_op jit(solution)/shard_map/all_to_all | solution.py:161
  55.0 1.9 %collective-permute-start.6 = (bf16[1024,640]{1,0:T(8,128)(2,1)S(1)}, bf16[1024,640]{1,0:T(8,128)(2,1)}, u32[]{:S(2)}, u32[]{:S(2)}) collective-permute-start(bf16[1024,640]{1,0:T(8,128)(2,1)S(1)} %bitcast.30), channel_id=1, source_target_pairs={{0,8},{8,0},{1,9},{9,1},{2,10},{10,2},{3,11},{11,3},{4,12},{12,4},... | collective-permute-start | bytes 3932168 | tf_op jit(solution)/shard_map/ppermute | solution.py:19
  57.9 1.9 %collective-permute-start = (bf16[16,1408]{1,0:T(8,128)(2,1)S(1)}, bf16[16,1408]{1,0:T(8,128)(2,1)S(1)}, u32[]{:S(2)}, u32[]{:S(2)}) collective-permute-start(bf16[16,1408]{1,0:T(8,128)(2,1)S(1)} %concatenate.9), channel_id=1, source_target_pairs={{0,9},{1,10},{2,11},{3,12},{4,13},{5,14},{6,15},{7,8},{8,17},{9,18... | collective-permute-start | bytes 135176 | tf_op jit(solution)/shard_map/ppermute | solution.py:145
  59.8 1.9 %collective-permute-start.1 = (s32[16,256]{1,0:T(8,128)S(1)}, s32[16,256]{1,0:T(8,128)S(1)}, u32[]{:S(2)}, u32[]{:S(2)}) collective-permute-start(s32[16,256]{1,0:T(8,128)S(1)} %pad_add_fusion.1), channel_id=1, source_target_pairs={{0,1},{1,2},{2,3},{3,4},{4,5},{5,6},{6,7},{7,0},{8,9},{9,10},{10,1... | collective-permute-start | bytes 49160 | tf_op jit(solution)/shard_map/ppermute | solution.py:19
  61.7 5.5 %collective-permute-done.8.one_ref = bf16[640,1280]{1,0:T(8,128)(2,1)S(1)} collective-permute-done((bf16[640,1280]{1,0:T(8,128)(2,1)}, bf16[640,1280]{1,0:T(8,128)(2,1)S(1)}, u32[]{:S(2)}, u32[]{:S(2)}) %collective-permute-start.8) | collective-permute-done | bytes 1638432 | tf_op jit(solution)/shard_map/ppermute | solution.py:19
  67.3 1.9 %collective-permute-start.9 = (bf16[640,1280]{1,0:T(8,128)(2,1)S(1)}, bf16[640,1280]{1,0:T(8,128)(2,1)}, u32[]{:S(2)}, u32[]{:S(2)}) collective-permute-start(bf16[640,1280]{1,0:T(8,128)(2,1)S(1)} %collective-permute-done.8.one_ref), channel_id=1, source_target_pairs={{0,8},{8,0},{1,9},{9,1},{2,10},{10,2},{3,11},{11,3},{4,12},{12,4},... | collective-permute-start | bytes 4915208 | tf_op jit(solution)/shard_map/ppermute | solution.py:19
  69.7 3.4 %collective-permute-start.2 = (s32[16,272]{1,0:T(8,128)S(1)}, s32[16,272]{1,0:T(8,128)S(1)}, u32[]{:S(2)}, u32[]{:S(2)}) collective-permute-start(s32[16,272]{1,0:T(8,128)S(1)} %get-tuple-element.28), channel_id=1, source_target_pairs={{0,128},{128,256},{256,384},{384,0},{1,129},{129,257},{257,385},{3... | collective-permute-start | bytes 52232 | tf_op jit(solution)/shard_map/ppermute | solution.py:19
  73.1 3.0 %collective-permute-start.3 = (s32[16,272]{1,0:T(8,128)S(1)}, s32[16,272]{1,0:T(8,128)S(1)}, u32[]{:S(2)}, u32[]{:S(2)}) collective-permute-start(s32[16,272]{1,0:T(8,128)S(1)} %get-tuple-element.27), channel_id=1, source_target_pairs={{0,256},{128,384},{256,0},{384,128},{1,257},{129,385},{257,1},{385... | collective-permute-start | bytes 52232 | tf_op jit(solution)/shard_map/ppermute | solution.py:19
  76.2 4.1 %collective-permute-start.4 = (s32[16,272]{1,0:T(8,128)S(1)}, s32[16,272]{1,0:T(8,128)S(1)}, u32[]{:S(2)}, u32[]{:S(2)}) collective-permute-start(s32[16,272]{1,0:T(8,128)S(1)} %get-tuple-element.26), channel_id=1, source_target_pairs={{0,384},{128,0},{256,128},{384,256},{1,385},{129,1},{257,129},{385... | collective-permute-start | bytes 52232 | tf_op jit(solution)/shard_map/ppermute | solution.py:19
  80.4 1.5 %collective-permute-done.4 = s32[16,272]{1,0:T(8,128)S(1)} collective-permute-done((s32[16,272]{1,0:T(8,128)S(1)}, s32[16,272]{1,0:T(8,128)S(1)}, u32[]{:S(2)}, u32[]{:S(2)}) %collective-permute-start.4) | collective-permute-done | bytes 17440 | tf_op jit(solution)/shard_map/ppermute | solution.py:19
  82.9 5.3 %pick_matrices.1 = (bf16[4,272,1024]{2,1,0:T(8,128)(2,1)}, bf16[4,272,1024]{2,1,0:T(8,128)(2,1)}) custom-call(s32[1]{0:T(128)} %bitcast.2.x_ref, s32[4,272,16]{2,1,0:T(8,128)} %bitcast.32), custom_call_target="tpu_custom_call" | custom-call | tf_op jit(solution)/shard_map/pick_matrices/pallas_call | solution.py:41
  88.2 5.4 %dot_own.1.own_ref = f32[4,272,640]{2,1,0:T(8,128)} custom-call(bf16[4,272,1024]{2,1,0:T(8,128)(2,1)} %get-tuple-element.8.pick_ref, bf16[1024,640]{1,0:T(8,128)(2,1)} %bitcast.31), custom_call_target="tpu_custom_call" | custom-call | tf_op jit(solution)/shard_map/dot_own/pallas_call | solution.py:57
  93.7 5.9 %dot_other.1 = bf16[4,272,640]{2,1,0:T(8,128)(2,1)} custom-call(bf16[4,272,1024]{2,1,0:T(8,128)(2,1)} %get-tuple-element.7.pick_ref, bf16[1024,640]{1,0:T(8,128)(2,1)} %collective-permute-done.6.rows_ref, f32[4,272,640]{2,1,0:T(8,128)} %dot_own.1.own_ref), custom_call_target="tpu_custom_call" | custom-call | tf_op jit(solution)/shard_map/dot_other/pallas_call | solution.py:72
  99.5 6.2 %all-to-all-start.1 = ((bf16[4,272,640]{2,1,0:T(8,128)(2,1)}), bf16[4,272,640]{2,1,0:T(8,128)(2,1)S(1)}, u32[]{:S(2)}, u32[]{:S(2)}) async-start(bf16[4,272,640]{2,1,0:T(8,128)(2,1)} %dot_other.1), calls=%async_computation.1 | async-start | bytes 2785280 | tf_op jit(solution)/shard_map/all_to_all | solution.py:184
  105.7 1.9 %collective-permute-start.7 = (bf16[256,1280]{1,0:T(8,128)(2,1)}, bf16[256,1280]{1,0:T(8,128)(2,1)}, u32[]{:S(2)}, u32[]{:S(2)}) collective-permute-start(bf16[256,1280]{1,0:T(8,128)(2,1)} %bitcast.38), channel_id=1, source_target_pairs={{0,1},{1,2},{2,3},{3,4},{4,5},{5,6},{6,7},{7,0},{8,9},{9,10},{10,1... | collective-permute-start | bytes 1966088 | tf_op jit(solution)/shard_map/ppermute | solution.py:19
  107.7 1.9 %collective-permute-start.10 = (f32[4,1280]{1,0:T(4,128)S(1)}, f32[4,1280]{1,0:T(4,128)S(1)}, u32[]{:S(2)}, u32[]{:S(2)}) collective-permute-start(f32[4,1280]{1,0:T(4,128)S(1)} %bitcast.40), channel_id=1, source_target_pairs={{0,1},{1,2},{2,3},{3,4},{4,5},{5,6},{6,7},{7,0},{8,9},{9,10},{10,1... | collective-permute-start | bytes 61448 | tf_op jit(solution)/shard_map/ppermute | solution.py:19
  110.2 14.1 %collective-permute-done.10.taps_ref = f32[4,1280]{1,0:T(4,128)S(1)} collective-permute-done((f32[4,1280]{1,0:T(4,128)S(1)}, f32[4,1280]{1,0:T(4,128)S(1)}, u32[]{:S(2)}, u32[]{:S(2)}) %collective-permute-start.10) | collective-permute-done | bytes 20512 | tf_op jit(solution)/shard_map/ppermute | solution.py:19
  126.0 6.3 %dense.1 = bf16[256,1280]{1,0:T(8,128)(2,1)} custom-call(s32[2]{0:T(128)} %pad_add_fusion.3.place_ref, bf16[4,272,640]{2,1,0:T(8,128)(2,1)} %copy-done, bf16[16,1408]{1,0:T(8,128)(2,1)} %copy-done.4, bf16[256,1280]{1,0:T(8,128)(2,1)} %collective-permute-done.7.hidden_ref, bf16[640,1280]{1,0:T(8,128)(2,1)} %copy-done.3, ...), custom_call_target="tpu_custom_call" | custom-call | tf_op jit(solution)/shard_map/dense/pallas_call | solution.py:111
  (44 shorter events, 5.2 us)
Async XLA Ops:
  0.0 15.3 %collective-permute-start.5 = (bf16[128,640]{1,0:T(8,128)(2,1)}, bf16[128,640]{1,0:T(8,128)(2,1)S(1)}, u32[]{:S(2)}, u32[]{:S(2)}) collective-permute-start(bf16[128,640]{1,0:T(8,128)(2,1)} %bitcast.39), channel_id=1, source_target_pairs={{0,1},{1,2},{2,3},{3,4},{4,5},{5,6},{6,7},{7,0},{8,9},{9,10},{10,1... | collective-permute-start | bytes 491528 | tf_op jit(solution)/shard_map/ppermute | solution.py:19
  16.5 7.6 %copy-start.2 = (bf16[1,640,1280]{2,1,0:T(8,128)(2,1)S(1)}, bf16[1,640,1280]{2,1,0:T(8,128)(2,1)}, u32[]{:S(2)}) copy-start(bf16[1,640,1280]{2,1,0:T(8,128)(2,1)} %param.11) | copy-start | bytes 4915204
  16.5 38.5 %all-to-all-start = ((bf16[8,128,640]{2,1,0:T(8,128)(2,1)}), bf16[8,128,640]{2,1,0:T(8,128)(2,1)S(1)}, u32[]{:S(2)}, u32[]{:S(2)}) async-start(bf16[8,128,640]{2,1,0:T(8,128)(2,1)} %broadcast_in_dim.101), calls=%async_computation | async-start | bytes 2621440 | tf_op jit(solution)/shard_map/all_to_all | solution.py:161
  24.1 3.3 %copy-start.7 = (s32[1,256,8]{1,2,0:T(8,128)S(1)}, s32[1,256,8]{1,2,0:T(8,128)}, u32[]{:S(2)}) copy-start(s32[1,256,8]{1,2,0:T(8,128)} %param.8) | copy-start | bytes 24580
  24.1 3.5 %copy-start.6 = (s32[1,256,8]{1,2,0:T(8,128)S(1)}, s32[1,256,8]{1,2,0:T(8,128)}, u32[]{:S(2)}) copy-start(s32[1,256,8]{1,2,0:T(8,128)} %param.9) | copy-start | bytes 24580
  25.5 41.8 %collective-permute-start.8 = (bf16[640,1280]{1,0:T(8,128)(2,1)}, bf16[640,1280]{1,0:T(8,128)(2,1)S(1)}, u32[]{:S(2)}, u32[]{:S(2)}) collective-permute-start(bf16[640,1280]{1,0:T(8,128)(2,1)} %select_bitcast_fusion), channel_id=1, source_target_pairs={{0,1},{1,2},{2,3},{3,4},{4,5},{5,6},{6,7},{7,0},{8,9},{9,10},{10,1... | collective-permute-start | bytes 4915208 | tf_op jit(solution)/shard_map/ppermute | solution.py:19
  55.0 33.2 %copy-start.1 = (bf16[8,128,640]{2,1,0:T(8,128)(2,1)}, bf16[8,128,640]{2,1,0:T(8,128)(2,1)S(1)}, u32[]{:S(2)}) copy-start(bf16[8,128,640]{2,1,0:T(8,128)(2,1)S(1)} %all-to-all-done) | copy-start | bytes 3932164
  55.0 38.6 %collective-permute-start.6 = (bf16[1024,640]{1,0:T(8,128)(2,1)S(1)}, bf16[1024,640]{1,0:T(8,128)(2,1)}, u32[]{:S(2)}, u32[]{:S(2)}) collective-permute-start(bf16[1024,640]{1,0:T(8,128)(2,1)S(1)} %bitcast.30), channel_id=1, source_target_pairs={{0,8},{8,0},{1,9},{9,1},{2,10},{10,2},{3,11},{11,3},{4,12},{12,4},... | collective-permute-start | bytes 3932168 | tf_op jit(solution)/shard_map/ppermute | solution.py:19
  57.9 11.3 %collective-permute-start = (bf16[16,1408]{1,0:T(8,128)(2,1)S(1)}, bf16[16,1408]{1,0:T(8,128)(2,1)S(1)}, u32[]{:S(2)}, u32[]{:S(2)}) collective-permute-start(bf16[16,1408]{1,0:T(8,128)(2,1)S(1)} %concatenate.9), channel_id=1, source_target_pairs={{0,9},{1,10},{2,11},{3,12},{4,13},{5,14},{6,15},{7,8},{8,17},{9,18... | collective-permute-start | bytes 135176 | tf_op jit(solution)/shard_map/ppermute | solution.py:145
  59.8 9.5 %collective-permute-start.1 = (s32[16,256]{1,0:T(8,128)S(1)}, s32[16,256]{1,0:T(8,128)S(1)}, u32[]{:S(2)}, u32[]{:S(2)}) collective-permute-start(s32[16,256]{1,0:T(8,128)S(1)} %pad_add_fusion.1), channel_id=1, source_target_pairs={{0,1},{1,2},{2,3},{3,4},{4,5},{5,6},{6,7},{7,0},{8,9},{9,10},{10,1... | collective-permute-start | bytes 49160 | tf_op jit(solution)/shard_map/ppermute | solution.py:19
  67.3 26.4 %copy-start.3 = (bf16[640,1280]{1,0:T(8,128)(2,1)}, bf16[640,1280]{1,0:T(8,128)(2,1)S(1)}, u32[]{:S(2)}) copy-start(bf16[640,1280]{1,0:T(8,128)(2,1)S(1)} %collective-permute-done.8.one_ref) | copy-start | bytes 4915204
  67.3 57.1 %collective-permute-start.9 = (bf16[640,1280]{1,0:T(8,128)(2,1)S(1)}, bf16[640,1280]{1,0:T(8,128)(2,1)}, u32[]{:S(2)}, u32[]{:S(2)}) collective-permute-start(bf16[640,1280]{1,0:T(8,128)(2,1)S(1)} %collective-permute-done.8.one_ref), channel_id=1, source_target_pairs={{0,8},{8,0},{1,9},{9,1},{2,10},{10,2},{3,11},{11,3},{4,12},{12,4},... | collective-permute-start | bytes 4915208 | tf_op jit(solution)/shard_map/ppermute | solution.py:19
  69.2 24.5 %copy-start.4 = (bf16[16,1408]{1,0:T(8,128)(2,1)}, bf16[16,1408]{1,0:T(8,128)(2,1)S(1)}, u32[]{:S(2)}) copy-start(bf16[16,1408]{1,0:T(8,128)(2,1)S(1)} %collective-permute-done.tail_ref) | copy-start | bytes 135172
  69.7 10.5 %collective-permute-start.2 = (s32[16,272]{1,0:T(8,128)S(1)}, s32[16,272]{1,0:T(8,128)S(1)}, u32[]{:S(2)}, u32[]{:S(2)}) collective-permute-start(s32[16,272]{1,0:T(8,128)S(1)} %get-tuple-element.28), channel_id=1, source_target_pairs={{0,128},{128,256},{256,384},{384,0},{1,129},{129,257},{257,385},{3... | collective-permute-start | bytes 52232 | tf_op jit(solution)/shard_map/ppermute | solution.py:19
  73.1 7.2 %collective-permute-start.3 = (s32[16,272]{1,0:T(8,128)S(1)}, s32[16,272]{1,0:T(8,128)S(1)}, u32[]{:S(2)}, u32[]{:S(2)}) collective-permute-start(s32[16,272]{1,0:T(8,128)S(1)} %get-tuple-element.27), channel_id=1, source_target_pairs={{0,256},{128,384},{256,0},{384,128},{1,257},{129,385},{257,1},{385... | collective-permute-start | bytes 52232 | tf_op jit(solution)/shard_map/ppermute | solution.py:19
  76.2 5.7 %collective-permute-start.4 = (s32[16,272]{1,0:T(8,128)S(1)}, s32[16,272]{1,0:T(8,128)S(1)}, u32[]{:S(2)}, u32[]{:S(2)}) collective-permute-start(s32[16,272]{1,0:T(8,128)S(1)} %get-tuple-element.26), channel_id=1, source_target_pairs={{0,384},{128,0},{256,128},{384,256},{1,385},{129,1},{257,129},{385... | collective-permute-start | bytes 52232 | tf_op jit(solution)/shard_map/ppermute | solution.py:19
  99.5 8.1 %copy-start.8 = (f32[1,4,1280]{2,1,0:T(4,128)S(1)}, f32[1,4,1280]{2,1,0:T(4,128)}, u32[]{:S(2)}) copy-start(f32[1,4,1280]{2,1,0:T(4,128)} %param.13) | copy-start | bytes 61444
  99.5 24.8 %all-to-all-start.1 = ((bf16[4,272,640]{2,1,0:T(8,128)(2,1)}), bf16[4,272,640]{2,1,0:T(8,128)(2,1)S(1)}, u32[]{:S(2)}, u32[]{:S(2)}) async-start(bf16[4,272,640]{2,1,0:T(8,128)(2,1)} %dot_other.1), calls=%async_computation.1 | async-start | bytes 2785280 | tf_op jit(solution)/shard_map/all_to_all | solution.py:184
  105.7 18.6 %collective-permute-start.7 = (bf16[256,1280]{1,0:T(8,128)(2,1)}, bf16[256,1280]{1,0:T(8,128)(2,1)}, u32[]{:S(2)}, u32[]{:S(2)}) collective-permute-start(bf16[256,1280]{1,0:T(8,128)(2,1)} %bitcast.38), channel_id=1, source_target_pairs={{0,1},{1,2},{2,3},{3,4},{4,5},{5,6},{6,7},{7,0},{8,9},{9,10},{10,1... | collective-permute-start | bytes 1966088 | tf_op jit(solution)/shard_map/ppermute | solution.py:19
  107.7 16.7 %collective-permute-start.10 = (f32[4,1280]{1,0:T(4,128)S(1)}, f32[4,1280]{1,0:T(4,128)S(1)}, u32[]{:S(2)}, u32[]{:S(2)}) collective-permute-start(f32[4,1280]{1,0:T(4,128)S(1)} %bitcast.40), channel_id=1, source_target_pairs={{0,1},{1,2},{2,3},{3,4},{4,5},{5,6},{6,7},{7,0},{8,9},{9,10},{10,1... | collective-permute-start | bytes 61448 | tf_op jit(solution)/shard_map/ppermute | solution.py:19
  124.3 0.6 copy-start.5
  124.9 1.1 copy-start

commit v2 on v1

--- a/solution.py
+++ b/solution.py
@@ -23,69 +23,39 @@
 SMEM = pl.BlockSpec(memory_space=pltpu.SMEM)
 
 
-def pick_matrices(x, asked, rows_dev):
+def pick_matrices(asked, rows_dev):
     groups, rows, _ = asked.shape
 
-    def body(x_ref, asked_ref, own_ref, other_ref):
+    def body(asked_ref, own_ref, other_ref):
         lane = lax.broadcasted_iota(jnp.int32, (rows, rows_dev), 1)
         for group in range(groups):
-            source = lax.rem(x_ref[0] - group + groups, groups)
             for swapped, out_ref in ((0, own_ref), (1, other_ref)):
                 for far in range(NY):
                     column = swapped * NY + far
-                    hit = asked_ref[source, :, column : column + 1] == lane
+                    hit = asked_ref[group, :, column : column + 1] == lane
                     hit = hit.astype(jnp.float32).astype(jnp.bfloat16)
                     out_ref[group, :, far * rows_dev : (far + 1) * rows_dev] = hit
 
     shape = jax.ShapeDtypeStruct((groups, rows, NY * rows_dev), jnp.bfloat16)
     return pl.pallas_call(
         body,
-        in_specs=[SMEM, VMEM],
+        in_specs=[VMEM],
         out_specs=[VMEM, VMEM],
         out_shape=[shape, shape],
         name="pick_matrices",
-    )(x, asked)
+    )(asked)
 
 
-def dot_own(pick, table_rows):
-    groups, rows, _ = pick.shape
-
-    def body(pick_ref, rows_ref, out_ref):
-        for group in range(groups):
-            out_ref[group] = jnp.dot(pick_ref[group], rows_ref[...], preferred_element_type=jnp.float32)
-
-    return pl.pallas_call(
-        body,
-        in_specs=[VMEM, VMEM],
-        out_specs=VMEM,
-        out_shape=jax.ShapeDtypeStruct((groups, rows, table_rows.shape[1]), jnp.float32),
-        name="dot_own",
-    )(pick, table_rows)
-
-
-def dot_other(pick, table_rows, own):
-    def body(pick_ref, rows_ref, own_ref, out_ref):
-        for group in range(own.shape[0]):
-            total = jnp.dot(pick_ref[group], rows_ref[...], preferred_element_type=jnp.float32)
-            out_ref[group] = (own_ref[group] + total).astype(jnp.bfloat16)
-
-    return pl.pallas_call(
-        body,
-        in_specs=[VMEM, VMEM, VMEM],
-        out_specs=VMEM,
-        out_shape=jax.ShapeDtypeStruct(own.shape, jnp.bfloat16),
-        name="dot_other",
-    )(pick, table_rows, own)
-
-
-def dense(place, sums, tail, hidden, weight_one, weight_two, taps):
+def dense(place, own, sums, tail, hidden, weight_one, weight_two, taps):
     chunk, features = hidden.shape
     rows = chunk + HALO
 
-    def body(place_ref, sums_ref, tail_ref, hidden_ref, one_ref, two_ref, taps_ref, out_ref, product_ref, normed_ref):
-        total = sums_ref[0].astype(jnp.float32)
-        for group in range(1, sums_ref.shape[0]):
-            total = total + sums_ref[group].astype(jnp.float32)
+    def body(place_ref, own_ref, *refs):
+        sums_refs, refs = refs[: len(sums)], refs[len(sums) :]
+        tail_ref, hidden_ref, one_ref, two_ref, taps_ref, out_ref, product_ref, normed_ref = refs
+        total = own_ref[...]
+        for sums_ref in sums_refs:
+            total = total + sums_ref[...].astype(jnp.float32)
         packed = total.astype(jnp.bfloat16)
         core = place_ref[1]
         product_ref[core] = jnp.dot(packed, one_ref[...], preferred_element_type=jnp.float32)
@@ -110,7 +80,7 @@
 
     return pl.pallas_call(
         body,
-        in_specs=[SMEM] + [VMEM] * 6,
+        in_specs=[SMEM] + [VMEM] * (6 + len(sums)),
         out_specs=VMEM,
         out_shape=jax.ShapeDtypeStruct((chunk, features), jnp.bfloat16),
         scratch_shapes=[
@@ -118,7 +88,7 @@
             pltpu.VMEM((rows, features), jnp.float32),
         ],
         name="dense",
-    )(place, sums, tail, hidden, weight_one, weight_two, taps)
+    )(place, own, *sums, tail, hidden, weight_one, weight_two, taps)
 
 
 def local(hidden, owner, slot, memory_table, key_weight, value_weight, conv_weight):
@@ -177,14 +147,19 @@
     for ahead in range(1, NX):
         received.append(rotated(asked[ahead], "x", ahead))
     asked = jnp.stack(received).transpose(0, 2, 1)
-    pick_own, pick_other = pick_matrices(x.astype(jnp.int32).reshape(1), asked, rows_dev)
+    pick_own, pick_other = pick_matrices(asked, rows_dev)
 
-    own_part = dot_own(pick_own, own_rows)
-    sums = dot_other(pick_other, other_rows, own_part)
-    sums = lax.all_to_all(sums, "x", split_axis=0, concat_axis=0, tiled=True)
+    rows = tok_rows + HALO
+    own_part = jnp.dot(pick_own.reshape(NX * rows, -1), own_rows, preferred_element_type=jnp.float32)
+    own_part = own_part.reshape(NX, rows, -1)
+    sums = []
+    for back in (2, 1, 3, 0):
+        part = own_part[back] + jnp.dot(pick_other[back], other_rows, preferred_element_type=jnp.float32)
+        if back > 0:
+            sums.append(rotated(part.astype(bf16), "x", -back))
     later = (x > 0) | (y > 0) | (core > 0)
     place = jnp.stack([later.astype(jnp.int32), core.astype(jnp.int32)])
-    return dense(place, sums, tail, states, weight_one, weight_two, taps)[None]
+    return dense(place, part, sums, tail, states, weight_one, weight_two, taps)[None]
 
 
 def solution(mesh):

time: 133 us -> 126 us (0.947)
  the two profiles are of different devices: /device:TPU:18 before, /device:TPU:1 now
where the time goes in v2:
time: 126 us; the launch traced here: 125 us
  starting transfers between devices  49.6 us (39%)
  waiting for transfers between devices  48.6 us (39%)
  Pallas kernels  11.7 us (9%)
  matrix products  7.36 us (6%)
  local copies, waits for them, and re-layouts  4.56 us (4%)
  other arithmetic  2.54 us (2%)
    ppermute x13, starting transfers between devices, rotated(): lax.ppermute(value, axis, [(i, (i + by) % count) for i in range(count)])  37.2 us
    all_to_all x1, waiting for transfers between devices, local(): lax.all_to_all(copies, 'y', split_axis=0, concat_axis=0, tiled=True)  22.9 us
    ppermute x13, waiting for transfers between devices, rotated(): lax.ppermute(value, axis, [(i, (i + by) % count) for i in range(count)])  18 us
    ppermute x1, waiting for transfers between devices, local(): lax.ppermute(tail, TABLE + ('segment',), [(i * sections + s, (i + 1) * se...  7.76 us
    all_to_all x1, starting transfers between devices, local(): lax.all_to_all(copies, 'y', split_axis=0, concat_axis=0, tiled=True)  6.95 us
    pallas_call x1, Pallas kernels, dense(): pl.pallas_call(body, in_specs=[SMEM] + [VMEM] * (6 + len(sums)), out_spec...  6.4 us
    ppermute x1, starting transfers between devices, local(): lax.ppermute(tail, TABLE + ('segment',), [(i * sections + s, (i + 1) * se...  5.48 us
    pallas_call x1, Pallas kernels, pick_matrices(): pl.pallas_call(body, in_specs=[VMEM], out_specs=[VMEM, VMEM], out_shape=[...  5.26 us
  transfers between devices with their start and end apart: 15, of which 5 were waited for; matrix products, arithmetic and copies ran while one was open for 10% of the time, Pallas kernels for 4%

profile of v2, /device:TPU:1, one launch (start us, length us, event | category | flops | bytes accessed | tf_op | source)
XLA Modules:
  0.0 124.7 jit_solution(7852177784075545909)
XLA Ops:
  0.0 4.8 %collective-permute-start.5 = (bf16[128,640]{1,0:T(8,128)(2,1)}, bf16[128,640]{1,0:T(8,128)(2,1)S(1)}, u32[]{:S(2)}, u32[]{:S(2)}) collective-permute-start(bf16[128,640]{1,0:T(8,128)(2,1)} %bitcast.64), channel_id=1, source_target_pairs={{0,1},{1,2},{2,3},{3,4},{4,5},{5,6},{6,7},{7,0},{8,9},{9,10},{10,1... | collective-permute-start | bytes 491528 | tf_op jit(solution)/shard_map/ppermute | solution.py:19
  4.8 10.8 %collective-permute-done.5 = bf16[128,640]{1,0:T(8,128)(2,1)S(1)} collective-permute-done((bf16[128,640]{1,0:T(8,128)(2,1)}, bf16[128,640]{1,0:T(8,128)(2,1)S(1)}, u32[]{:S(2)}, u32[]{:S(2)}) %collective-permute-start.5) | collective-permute-done | bytes 163872 | tf_op jit(solution)/shard_map/ppermute | solution.py:19
  16.8 7.0 %all-to-all-start = ((bf16[8,128,640]{2,1,0:T(8,128)(2,1)}), bf16[8,128,640]{2,1,0:T(8,128)(2,1)}, u32[]{:S(2)}, u32[]{:S(2)}) async-start(bf16[8,128,640]{2,1,0:T(8,128)(2,1)} %broadcast_in_dim.101), calls=%async_computation | async-start | bytes 2621440 | tf_op jit(solution)/shard_map/all_to_all | solution.py:131
  23.7 1.9 %collective-permute-start.1 = (s32[16,256]{1,0:T(8,128)S(1)}, s32[16,256]{1,0:T(8,128)S(1)}, u32[]{:S(2)}, u32[]{:S(2)}) collective-permute-start(s32[16,256]{1,0:T(8,128)S(1)} %pad_add_fusion.1), channel_id=1, source_target_pairs={{0,1},{1,2},{2,3},{3,4},{4,5},{5,6},{6,7},{7,0},{8,9},{9,10},{10,1... | collective-permute-start | bytes 49160 | tf_op jit(solution)/shard_map/ppermute | solution.py:19
  25.7 1.4 %select_bitcast_fusion = bf16[640,1280]{1,0:T(8,128)(2,1)} fusion(bf16[1,640,1280]{2,1,0:T(8,128)(2,1)S(1)} %copy-done.1, bf16[1,640,1280]{2,1,0:T(8,128)(2,1)S(1)} %copy-done.2, pred[]{:T(512)S(6)} %eq.138), kind=kLoop, calls=%fused_computation | loop fusion | flops 819200 | bytes 4915201 | tf_op jit(solution)/shard_map/jit(_where)/select_n | solution.py:125
  27.1 1.9 %collective-permute-start.11 = (bf16[640,1280]{1,0:T(8,128)(2,1)}, bf16[640,1280]{1,0:T(8,128)(2,1)S(1)}, u32[]{:S(2)}, u32[]{:S(2)}) collective-permute-start(bf16[640,1280]{1,0:T(8,128)(2,1)} %select_bitcast_fusion), channel_id=1, source_target_pairs={{0,1},{1,2},{2,3},{3,4},{4,5},{5,6},{6,7},{7,0},{8,9},{9,10},{10,1... | collective-permute-start | bytes 4915208 | tf_op jit(solution)/shard_map/ppermute | solution.py:19
  30.2 5.5 %collective-permute-start = (bf16[16,1408]{1,0:T(8,128)(2,1)S(1)}, bf16[16,1408]{1,0:T(8,128)(2,1)S(1)}, u32[]{:S(2)}, u32[]{:S(2)}) collective-permute-start(bf16[16,1408]{1,0:T(8,128)(2,1)S(1)} %concatenate.9), channel_id=1, source_target_pairs={{0,9},{1,10},{2,11},{3,12},{4,13},{5,14},{6,15},{7,8},{8,17},{9,18... | collective-permute-start | bytes 135176 | tf_op jit(solution)/shard_map/ppermute | solution.py:115
  35.7 22.9 %all-to-all-done = bf16[8,128,640]{2,1,0:T(8,128)(2,1)} async-done(((bf16[8,128,640]{2,1,0:T(8,128)(2,1)}), bf16[8,128,640]{2,1,0:T(8,128)(2,1)}, u32[]{:S(2)}, u32[]{:S(2)}) %all-to-all-start) | async-done | bytes 1310752 | tf_op jit(solution)/shard_map/all_to_all | solution.py:131
  58.6 2.5 %collective-permute-start.6 = (bf16[1024,640]{1,0:T(8,128)(2,1)}, bf16[1024,640]{1,0:T(8,128)(2,1)S(1)}, u32[]{:S(2)}, u32[]{:S(2)}) collective-permute-start(bf16[1024,640]{1,0:T(8,128)(2,1)} %bitcast.17), channel_id=1, source_target_pairs={{0,8},{8,0},{1,9},{9,1},{2,10},{10,2},{3,11},{11,3},{4,12},{12,4},... | collective-permute-start | bytes 3932168 | tf_op jit(solution)/shard_map/ppermute | solution.py:19
  61.1 7.8 %collective-permute-done.refs_3_ = bf16[16,1408]{1,0:T(8,128)(2,1)S(1)} collective-permute-done((bf16[16,1408]{1,0:T(8,128)(2,1)S(1)}, bf16[16,1408]{1,0:T(8,128)(2,1)S(1)}, u32[]{:S(2)}, u32[]{:S(2)}) %collective-permute-start) | collective-permute-done | bytes 45088 | tf_op jit(solution)/shard_map/ppermute | solution.py:115
  69.4 3.9 %collective-permute-start.4 = (s32[16,272]{1,0:T(8,128)S(1)}, s32[16,272]{1,0:T(8,128)S(1)}, u32[]{:S(2)}, u32[]{:S(2)}) collective-permute-start(s32[16,272]{1,0:T(8,128)S(1)} %get-tuple-element.26), channel_id=1, source_target_pairs={{0,384},{128,0},{256,128},{384,256},{1,385},{129,1},{257,129},{385... | collective-permute-start | bytes 52232 | tf_op jit(solution)/shard_map/ppermute | solution.py:19
  73.3 2.9 %collective-permute-start.3 = (s32[16,272]{1,0:T(8,128)S(1)}, s32[16,272]{1,0:T(8,128)S(1)}, u32[]{:S(2)}, u32[]{:S(2)}) collective-permute-start(s32[16,272]{1,0:T(8,128)S(1)} %get-tuple-element.27), channel_id=1, source_target_pairs={{0,256},{128,384},{256,0},{384,128},{1,257},{129,385},{257,1},{385... | collective-permute-start | bytes 52232 | tf_op jit(solution)/shard_map/ppermute | solution.py:19
  76.2 2.5 %collective-permute-start.2 = (s32[16,272]{1,0:T(8,128)S(1)}, s32[16,272]{1,0:T(8,128)S(1)}, u32[]{:S(2)}, u32[]{:S(2)}) collective-permute-start(s32[16,272]{1,0:T(8,128)S(1)} %get-tuple-element.28), channel_id=1, source_target_pairs={{0,128},{128,256},{256,384},{384,0},{1,129},{129,257},{257,385},{3... | collective-permute-start | bytes 52232 | tf_op jit(solution)/shard_map/ppermute | solution.py:19
  78.8 1.9 %collective-permute-start.10 = (bf16[256,1280]{1,0:T(8,128)(2,1)}, bf16[256,1280]{1,0:T(8,128)(2,1)}, u32[]{:S(2)}, u32[]{:S(2)}) collective-permute-start(bf16[256,1280]{1,0:T(8,128)(2,1)} %bitcast.62), channel_id=1, source_target_pairs={{0,1},{1,2},{2,3},{3,4},{4,5},{5,6},{6,7},{7,0},{8,9},{9,10},{10,1... | collective-permute-start | bytes 1966088 | tf_op jit(solution)/shard_map/ppermute | solution.py:19
  80.7 1.9 %collective-permute-start.13 = (f32[4,1280]{1,0:T(4,128)S(1)}, f32[4,1280]{1,0:T(4,128)S(1)}, u32[]{:S(2)}, u32[]{:S(2)}) collective-permute-start(f32[4,1280]{1,0:T(4,128)S(1)} %bitcast.65), channel_id=1, source_target_pairs={{0,1},{1,2},{2,3},{3,4},{4,5},{5,6},{6,7},{7,0},{8,9},{9,10},{10,1... | collective-permute-start | bytes 61448 | tf_op jit(solution)/shard_map/ppermute | solution.py:19
  83.7 5.3 %pick_matrices.1 = (bf16[4,272,1024]{2,1,0:T(8,128)(2,1)}, bf16[4,272,1024]{2,1,0:T(8,128)(2,1)}) custom-call(s32[4,272,16]{2,1,0:T(8,128)} %bitcast.56), custom_call_target="tpu_custom_call" | custom-call | tf_op jit(solution)/shard_map/pick_matrices/pallas_call | solution.py:40
  89.0 3.7 %collective-permute-start.12 = (bf16[640,1280]{1,0:T(8,128)(2,1)S(1)}, bf16[640,1280]{1,0:T(8,128)(2,1)S(1)}, u32[]{:S(2)}, u32[]{:S(2)}) collective-permute-start(bf16[640,1280]{1,0:T(8,128)(2,1)S(1)} %collective-permute-done.11.refs_5_), channel_id=1, source_target_pairs={{0,8},{8,0},{1,9},{9,1},{2,10},{10,2},{3,11},{11,3},{4,12},{12,4},... | collective-permute-start | bytes 4915208 | tf_op jit(solution)/shard_map/ppermute | solution.py:19
  92.8 4.0 %fusion.64 = f32[1088,640]{1,0:T(8,128)S(1)} fusion(bf16[1088,1024]{1,0:T(8,128)(2,1)} %bitcast.63, bf16[1024,640]{1,0:T(8,128)(2,1)} %bitcast.17), kind=kOutput, calls=%fused_computation.113 | convolution fusion | flops 1426063360 | bytes 6324224 | tf_op jit(solution)/shard_map/dot_general | solution.py:153
  97.5 3.4 %collective-permute-start.7 = (bf16[272,640]{1,0:T(8,128)(2,1)S(1)}, bf16[272,640]{1,0:T(8,128)(2,1)S(1)}, u32[]{:S(2)}, u32[]{:S(2)}) collective-permute-start(bf16[272,640]{1,0:T(8,128)(2,1)S(1)} %fusion.2), channel_id=1, source_target_pairs={{0,256},{128,384},{256,0},{384,128},{1,257},{129,385},{257,1},{385... | collective-permute-start | bytes 1044488 | tf_op jit(solution)/shard_map/ppermute | solution.py:19
  101.4 3.9 %collective-permute-start.8 = (bf16[272,640]{1,0:T(8,128)(2,1)S(1)}, bf16[272,640]{1,0:T(8,128)(2,1)}, u32[]{:S(2)}, u32[]{:S(2)}) collective-permute-start(bf16[272,640]{1,0:T(8,128)(2,1)S(1)} %fusion.1), channel_id=1, source_target_pairs={{0,384},{128,0},{256,128},{384,256},{1,385},{129,1},{257,129},{385... | collective-permute-start | bytes 1044488 | tf_op jit(solution)/shard_map/ppermute | solution.py:19
  106.0 1.9 %collective-permute-start.9 = (bf16[272,640]{1,0:T(8,128)(2,1)S(1)}, bf16[272,640]{1,0:T(8,128)(2,1)}, u32[]{:S(2)}, u32[]{:S(2)}) collective-permute-start(bf16[272,640]{1,0:T(8,128)(2,1)S(1)} %fusion), channel_id=1, source_target_pairs={{0,128},{128,256},{256,384},{384,0},{1,129},{129,257},{257,385},{3... | collective-permute-start | bytes 1044488 | tf_op jit(solution)/shard_map/ppermute | solution.py:19
  108.5 1.5 %slice_add_fusion.3.own_ref = f32[272,640]{1,0:T(8,128)} fusion(f32[1088,640]{1,0:T(8,128)S(1)} %fusion.64, bf16[1024,640]{1,0:T(8,128)(2,1)S(1)} %collective-permute-done.6, bf16[4,272,1024]{2,1,0:T(8,128)(2,1)S(1)} %copy-done), kind=kOutput, calls=%fused_computation.7 | convolution fusion | flops 356689920 | bytes 3260416 | tf_op jit(solution)/shard_map/dot_general | solution.py:157
  111.2 6.7 %collective-permute-done.8.refs_1_ = bf16[272,640]{1,0:T(8,128)(2,1)} collective-permute-done((bf16[272,640]{1,0:T(8,128)(2,1)S(1)}, bf16[272,640]{1,0:T(8,128)(2,1)}, u32[]{:S(2)}, u32[]{:S(2)}) %collective-permute-start.8) | collective-permute-done | bytes 348192 | tf_op jit(solution)/shard_map/ppermute | solution.py:19
  118.3 6.4 %dense.1 = bf16[256,1280]{1,0:T(8,128)(2,1)} custom-call(s32[2]{0:T(128)} %pad_add_fusion.3.place_ref, f32[272,640]{1,0:T(8,128)} %slice_add_fusion.3.own_ref, bf16[272,640]{1,0:T(8,128)(2,1)} %copy-done.5, bf16[272,640]{1,0:T(8,128)(2,1)} %collective-permute-done.8.refs_1_, bf16[272,640]{1,0:T(8,128)(2,1)} %collective-permute-done.9.refs_2_, ...), custom_call_target="tpu_custom_call" | custom-call | tf_op jit(solution)/shard_map/dense/pallas_call | solution.py:81
  (55 shorter events, 8.1 us)
Async XLA Ops:
  0.0 15.6 %collective-permute-start.5 = (bf16[128,640]{1,0:T(8,128)(2,1)}, bf16[128,640]{1,0:T(8,128)(2,1)S(1)}, u32[]{:S(2)}, u32[]{:S(2)}) collective-permute-start(bf16[128,640]{1,0:T(8,128)(2,1)} %bitcast.64), channel_id=1, source_target_pairs={{0,1},{1,2},{2,3},{3,4},{4,5},{5,6},{6,7},{7,0},{8,9},{9,10},{10,1... | collective-permute-start | bytes 491528 | tf_op jit(solution)/shard_map/ppermute | solution.py:19
  15.6 10.1 %copy-start.2 = (bf16[1,640,1280]{2,1,0:T(8,128)(2,1)S(1)}, bf16[1,640,1280]{2,1,0:T(8,128)(2,1)}, u32[]{:S(2)}) copy-start(bf16[1,640,1280]{2,1,0:T(8,128)(2,1)} %param.12) | copy-start | bytes 4915204
  16.8 7.0 %copy-start.8 = (s32[1,256,8]{1,2,0:T(8,128)S(1)}, s32[1,256,8]{1,2,0:T(8,128)}, u32[]{:S(2)}) copy-start(s32[1,256,8]{1,2,0:T(8,128)} %param.8) | copy-start | bytes 24580
  16.8 7.0 %copy-start.9 = (s32[1,256,8]{1,2,0:T(8,128)S(1)}, s32[1,256,8]{1,2,0:T(8,128)}, u32[]{:S(2)}) copy-start(s32[1,256,8]{1,2,0:T(8,128)} %param.9) | copy-start | bytes 24580
  16.8 8.9 %copy-start.1 = (bf16[1,640,1280]{2,1,0:T(8,128)(2,1)S(1)}, bf16[1,640,1280]{2,1,0:T(8,128)(2,1)}, u32[]{:S(2)}) copy-start(bf16[1,640,1280]{2,1,0:T(8,128)(2,1)} %param.11) | copy-start | bytes 4915204
  16.8 41.9 %all-to-all-start = ((bf16[8,128,640]{2,1,0:T(8,128)(2,1)}), bf16[8,128,640]{2,1,0:T(8,128)(2,1)}, u32[]{:S(2)}, u32[]{:S(2)}) async-start(bf16[8,128,640]{2,1,0:T(8,128)(2,1)} %broadcast_in_dim.101), calls=%async_computation | async-start | bytes 2621440 | tf_op jit(solution)/shard_map/all_to_all | solution.py:131
  23.7 45.2 %collective-permute-start.1 = (s32[16,256]{1,0:T(8,128)S(1)}, s32[16,256]{1,0:T(8,128)S(1)}, u32[]{:S(2)}, u32[]{:S(2)}) collective-permute-start(s32[16,256]{1,0:T(8,128)S(1)} %pad_add_fusion.1), channel_id=1, source_target_pairs={{0,1},{1,2},{2,3},{3,4},{4,5},{5,6},{6,7},{7,0},{8,9},{9,10},{10,1... | collective-permute-start | bytes 49160 | tf_op jit(solution)/shard_map/ppermute | solution.py:19
  25.7 55.0 %copy-start.10 = (f32[1,4,1280]{2,1,0:T(4,128)S(1)}, f32[1,4,1280]{2,1,0:T(4,128)}, u32[]{:S(2)}) copy-start(f32[1,4,1280]{2,1,0:T(4,128)} %param.13) | copy-start | bytes 61444
  27.1 61.9 %collective-permute-start.11 = (bf16[640,1280]{1,0:T(8,128)(2,1)}, bf16[640,1280]{1,0:T(8,128)(2,1)S(1)}, u32[]{:S(2)}, u32[]{:S(2)}) collective-permute-start(bf16[640,1280]{1,0:T(8,128)(2,1)} %select_bitcast_fusion), channel_id=1, source_target_pairs={{0,1},{1,2},{2,3},{3,4},{4,5},{5,6},{6,7},{7,0},{8,9},{9,10},{10,1... | collective-permute-start | bytes 4915208 | tf_op jit(solution)/shard_map/ppermute | solution.py:19
  30.2 38.7 %collective-permute-start = (bf16[16,1408]{1,0:T(8,128)(2,1)S(1)}, bf16[16,1408]{1,0:T(8,128)(2,1)S(1)}, u32[]{:S(2)}, u32[]{:S(2)}) collective-permute-start(bf16[16,1408]{1,0:T(8,128)(2,1)S(1)} %concatenate.9), channel_id=1, source_target_pairs={{0,9},{1,10},{2,11},{3,12},{4,13},{5,14},{6,15},{7,8},{8,17},{9,18... | collective-permute-start | bytes 135176 | tf_op jit(solution)/shard_map/ppermute | solution.py:115
  58.6 38.2 %collective-permute-start.6 = (bf16[1024,640]{1,0:T(8,128)(2,1)}, bf16[1024,640]{1,0:T(8,128)(2,1)S(1)}, u32[]{:S(2)}, u32[]{:S(2)}) collective-permute-start(bf16[1024,640]{1,0:T(8,128)(2,1)} %bitcast.17), channel_id=1, source_target_pairs={{0,8},{8,0},{1,9},{9,1},{2,10},{10,2},{3,11},{11,3},{4,12},{12,4},... | collective-permute-start | bytes 3932168 | tf_op jit(solution)/shard_map/ppermute | solution.py:19
  68.9 27.9 %copy-start.6 = (bf16[16,1408]{1,0:T(8,128)(2,1)}, bf16[16,1408]{1,0:T(8,128)(2,1)S(1)}, u32[]{:S(2)}) copy-start(bf16[16,1408]{1,0:T(8,128)(2,1)S(1)} %collective-permute-done.refs_3_) | copy-start | bytes 135172
  69.4 9.4 %collective-permute-start.4 = (s32[16,272]{1,0:T(8,128)S(1)}, s32[16,272]{1,0:T(8,128)S(1)}, u32[]{:S(2)}, u32[]{:S(2)}) collective-permute-start(s32[16,272]{1,0:T(8,128)S(1)} %get-tuple-element.26), channel_id=1, source_target_pairs={{0,384},{128,0},{256,128},{384,256},{1,385},{129,1},{257,129},{385... | collective-permute-start | bytes 52232 | tf_op jit(solution)/shard_map/ppermute | solution.py:19
  73.3 7.4 %collective-permute-start.3 = (s32[16,272]{1,0:T(8,128)S(1)}, s32[16,272]{1,0:T(8,128)S(1)}, u32[]{:S(2)}, u32[]{:S(2)}) collective-permute-start(s32[16,272]{1,0:T(8,128)S(1)} %get-tuple-element.27), channel_id=1, source_target_pairs={{0,256},{128,384},{256,0},{384,128},{1,257},{129,385},{257,1},{385... | collective-permute-start | bytes 52232 | tf_op jit(solution)/shard_map/ppermute | solution.py:19
  76.2 6.4 %collective-permute-start.2 = (s32[16,272]{1,0:T(8,128)S(1)}, s32[16,272]{1,0:T(8,128)S(1)}, u32[]{:S(2)}, u32[]{:S(2)}) collective-permute-start(s32[16,272]{1,0:T(8,128)S(1)} %get-tuple-element.28), channel_id=1, source_target_pairs={{0,128},{128,256},{256,384},{384,0},{1,129},{129,257},{257,385},{3... | collective-permute-start | bytes 52232 | tf_op jit(solution)/shard_map/ppermute | solution.py:19
  78.8 31.2 %collective-permute-start.10 = (bf16[256,1280]{1,0:T(8,128)(2,1)}, bf16[256,1280]{1,0:T(8,128)(2,1)}, u32[]{:S(2)}, u32[]{:S(2)}) collective-permute-start(bf16[256,1280]{1,0:T(8,128)(2,1)} %bitcast.62), channel_id=1, source_target_pairs={{0,1},{1,2},{2,3},{3,4},{4,5},{5,6},{6,7},{7,0},{8,9},{9,10},{10,1... | collective-permute-start | bytes 1966088 | tf_op jit(solution)/shard_map/ppermute | solution.py:19
  80.7 25.2 %collective-permute-start.13 = (f32[4,1280]{1,0:T(4,128)S(1)}, f32[4,1280]{1,0:T(4,128)S(1)}, u32[]{:S(2)}, u32[]{:S(2)}) collective-permute-start(f32[4,1280]{1,0:T(4,128)S(1)} %bitcast.65), channel_id=1, source_target_pairs={{0,1},{1,2},{2,3},{3,4},{4,5},{5,6},{6,7},{7,0},{8,9},{9,10},{10,1... | collective-permute-start | bytes 61448 | tf_op jit(solution)/shard_map/ppermute | solution.py:19
  89.0 7.8 %copy-start.3 = (bf16[640,1280]{1,0:T(8,128)(2,1)}, bf16[640,1280]{1,0:T(8,128)(2,1)S(1)}, u32[]{:S(2)}) copy-start(bf16[640,1280]{1,0:T(8,128)(2,1)S(1)} %collective-permute-done.11.refs_5_) | copy-start | bytes 4915204
  89.0 21.0 %collective-permute-start.12 = (bf16[640,1280]{1,0:T(8,128)(2,1)S(1)}, bf16[640,1280]{1,0:T(8,128)(2,1)S(1)}, u32[]{:S(2)}, u32[]{:S(2)}) collective-permute-start(bf16[640,1280]{1,0:T(8,128)(2,1)S(1)} %collective-permute-done.11.refs_5_), channel_id=1, source_target_pairs={{0,8},{8,0},{1,9},{9,1},{2,10},{10,2},{3,11},{11,3},{4,12},{12,4},... | collective-permute-start | bytes 4915208 | tf_op jit(solution)/shard_map/ppermute | solution.py:19
  97.5 13.7 %collective-permute-start.7 = (bf16[272,640]{1,0:T(8,128)(2,1)S(1)}, bf16[272,640]{1,0:T(8,128)(2,1)S(1)}, u32[]{:S(2)}, u32[]{:S(2)}) collective-permute-start(bf16[272,640]{1,0:T(8,128)(2,1)S(1)} %fusion.2), channel_id=1, source_target_pairs={{0,256},{128,384},{256,0},{384,128},{1,257},{129,385},{257,1},{385... | collective-permute-start | bytes 1044488 | tf_op jit(solution)/shard_map/ppermute | solution.py:19
  101.4 16.4 %collective-permute-start.8 = (bf16[272,640]{1,0:T(8,128)(2,1)S(1)}, bf16[272,640]{1,0:T(8,128)(2,1)}, u32[]{:S(2)}, u32[]{:S(2)}) collective-permute-start(bf16[272,640]{1,0:T(8,128)(2,1)S(1)} %fusion.1), channel_id=1, source_target_pairs={{0,384},{128,0},{256,128},{384,256},{1,385},{129,1},{257,129},{385... | collective-permute-start | bytes 1044488 | tf_op jit(solution)/shard_map/ppermute | solution.py:19
  106.0 12.4 %copy-start.7 = (f32[4,1280]{1,0:T(4,128)}, f32[4,1280]{1,0:T(4,128)S(1)}, u32[]{:S(2)}) copy-start(f32[4,1280]{1,0:T(4,128)S(1)} %collective-permute-done.13.refs_7_) | copy-start | bytes 61444
  106.0 12.3 %collective-permute-start.9 = (bf16[272,640]{1,0:T(8,128)(2,1)S(1)}, bf16[272,640]{1,0:T(8,128)(2,1)}, u32[]{:S(2)}, u32[]{:S(2)}) collective-permute-start(bf16[272,640]{1,0:T(8,128)(2,1)S(1)} %fusion), channel_id=1, source_target_pairs={{0,128},{128,256},{256,384},{384,0},{1,129},{129,257},{257,385},{3... | collective-permute-start | bytes 1044488 | tf_op jit(solution)/shard_map/ppermute | solution.py:19
  111.2 7.2 %copy-start.5 = (bf16[272,640]{1,0:T(8,128)(2,1)}, bf16[272,640]{1,0:T(8,128)(2,1)S(1)}, u32[]{:S(2)}) copy-start(bf16[272,640]{1,0:T(8,128)(2,1)S(1)} %collective-permute-done.7.refs_0_) | copy-start | bytes 1044484
  (2 other events, 5.3 us)

commit v3 on v2

v3 whole, which is shorter than its diff:
```python
import math

import jax
import jax.numpy as jnp
from jax import lax
from jax.experimental import pallas as pl
from jax.experimental.pallas import tpu as pltpu
from jax.sharding import Mesh, PartitionSpec as P


CONV_DILATION = 3
NX, NY, NC = 4, 8, 2
HALO = 16
TABLE = ("x", "y", "core")


def rotated(value, axis, by):
    count = lax.axis_size(axis)
    return lax.ppermute(value, axis, [(i, (i + by) % count) for i in range(count)])


VMEM = pl.BlockSpec(memory_space=pltpu.VMEM)
SMEM = pl.BlockSpec(memory_space=pltpu.SMEM)


def pick_matrices(asked, rows_dev):
    groups, rows, _ = asked.shape

    def body(asked_ref, own_ref, other_ref):
        lane = lax.broadcasted_iota(jnp.int32, (rows, rows_dev), 1)
        for group in range(groups):
            for swapped, out_ref in ((0, own_ref), (1, other_ref)):
                for far in range(NY):
                    column = swapped * NY + far
                    hit = asked_ref[group, :, column : column + 1] == lane
                    hit = hit.astype(jnp.float32).astype(jnp.bfloat16)
                    out_ref[group, :, far * rows_dev : (far + 1) * rows_dev] = hit

    shape = jax.ShapeDtypeStruct((groups, rows, NY * rows_dev), jnp.bfloat16)
    return pl.pallas_call(
        body,
        in_specs=[VMEM],
        out_specs=[VMEM, VMEM],
        out_shape=[shape, shape],
        name="pick_matrices",
    )(asked)


ANY = pl.BlockSpec(memory_space=pl.ANY)


def edge_packet(hidden, owners, slots):
    heads, tok_rows = owners.shape
    features = hidden.shape[1]

    def body(hidden_ref, owners_ref, slots_ref, numbers_ref, tail_ref):
        numbers_ref[:heads] = owners_ref[...]
        numbers_ref[heads:] = slots_ref[...]
        tail_ref[:HALO] = hidden_ref[...]
        last = numbers_ref[:, tok_rows - 128 :].astype(jnp.float32)
        tail_ref[HALO:, :128] = last.astype(jnp.bfloat16)
        tail_ref[HALO:, 128:] = jnp.zeros((2 * heads, features - 128), jnp.bfloat16)

    return pl.pallas_call(
        body,
        grid=(1,),
        in_specs=[
            pl.BlockSpec((HALO, features), lambda i: (tok_rows // HALO - 1, 0)),
            pl.BlockSpec((heads, tok_rows), lambda i: (0, 0)),
            pl.BlockSpec((heads, tok_rows), lambda i: (0, 0)),
        ],
        out_specs=[
            pl.BlockSpec((2 * heads, tok_rows), lambda i: (0, 0)),
            pl.BlockSpec((HALO + 2 * heads, features), lambda i: (0, 0)),
        ],
        out_shape=[
            jax.ShapeDtypeStruct((2 * heads, tok_rows), jnp.int32),
            jax.ShapeDtypeStruct((HALO + 2 * heads, features), jnp.bfloat16),
        ],
        name="edge_packet",
    )(hidden, owners, slots)


def section_packet(core, key_weight, value_weight, hidden, taps):
    depth, features = key_weight.shape
    tok_rows, count = hidden.shape[0], taps.shape[0]
    total = depth + tok_rows + 4 * count
    parts = 4
    part = depth // parts

    def body(core_ref, key_ref, value_ref, hidden_ref, taps_ref, out_ref, terms_ref, sems):
        def weight_copy(source, i):
            span = pl.ds(i * part, part)
            return pltpu.make_async_copy(source.at[span], out_ref.at[span], sems.at[i])

        for mine, source in ((0, key_ref), (1, value_ref)):

            @pl.when(core_ref[0] == mine)
            def _(source=source):
                for i in range(parts):
                    weight_copy(source, i).start()

        rows_copy = pltpu.make_async_copy(hidden_ref, out_ref.at[pl.ds(depth, tok_rows)], sems.at[parts])
        rows_copy.start()
        taps_value = taps_ref[...]
        high = taps_value.astype(jnp.bfloat16).astype(jnp.float32)
        middle = (taps_value - high).astype(jnp.bfloat16).astype(jnp.float32)
        low = taps_value - high - middle
        terms = jnp.concatenate([high, middle, low, jnp.zeros_like(low)], axis=0)
        terms_ref[...] = terms.astype(jnp.bfloat16)
        taps_copy = pltpu.make_async_copy(
            terms_ref, out_ref.at[pl.ds(depth + tok_rows, 4 * count)], sems.at[parts + 1]
        )
        taps_copy.start()
        for i in range(parts):
            weight_copy(key_ref, i).wait()
        rows_copy.wait()
        taps_copy.wait()

    return pl.pallas_call(
        body,
        in_specs=[SMEM, ANY, ANY, ANY, VMEM],
        out_specs=ANY,
        out_shape=jax.ShapeDtypeStruct((total, features), jnp.bfloat16),
        scratch_shapes=[pltpu.VMEM((4 * count, features), jnp.bfloat16), pltpu.SemaphoreType.DMA((parts + 2,))],
        name="section_packet",
    )(core, key_weight, value_weight, hidden, taps)


def dense(place, own, sums, tail, packet, other_packet, depth, chunk, taps_count):
    features = packet.shape[1]
    rows = chunk + HALO

    def body(place_ref, own_ref, *refs):
        sums_refs, refs = refs[: len(sums)], refs[len(sums) :]
        tail_ref, packet_ref, other_ref, out_ref, product_ref, normed_ref = refs
        total = own_ref[...]
        for sums_ref in sums_refs:
            total = total + sums_ref[...].astype(jnp.float32)
        packed = total.astype(jnp.bfloat16)
        core = place_ref[1]
        product_ref[core] = jnp.dot(packed, packet_ref[:depth], preferred_element_type=jnp.float32)
        product_ref[1 - core] = jnp.dot(packed, other_ref[:depth], preferred_element_type=jnp.float32)

        def gate(at, states):
            states = states.astype(jnp.float32)
            keys = product_ref[0, pl.ds(at, HALO)]
            mean_states = jnp.mean(states * states, axis=-1, keepdims=True)
            mean_keys = jnp.mean(keys * keys, axis=-1, keepdims=True)
            affinity = jnp.sum(states * keys, axis=-1, keepdims=True)
            affinity = affinity * lax.rsqrt(mean_states + 1e-06) * lax.rsqrt(mean_keys + 1e-06)
            gated = jax.nn.sigmoid(affinity / math.sqrt(features)) * product_ref[1, pl.ds(at, HALO)]
            product_ref[1, pl.ds(at, HALO)] = gated
            return gated * lax.rsqrt(jnp.mean(gated * gated, axis=-1, keepdims=True) + 1e-06)

        normed_ref[:HALO] = jnp.where(place_ref[0] > 0, gate(0, tail_ref[:HALO]), 0.0)
        terms = packet_ref[depth + chunk :].astype(jnp.float32)
        taps = terms[:taps_count] + terms[taps_count : 2 * taps_count] + terms[2 * taps_count : 3 * taps_count]

        def step(i, carry):
            at = pl.multiple_of((i + 1) * HALO, HALO)
            before = pl.multiple_of(i * HALO, HALO)
            states = packet_ref[pl.ds(pl.multiple_of(depth + i * HALO, HALO), HALO)]
            normed = gate(at, states)
            normed_ref[pl.ds(at, HALO)] = normed
            window = jnp.concatenate([normed_ref[pl.ds(before, HALO)], normed], axis=0)
            convolved = taps[0:1] * normed
            for k in range(1, taps_count):
                start = HALO - k * CONV_DILATION
                convolved = convolved + taps[k : k + 1] * window[start : start + HALO]
            branch = convolved * jax.nn.sigmoid(convolved) + product_ref[1, pl.ds(at, HALO)]
            out_ref[pl.ds(before, HALO)] = (states.astype(jnp.float32) + branch).astype(jnp.bfloat16)
            return carry

        lax.fori_loop(0, chunk // HALO, step, 0)

    return pl.pallas_call(
        body,
        in_specs=[SMEM] + [VMEM] * (4 + len(sums)),
        out_specs=VMEM,
        out_shape=jax.ShapeDtypeStruct((chunk, features), jnp.bfloat16),
        scratch_shapes=[
            pltpu.VMEM((2, rows, features), jnp.float32),
            pltpu.VMEM((rows, features), jnp.float32),
        ],
        name="dense",
    )(place, own, *sums, tail, packet, other_packet)


def local(hidden, owner, slot, memory_table, key_weight, value_weight, conv_weight):
    bf16 = jnp.bfloat16
    tok_rows, head_count = owner.shape[1:]
    rows_dev, row_features = memory_table.shape[1:]
    x, y, core = (lax.axis_index(name) for name in TABLE)

    table = rotated(memory_table[0], "segment", 1)
    numbers, tail = edge_packet(hidden[0], owner[0].T, slot[0].T)
    numbers = rotated(numbers, "segment", 1)
    shards = NX * NY * NC
    sections = lax.axis_size("segment")
    tail = lax.ppermute(
        tail,
        TABLE + ("segment",),
        [
            (i * sections + s, (i + 1) * sections + (s + 1) % sections)
            for i in range(shards - 1)
            for s in range(sections)
        ],
    )
    packet = section_packet(
        core.astype(jnp.int32).reshape(1), key_weight[0], value_weight[0], hidden[0], conv_weight[0]
    )
    packet = rotated(packet, "segment", 1)
    other_packet = rotated(packet, "core", 1)

    copies = jnp.broadcast_to(table[None], (NY, rows_dev, row_features))
    own_rows = lax.all_to_all(copies, "y", split_axis=0, concat_axis=0, tiled=True)
    own_rows = own_rows.reshape(NY * rows_dev, row_features)
    other_rows = rotated(own_rows, "core", 1)

    head_numbers = tail[HALO:, 128 - HALO : 128].astype(jnp.int32)
    numbers = jnp.concatenate([head_numbers, numbers], axis=1)
    place = lax.broadcasted_iota(jnp.int32, (shards, 1), 0)
    ahead, swapped, far = place // (NY * NC), place // NY % NC, place % NY
    shard = (x + ahead) % NX * (NY * NC) + far * NC + (core ^ swapped)
    asked = jnp.full((shards, tok_rows + HALO), -1, jnp.int32)
    for h in range(head_count):
        asked = jnp.maximum(
            asked, jnp.where(numbers[h][None, :] == shard, numbers[head_count + h][None, :], -1)
        )
    asked = asked.reshape(NX, NY * NC, tok_rows + HALO)
    received = [asked[0]]
    for ahead in range(1, NX):
        received.append(rotated(asked[ahead], "x", ahead))
    asked = jnp.stack(received).transpose(0, 2, 1)
    pick_own, pick_other = pick_matrices(asked, rows_dev)

    rows = tok_rows + HALO
    rows = tok_rows + HALO
    own_part = jnp.dot(
        pick_own[1:].reshape((NX - 1) * rows, -1), own_rows, preferred_element_type=jnp.float32
    ).reshape(NX - 1, rows, -1)
    sums = []
    for back in (2, 1, 3):
        part = own_part[back - 1] + jnp.dot(pick_other[back], other_rows, preferred_element_type=jnp.float32)
        sums.append(rotated(part.astype(bf16), "x", -back))
    mine = jnp.dot(pick_own[0], own_rows, preferred_element_type=jnp.float32) + jnp.dot(
        pick_other[0], other_rows, preferred_element_type=jnp.float32
    )
    later = (x > 0) | (y > 0) | (core > 0)
    place = jnp.stack([later.astype(jnp.int32), core.astype(jnp.int32)])
    taps_count, depth = conv_weight.shape[1], key_weight.shape[1]
    return dense(place, mine, sums, tail, packet, other_packet, depth, tok_rows, taps_count)[None]


def solution(mesh):
    grid = Mesh(mesh.devices.reshape(NX, NY, NC, -1), TABLE + ("segment",))
    in_specs = (
        P("segment", TABLE, None),
        P("segment", TABLE, None),
        P("segment", TABLE, None),
        P("segment", TABLE, None),
        P("segment", None, None),
        P("segment", None, None),
        P("segment", None, None),
    )
    out_specs = P("segment", TABLE, None)

    return jax.shard_map(local, mesh=grid, in_specs=in_specs, out_specs=out_specs, check_vma=False)
```

time: 126 us -> 209 us (1.66)
  Pallas kernels: 11.7 us -> 87.8 us
  waiting for transfers between devices: 48.6 us -> 65.5 us
  starting transfers between devices: 49.6 us -> 41.7 us
    pallas_call x1 -> x3, Pallas kernels: 6.4 us -> 82.5 us  [the longest x1 71.4 us: section_packet(): pl.pallas_call(body, in_specs=[SMEM, ANY, ANY, ANY, VMEM], out_specs=ANY,...]
    ppermute x1, waiting for transfers between devices: 7.76 us -> 45.1 us  [local(): lax.ppermute(tail, TABLE + ('segment',), [(i * sections + s, (i + 1) * se...]
    all_to_all x1, waiting for transfers between devices: 22.9 us -> 0.01 us  [local(): lax.all_to_all(copies, 'y', split_axis=0, concat_axis=0, tiled=True)]
    ppermute x13 -> x11, starting transfers between devices: 37.2 us -> 29.4 us  [rotated(): lax.ppermute(value, axis, [(i, (i + by) % count) for i in range(count)])]
    ppermute x13 -> x11, waiting for transfers between devices: 18 us -> 20.4 us  [rotated(): lax.ppermute(value, axis, [(i, (i + by) % count) for i in range(count)])]
    dot_general x1 -> x3, matrix products: 4.04 us -> 4.57 us  [the longest x1 2.51 us: local(): jnp.dot(pick_own[0], own_rows, preferred_element_type=jnp.float32)]
  transfers between devices with their start and end apart: 15 -> 13, of which waited for: 5 -> 5; matrix products, arithmetic and copies ran while one was open for 10% -> 5% of each run, Pallas kernels for 4% -> 38%
where the time goes in v3:
time: 209 us; the launch traced here: 207 us
  Pallas kernels  87.8 us (42%)
  waiting for transfers between devices  65.5 us (31%)
  starting transfers between devices  41.7 us (20%)
  matrix products  6.36 us (3%)
  local copies, waits for them, and re-layouts  3.95 us (2%)
    pallas_call x1, Pallas kernels, section_packet(): pl.pallas_call(body, in_specs=[SMEM, ANY, ANY, ANY, VMEM], out_specs=ANY,...  71.4 us
    ppermute x1, waiting for transfers between devices, local(): lax.ppermute(tail, TABLE + ('segment',), [(i * sections + s, (i + 1) * se...  45.1 us
    ppermute x11, starting transfers between devices, rotated(): lax.ppermute(value, axis, [(i, (i + by) % count) for i in range(count)])  29.4 us
    ppermute x11, waiting for transfers between devices, rotated(): lax.ppermute(value, axis, [(i, (i + by) % count) for i in range(count)])  20.4 us
    pallas_call x1, Pallas kernels, dense(): pl.pallas_call(body, in_specs=[SMEM] + [VMEM] * (4 + len(sums)), out_spec...  9.66 us
    all_to_all x1, starting transfers between devices, local(): lax.all_to_all(copies, 'y', split_axis=0, concat_axis=0, tiled=True)  6.82 us
    ppermute x1, starting transfers between devices, local(): lax.ppermute(tail, TABLE + ('segment',), [(i * sections + s, (i + 1) * se...  5.49 us
    pallas_call x1, Pallas kernels, pick_matrices(): pl.pallas_call(body, in_specs=[VMEM], out_specs=[VMEM, VMEM], out_shape=[...  5.31 us
  transfers between devices with their start and end apart: 13, of which 5 were waited for; matrix products, arithmetic and copies ran while one was open for 5% of the time, Pallas kernels for 38%

profile of v3, /device:TPU:1, one launch (start us, length us, event | category | flops | bytes accessed | tf_op | source)
XLA Modules:
  0.0 206.6 jit_solution(6798370614614686050)
XLA Ops:
  0.0 4.8 %collective-permute-start.5 = (bf16[128,640]{1,0:T(8,128)(2,1)}, bf16[128,640]{1,0:T(8,128)(2,1)S(1)}, u32[]{:S(2)}, u32[]{:S(2)}) collective-permute-start(bf16[128,640]{1,0:T(8,128)(2,1)} %bitcast.65), channel_id=1, source_target_pairs={{0,1},{1,2},{2,3},{3,4},{4,5},{5,6},{6,7},{7,0},{8,9},{9,10},{10,1... | collective-permute-start | bytes 491528 | tf_op jit(solution)/shard_map/ppermute | solution.py:19
  4.8 10.8 %collective-permute-done.5 = bf16[128,640]{1,0:T(8,128)(2,1)S(1)} collective-permute-done((bf16[128,640]{1,0:T(8,128)(2,1)}, bf16[128,640]{1,0:T(8,128)(2,1)S(1)}, u32[]{:S(2)}, u32[]{:S(2)}) %collective-permute-start.5) | collective-permute-done | bytes 163872 | tf_op jit(solution)/shard_map/ppermute | solution.py:19
  16.8 6.8 %all-to-all-start = ((bf16[8,128,640]{2,1,0:T(8,128)(2,1)}), bf16[8,128,640]{2,1,0:T(8,128)(2,1)S(1)}, u32[]{:S(2)}, u32[]{:S(2)}) async-start(bf16[8,128,640]{2,1,0:T(8,128)(2,1)} %broadcast_in_dim.97), calls=%async_computation | async-start | bytes 2621440 | tf_op jit(solution)/shard_map/all_to_all | solution.py:217
  23.6 71.4 %section_packet.1 = bf16[912,1280]{1,0:T(8,128)(2,1)} custom-call(s32[1]{0:T(128)} %bitcast.1.core_ref, bf16[640,1280]{1,0:T(8,128)(2,1)} %bitcast.57, bf16[640,1280]{1,0:T(8,128)(2,1)} %bitcast.58, bf16[256,1280]{1,0:T(8,128)(2,1)} %bitcast.53, f32[4,1280]{1,0:T(4,128)} %bitcast.62), custom_call_target="tpu_custom_call" | custom-call | tf_op jit(solution)/shard_map/section_packet/pallas_call | solution.py:120
  95.0 1.9 collective-permute-start.10
  98.4 1.9 collective-permute-start.1
  100.3 5.5 %collective-permute-start = (bf16[32,1280]{1,0:T(8,128)(2,1)}, bf16[32,1280]{1,0:T(8,128)(2,1)S(1)}, u32[]{:S(2)}, u32[]{:S(2)}) collective-permute-start(bf16[32,1280]{1,0:T(8,128)(2,1)} %get-tuple-element.9), channel_id=1, source_target_pairs={{0,9},{1,10},{2,11},{3,12},{4,13},{5,14},{6,15},{7,8},{8,17},{9,18... | collective-permute-start | bytes 245768 | tf_op jit(solution)/shard_map/ppermute | solution.py:201
  105.8 1.9 collective-permute-start.6
  107.8 45.1 %collective-permute-done.refs_3_ = bf16[32,1280]{1,0:T(8,128)(2,1)S(1)} collective-permute-done((bf16[32,1280]{1,0:T(8,128)(2,1)}, bf16[32,1280]{1,0:T(8,128)(2,1)S(1)}, u32[]{:S(2)}, u32[]{:S(2)}) %collective-permute-start) | collective-permute-done | bytes 81952 | tf_op jit(solution)/shard_map/ppermute | solution.py:201
  153.2 1.9 collective-permute-start.11
  155.3 3.5 %collective-permute-start.4 = (s32[16,272]{1,0:T(8,128)S(1)}, s32[16,272]{1,0:T(8,128)S(1)}, u32[]{:S(2)}, u32[]{:S(2)}) collective-permute-start(s32[16,272]{1,0:T(8,128)S(1)} %get-tuple-element.30), channel_id=1, source_target_pairs={{0,384},{128,0},{256,128},{384,256},{1,385},{129,1},{257,129},{385... | collective-permute-start | bytes 52232 | tf_op jit(solution)/shard_map/ppermute | solution.py:19
  158.8 3.3 %collective-permute-start.3 = (s32[16,272]{1,0:T(8,128)S(1)}, s32[16,272]{1,0:T(8,128)S(1)}, u32[]{:S(2)}, u32[]{:S(2)}) collective-permute-start(s32[16,272]{1,0:T(8,128)S(1)} %get-tuple-element.31), channel_id=1, source_target_pairs={{0,256},{128,384},{256,0},{384,128},{1,257},{129,385},{257,1},{385... | collective-permute-start | bytes 52232 | tf_op jit(solution)/shard_map/ppermute | solution.py:19
  162.1 2.5 %collective-permute-start.2 = (s32[16,272]{1,0:T(8,128)S(1)}, s32[16,272]{1,0:T(8,128)S(1)}, u32[]{:S(2)}, u32[]{:S(2)}) collective-permute-start(s32[16,272]{1,0:T(8,128)S(1)} %get-tuple-element.32), channel_id=1, source_target_pairs={{0,128},{128,256},{256,384},{384,0},{1,129},{129,257},{257,385},{3... | collective-permute-start | bytes 52232 | tf_op jit(solution)/shard_map/ppermute | solution.py:19
  165.3 2.7 %collective-permute-done.2 = s32[16,272]{1,0:T(8,128)S(1)} collective-permute-done((s32[16,272]{1,0:T(8,128)S(1)}, s32[16,272]{1,0:T(8,128)S(1)}, u32[]{:S(2)}, u32[]{:S(2)}) %collective-permute-start.2) | collective-permute-done | bytes 17440 | tf_op jit(solution)/shard_map/ppermute | solution.py:19
  168.9 5.3 %pick_matrices.1 = (bf16[4,272,1024]{2,1,0:T(8,128)(2,1)}, bf16[4,272,1024]{2,1,0:T(8,128)(2,1)}) custom-call(s32[4,272,16]{2,1,0:T(8,128)} %bitcast.55), custom_call_target="tpu_custom_call" | custom-call | tf_op jit(solution)/shard_map/pick_matrices/pallas_call | solution.py:40
  174.3 1.6 slice.123
  175.9 1.5 fusion.62
  178.1 2.3 %collective-permute-start.7 = (bf16[272,640]{1,0:T(8,128)(2,1)S(1)}, bf16[272,640]{1,0:T(8,128)(2,1)S(1)}, u32[]{:S(2)}, u32[]{:S(2)}) collective-permute-start(bf16[272,640]{1,0:T(8,128)(2,1)S(1)} %fusion.2), channel_id=1, source_target_pairs={{0,256},{128,384},{256,0},{384,128},{1,257},{129,385},{257,1},{385... | collective-permute-start | bytes 1044488 | tf_op jit(solution)/shard_map/ppermute | solution.py:19
  181.0 3.3 %collective-permute-start.8 = (bf16[272,640]{1,0:T(8,128)(2,1)S(1)}, bf16[272,640]{1,0:T(8,128)(2,1)S(1)}, u32[]{:S(2)}, u32[]{:S(2)}) collective-permute-start(bf16[272,640]{1,0:T(8,128)(2,1)S(1)} %fusion.1), channel_id=1, source_target_pairs={{0,384},{128,0},{256,128},{384,256},{1,385},{129,1},{257,129},{385... | collective-permute-start | bytes 1044488 | tf_op jit(solution)/shard_map/ppermute | solution.py:19
  184.9 1.9 collective-permute-start.9
  187.5 2.5 %convolution_add_fusion.own_ref = f32[272,640]{1,0:T(8,128)} fusion(f32[272,640]{1,0:T(8,128)S(1)} %fusion.15, bf16[1024,640]{1,0:T(8,128)(2,1)S(1)} %bitcast.52, bf16[4,272,1024]{2,1,0:T(8,128)(2,1)} %get-tuple-element.11), kind=kOutput, calls=%fused_computation | convolution fusion | flops 356689920 | bytes 3260416 | tf_op jit(solution)/shard_map/dot_general | solution.py:247
  190.0 4.7 %collective-permute-done.8.refs_1_ = bf16[272,640]{1,0:T(8,128)(2,1)S(1)} collective-permute-done((bf16[272,640]{1,0:T(8,128)(2,1)S(1)}, bf16[272,640]{1,0:T(8,128)(2,1)S(1)}, u32[]{:S(2)}, u32[]{:S(2)}) %collective-permute-start.8) | collective-permute-done | bytes 348192 | tf_op jit(solution)/shard_map/ppermute | solution.py:19
  194.7 2.3 %collective-permute-done.9.refs_2_ = bf16[272,640]{1,0:T(8,128)(2,1)} collective-permute-done((bf16[272,640]{1,0:T(8,128)(2,1)S(1)}, bf16[272,640]{1,0:T(8,128)(2,1)}, u32[]{:S(2)}, u32[]{:S(2)}) %collective-permute-start.9) | collective-permute-done | bytes 348192 | tf_op jit(solution)/shard_map/ppermute | solution.py:19
  196.9 9.7 %dense.1 = bf16[256,1280]{1,0:T(8,128)(2,1)} custom-call(s32[2]{0:T(128)} %pad_add_fusion.2.place_ref, f32[272,640]{1,0:T(8,128)} %convolution_add_fusion.own_ref, bf16[272,640]{1,0:T(8,128)(2,1)} %copy-done.1, bf16[272,640]{1,0:T(8,128)(2,1)} %copy-done.2, bf16[272,640]{1,0:T(8,128)(2,1)} %collective-permute-done.9.refs_2_, bf16[32,1280]{1,0:T(8,128)(2,1)} %copy-done.3, ...), custom_call_target="tpu_custom_call" | custom-call | tf_op jit(solution)/shard_map/dense/pallas_call | solution.py:177
  (31 shorter events, 7.3 us)
Async XLA Ops:
  0.0 15.6 %collective-permute-start.5 = (bf16[128,640]{1,0:T(8,128)(2,1)}, bf16[128,640]{1,0:T(8,128)(2,1)S(1)}, u32[]{:S(2)}, u32[]{:S(2)}) collective-permute-start(bf16[128,640]{1,0:T(8,128)(2,1)} %bitcast.65), channel_id=1, source_target_pairs={{0,1},{1,2},{2,3},{3,4},{4,5},{5,6},{6,7},{7,0},{8,9},{9,10},{10,1... | collective-permute-start | bytes 491528 | tf_op jit(solution)/shard_map/ppermute | solution.py:19
  16.8 89.0 %all-to-all-start = ((bf16[8,128,640]{2,1,0:T(8,128)(2,1)}), bf16[8,128,640]{2,1,0:T(8,128)(2,1)S(1)}, u32[]{:S(2)}, u32[]{:S(2)}) async-start(bf16[8,128,640]{2,1,0:T(8,128)(2,1)} %broadcast_in_dim.97), calls=%async_computation | async-start | bytes 2621440 | tf_op jit(solution)/shard_map/all_to_all | solution.py:217
  95.0 58.2 %collective-permute-start.10 = (bf16[912,1280]{1,0:T(8,128)(2,1)}, bf16[912,1280]{1,0:T(8,128)(2,1)}, u32[]{:S(2)}, u32[]{:S(2)}) collective-permute-start(bf16[912,1280]{1,0:T(8,128)(2,1)} %section_packet.1), channel_id=1, source_target_pairs={{0,1},{1,2},{2,3},{3,4},{4,5},{5,6},{6,7},{7,0},{8,9},{9,10},{10,1... | collective-permute-start | bytes 7004168 | tf_op jit(solution)/shard_map/ppermute | solution.py:19
  98.4 54.6 %collective-permute-start.1 = (s32[16,256]{1,0:T(8,128)}, s32[16,256]{1,0:T(8,128)S(1)}, u32[]{:S(2)}, u32[]{:S(2)}) collective-permute-start(s32[16,256]{1,0:T(8,128)} %get-tuple-element.10), channel_id=1, source_target_pairs={{0,1},{1,2},{2,3},{3,4},{4,5},{5,6},{6,7},{7,0},{8,9},{9,10},{10,1... | collective-permute-start | bytes 49160 | tf_op jit(solution)/shard_map/ppermute | solution.py:19
  100.3 52.6 %collective-permute-start = (bf16[32,1280]{1,0:T(8,128)(2,1)}, bf16[32,1280]{1,0:T(8,128)(2,1)S(1)}, u32[]{:S(2)}, u32[]{:S(2)}) collective-permute-start(bf16[32,1280]{1,0:T(8,128)(2,1)} %get-tuple-element.9), channel_id=1, source_target_pairs={{0,9},{1,10},{2,11},{3,12},{4,13},{5,14},{6,15},{7,8},{8,17},{9,18... | collective-permute-start | bytes 245768 | tf_op jit(solution)/shard_map/ppermute | solution.py:201
  105.8 71.5 %collective-permute-start.6 = (bf16[1024,640]{1,0:T(8,128)(2,1)S(1)}, bf16[1024,640]{1,0:T(8,128)(2,1)S(1)}, u32[]{:S(2)}, u32[]{:S(2)}) collective-permute-start(bf16[1024,640]{1,0:T(8,128)(2,1)S(1)} %bitcast.50), channel_id=1, source_target_pairs={{0,8},{8,0},{1,9},{9,1},{2,10},{10,2},{3,11},{11,3},{4,12},{12,4},... | collective-permute-start | bytes 3932168 | tf_op jit(solution)/shard_map/ppermute | solution.py:19
  152.8 23.0 %copy-start.3 = (bf16[32,1280]{1,0:T(8,128)(2,1)}, bf16[32,1280]{1,0:T(8,128)(2,1)S(1)}, u32[]{:S(2)}) copy-start(bf16[32,1280]{1,0:T(8,128)(2,1)S(1)} %collective-permute-done.refs_3_) | copy-start | bytes 245764
  153.2 43.8 %collective-permute-start.11 = (bf16[912,1280]{1,0:T(8,128)(2,1)}, bf16[912,1280]{1,0:T(8,128)(2,1)}, u32[]{:S(2)}, u32[]{:S(2)}) collective-permute-start(bf16[912,1280]{1,0:T(8,128)(2,1)} %collective-permute-done.10.refs_4_), channel_id=1, source_target_pairs={{0,8},{8,0},{1,9},{9,1},{2,10},{10,2},{3,11},{11,3},{4,12},{12,4},... | collective-permute-start | bytes 7004168 | tf_op jit(solution)/shard_map/ppermute | solution.py:19
  155.3 9.9 %collective-permute-start.4 = (s32[16,272]{1,0:T(8,128)S(1)}, s32[16,272]{1,0:T(8,128)S(1)}, u32[]{:S(2)}, u32[]{:S(2)}) collective-permute-start(s32[16,272]{1,0:T(8,128)S(1)} %get-tuple-element.30), channel_id=1, source_target_pairs={{0,384},{128,0},{256,128},{384,256},{1,385},{129,1},{257,129},{385... | collective-permute-start | bytes 52232 | tf_op jit(solution)/shard_map/ppermute | solution.py:19
  158.8 6.4 %collective-permute-start.3 = (s32[16,272]{1,0:T(8,128)S(1)}, s32[16,272]{1,0:T(8,128)S(1)}, u32[]{:S(2)}, u32[]{:S(2)}) collective-permute-start(s32[16,272]{1,0:T(8,128)S(1)} %get-tuple-element.31), channel_id=1, source_target_pairs={{0,256},{128,384},{256,0},{384,128},{1,257},{129,385},{257,1},{385... | collective-permute-start | bytes 52232 | tf_op jit(solution)/shard_map/ppermute | solution.py:19
  162.1 5.8 %collective-permute-start.2 = (s32[16,272]{1,0:T(8,128)S(1)}, s32[16,272]{1,0:T(8,128)S(1)}, u32[]{:S(2)}, u32[]{:S(2)}) collective-permute-start(s32[16,272]{1,0:T(8,128)S(1)} %get-tuple-element.32), channel_id=1, source_target_pairs={{0,128},{128,256},{256,384},{384,0},{1,129},{129,257},{257,385},{3... | collective-permute-start | bytes 52232 | tf_op jit(solution)/shard_map/ppermute | solution.py:19
  175.8 1.6 copy-start
  178.1 11.9 %collective-permute-start.7 = (bf16[272,640]{1,0:T(8,128)(2,1)S(1)}, bf16[272,640]{1,0:T(8,128)(2,1)S(1)}, u32[]{:S(2)}, u32[]{:S(2)}) collective-permute-start(bf16[272,640]{1,0:T(8,128)(2,1)S(1)} %fusion.2), channel_id=1, source_target_pairs={{0,256},{128,384},{256,0},{384,128},{1,257},{129,385},{257,1},{385... | collective-permute-start | bytes 1044488 | tf_op jit(solution)/shard_map/ppermute | solution.py:19
  181.0 13.7 %collective-permute-start.8 = (bf16[272,640]{1,0:T(8,128)(2,1)S(1)}, bf16[272,640]{1,0:T(8,128)(2,1)S(1)}, u32[]{:S(2)}, u32[]{:S(2)}) collective-permute-start(bf16[272,640]{1,0:T(8,128)(2,1)S(1)} %fusion.1), channel_id=1, source_target_pairs={{0,384},{128,0},{256,128},{384,256},{1,385},{129,1},{257,129},{385... | collective-permute-start | bytes 1044488 | tf_op jit(solution)/shard_map/ppermute | solution.py:19
  184.9 12.0 %collective-permute-start.9 = (bf16[272,640]{1,0:T(8,128)(2,1)S(1)}, bf16[272,640]{1,0:T(8,128)(2,1)}, u32[]{:S(2)}, u32[]{:S(2)}) collective-permute-start(bf16[272,640]{1,0:T(8,128)(2,1)S(1)} %fusion), channel_id=1, source_target_pairs={{0,128},{128,256},{256,384},{384,0},{1,129},{129,257},{257,385},{3... | collective-permute-start | bytes 1044488 | tf_op jit(solution)/shard_map/ppermute | solution.py:19
  190.0 7.0 %copy-start.1 = (bf16[272,640]{1,0:T(8,128)(2,1)}, bf16[272,640]{1,0:T(8,128)(2,1)S(1)}, u32[]{:S(2)}) copy-start(bf16[272,640]{1,0:T(8,128)(2,1)S(1)} %collective-permute-done.7.refs_0_) | copy-start | bytes 1044484
  194.7 2.3 %copy-start.2 = (bf16[272,640]{1,0:T(8,128)(2,1)}, bf16[272,640]{1,0:T(8,128)(2,1)S(1)}, u32[]{:S(2)}) copy-start(bf16[272,640]{1,0:T(8,128)(2,1)S(1)} %collective-permute-done.8.refs_1_) | copy-start | bytes 1044484

commit v4 on v0

v4 whole, which is shorter than its diff:
```python
import math

import jax
import jax.numpy as jnp
from jax import lax
from jax.experimental import pallas as pl
from jax.experimental.pallas import tpu as pltpu
from jax.sharding import Mesh, PartitionSpec as P


CONV_DILATION = 3
NX, NY, NC = 4, 8, 2
HALO = 16
TABLE = ("x", "y", "core")


def rotated(value, axis, by):
    count = lax.axis_size(axis)
    return lax.ppermute(value, axis, [(i, (i + by) % count) for i in range(count)])


VMEM = pl.BlockSpec(memory_space=pltpu.VMEM)


def pick_matrices(asked, rows_dev):
    groups, rows, _ = asked.shape

    def body(asked_ref, own_ref, other_ref):
        lane = lax.broadcasted_iota(jnp.int32, (rows, rows_dev), 1)
        for group in range(groups):
            for swapped, out_ref in ((0, own_ref), (1, other_ref)):
                for far in range(NY):
                    column = swapped * NY + far
                    hit = asked_ref[group, :, column : column + 1] == lane
                    hit = hit.astype(jnp.float32).astype(jnp.bfloat16)
                    out_ref[group, :, far * rows_dev : (far + 1) * rows_dev] = hit

    shape = jax.ShapeDtypeStruct((groups, rows, NY * rows_dev), jnp.bfloat16)
    return pl.pallas_call(
        body,
        in_specs=[VMEM],
        out_specs=[VMEM, VMEM],
        out_shape=[shape, shape],
        name="pick_matrices",
    )(asked)


def rms_scale(values):
    return values * lax.rsqrt(jnp.mean(values * values, axis=-1, keepdims=True) + 1e-06)


def edge_packet(hidden, owners, slots):
    heads, tok_rows = owners.shape
    features = hidden.shape[1]

    def body(hidden_ref, owners_ref, slots_ref, numbers_ref, tail_ref):
        numbers_ref[:heads] = owners_ref[...]
        numbers_ref[heads:] = slots_ref[...]
        tail_ref[:HALO] = hidden_ref[...]
        last = numbers_ref[:, tok_rows - 128 :].astype(jnp.float32)
        tail_ref[HALO:, :128] = last.astype(jnp.bfloat16)
        tail_ref[HALO:, 128:] = jnp.zeros((2 * heads, features - 128), jnp.bfloat16)

    return pl.pallas_call(
        body,
        grid=(1,),
        in_specs=[
            pl.BlockSpec((HALO, features), lambda i: (tok_rows // HALO - 1, 0)),
            pl.BlockSpec((heads, tok_rows), lambda i: (0, 0)),
            pl.BlockSpec((heads, tok_rows), lambda i: (0, 0)),
        ],
        out_specs=[
            pl.BlockSpec((2 * heads, tok_rows), lambda i: (0, 0)),
            pl.BlockSpec((HALO + 2 * heads, features), lambda i: (0, 0)),
        ],
        out_shape=[
            jax.ShapeDtypeStruct((2 * heads, tok_rows), jnp.int32),
            jax.ShapeDtypeStruct((HALO + 2 * heads, features), jnp.bfloat16),
        ],
        name="edge_packet",
    )(hidden, owners, slots)


def local(hidden, owner, slot, memory_table, key_weight, value_weight, conv_weight):
    bf16 = jnp.bfloat16
    tok_rows, head_count = owner.shape[1:]
    features = hidden.shape[2]
    rows_dev, row_features = memory_table.shape[1:]
    x, y, core = (lax.axis_index(name) for name in TABLE)
    first = (x == 0) & (y == 0) & (core == 0)

    table = rotated(memory_table[0], "segment", 1)
    numbers, tail = edge_packet(hidden[0], owner[0].T, slot[0].T)
    numbers = rotated(numbers, "segment", 1)
    shards = NX * NY * NC
    sections = lax.axis_size("segment")
    tail = lax.ppermute(
        tail,
        TABLE + ("segment",),
        [
            (i * sections + s, (i + 1) * sections + (s + 1) % sections)
            for i in range(shards - 1)
            for s in range(sections)
        ],
    )
    states = rotated(hidden[0], "segment", 1)
    weight_one = jnp.where(core == 0, key_weight[0], value_weight[0])
    weight_one = rotated(weight_one, "segment", 1)
    weight_two = rotated(weight_one, "core", 1)
    taps = rotated(conv_weight[0], "segment", 1)

    copies = jnp.broadcast_to(table[None], (NY, rows_dev, row_features))
    own_rows = lax.all_to_all(copies, "y", split_axis=0, concat_axis=0, tiled=True)
    own_rows = own_rows.reshape(NY * rows_dev, row_features)
    other_rows = rotated(own_rows, "core", 1)

    head_numbers = tail[HALO:, 128 - HALO : 128].astype(jnp.int32)
    numbers = jnp.concatenate([head_numbers, numbers], axis=1)
    place = lax.broadcasted_iota(jnp.int32, (shards, 1), 0)
    ahead, swapped, far = place // (NY * NC), place // NY % NC, place % NY
    shard = (x + ahead) % NX * (NY * NC) + far * NC + (core ^ swapped)
    asked = jnp.full((shards, tok_rows + HALO), -1, jnp.int32)
    for h in range(head_count):
        asked = jnp.maximum(
            asked, jnp.where(numbers[h][None, :] == shard, numbers[head_count + h][None, :], -1)
        )
    asked = asked.reshape(NX, NY * NC, tok_rows + HALO)
    received = [asked[0]]
    for ahead in range(1, NX):
        received.append(rotated(asked[ahead], "x", ahead))
    asked = jnp.stack(received).transpose(0, 2, 1)
    pick_own, pick_other = pick_matrices(asked, rows_dev)

    rows = tok_rows + HALO
    pick_sent = pick_own[1:].reshape((NX - 1) * rows, -1)
    own_part = jnp.dot(pick_sent, own_rows, preferred_element_type=jnp.float32).reshape(NX - 1, rows, -1)
    sums = []
    for back in (2, 1, 3):
        part = own_part[back - 1] + jnp.dot(pick_other[back], other_rows, preferred_element_type=jnp.float32)
        sums.append(rotated(part.astype(bf16), "x", -back))
    total = jnp.dot(pick_own[0], own_rows, preferred_element_type=jnp.float32) + jnp.dot(
        pick_other[0], other_rows, preferred_element_type=jnp.float32
    )
    total = lax.optimization_barrier(total)
    key_here = jnp.where(core == 0, weight_one, weight_two)
    value_here = jnp.where(core == 0, weight_two, weight_one)
    key_here, value_here = lax.optimization_barrier((key_here, value_here))
    for part in sums:
        total = total + part.astype(jnp.float32)
    packed = total.astype(bf16)

    states_float = jnp.concatenate([tail[:HALO], states], axis=0).astype(jnp.float32)
    keys_out = jnp.dot(packed, key_here, preferred_element_type=jnp.float32)
    values_out = jnp.dot(packed, value_here, preferred_element_type=jnp.float32)
    affinity = jnp.sum(rms_scale(states_float) * rms_scale(keys_out), axis=-1, keepdims=True) / math.sqrt(features)
    gated = jax.nn.sigmoid(affinity) * values_out
    normed = rms_scale(gated)
    before = lax.broadcasted_iota(jnp.int32, (rows, 1), 0) < HALO
    normed = jnp.where(before & first, 0.0, normed)
    convolved = jnp.zeros((tok_rows, features), jnp.float32)
    for k in range(taps.shape[0]):
        start = HALO - k * CONV_DILATION
        convolved = convolved + taps[k] * normed[start : start + tok_rows]
    branch = jax.nn.silu(convolved) + gated[HALO:]
    return (states_float[HALO:] + branch).astype(bf16)[None]


def solution(mesh):
    grid = Mesh(mesh.devices.reshape(NX, NY, NC, -1), TABLE + ("segment",))
    in_specs = (
        P("segment", TABLE, None),
        P("segment", TABLE, None),
        P("segment", TABLE, None),
        P("segment", TABLE, None),
        P("segment", None, None),
        P("segment", None, None),
        P("segment", None, None),
    )
    out_specs = P("segment", TABLE, None)

    return jax.shard_map(local, mesh=grid, in_specs=in_specs, out_specs=out_specs, check_vma=False)
```

time: 130 us -> 151 us (1.16)
  the two profiles are of different devices: /device:TPU:1 before, /device:TPU:47 now
where the time goes in v4:
time: 151 us; the launch traced here: 150 us
  waiting for transfers between devices  60.8 us (40%)
  starting transfers between devices  60 us (40%)
  matrix products  8.61 us (6%)
  other arithmetic  8.48 us (6%)
  Pallas kernels  6.69 us (4%)
  local copies, waits for them, and re-layouts  5.33 us (4%)
    ppermute x13, waiting for transfers between devices, rotated(): lax.ppermute(value, axis, [(i, (i + by) % count) for i in range(count)])  54.7 us
    ppermute x13, starting transfers between devices, rotated(): lax.ppermute(value, axis, [(i, (i + by) % count) for i in range(count)])  51.4 us
    all_to_all x1, starting transfers between devices, local(): lax.all_to_all(copies, 'y', split_axis=0, concat_axis=0, tiled=True)  6.66 us
    ppermute x1, waiting for transfers between devices, local(): lax.ppermute(tail, TABLE + ('segment',), [(i * sections + s, (i + 1) * se...  6.11 us
    pallas_call x1, Pallas kernels, pick_matrices(): pl.pallas_call(body, in_specs=[VMEM], out_specs=[VMEM, VMEM], out_shape=[...  5.24 us
  transfers between devices with their start and end apart: 15, of which 6 were waited for; matrix products, arithmetic and copies ran while one was open for 10% of the time, Pallas kernels for 4%

profile of v4, /device:TPU:47, one launch (start us, length us, event | category | flops | bytes accessed | tf_op | source)
XLA Modules:
  0.0 150.3 jit_solution(12110997904995864105)
XLA Ops:
  0.0 2.8 %select_bitcast_fusion = bf16[640,1280]{1,0:T(8,128)(2,1)} fusion(bf16[1,640,1280]{2,1,0:T(8,128)(2,1)} %param.11, bf16[1,640,1280]{2,1,0:T(8,128)(2,1)} %param.12, pred[]{:T(512)S(6)} %eq.62), kind=kLoop, calls=%fused_computation.1 | loop fusion | flops 819200 | bytes 4915201 | tf_op jit(solution)/shard_map/jit(_where)/select_n | solution.py:107
  2.8 4.0 %collective-permute-start.12 = (bf16[640,1280]{1,0:T(8,128)(2,1)}, bf16[640,1280]{1,0:T(8,128)(2,1)}, u32[]{:S(2)}, u32[]{:S(2)}) collective-permute-start(bf16[640,1280]{1,0:T(8,128)(2,1)} %select_bitcast_fusion), channel_id=1, source_target_pairs={{0,1},{1,2},{2,3},{3,4},{4,5},{5,6},{6,7},{7,0},{8,9},{9,10},{10,1... | collective-permute-start | bytes 4915208 | tf_op jit(solution)/shard_map/ppermute | solution.py:19
  6.8 4.0 %collective-permute-start.7 = (bf16[128,640]{1,0:T(8,128)(2,1)S(1)}, bf16[128,640]{1,0:T(8,128)(2,1)S(1)}, u32[]{:S(2)}, u32[]{:S(2)}) collective-permute-start(bf16[128,640]{1,0:T(8,128)(2,1)S(1)} %bitcast.65), channel_id=1, source_target_pairs={{0,1},{1,2},{2,3},{3,4},{4,5},{5,6},{6,7},{7,0},{8,9},{9,10},{10,1... | collective-permute-start | bytes 491528 | tf_op jit(solution)/shard_map/ppermute | solution.py:19
  10.8 41.9 %collective-permute-done.7 = bf16[128,640]{1,0:T(8,128)(2,1)S(1)} collective-permute-done((bf16[128,640]{1,0:T(8,128)(2,1)S(1)}, bf16[128,640]{1,0:T(8,128)(2,1)S(1)}, u32[]{:S(2)}, u32[]{:S(2)}) %collective-permute-start.7) | collective-permute-done | bytes 163872 | tf_op jit(solution)/shard_map/ppermute | solution.py:19
  53.9 6.7 %all-to-all-start = ((bf16[8,128,640]{2,1,0:T(8,128)(2,1)}), bf16[8,128,640]{2,1,0:T(8,128)(2,1)S(1)}, u32[]{:S(2)}, u32[]{:S(2)}) async-start(bf16[8,128,640]{2,1,0:T(8,128)(2,1)} %broadcast_in_dim.115), calls=%async_computation | async-start | bytes 2621440 | tf_op jit(solution)/shard_map/all_to_all | solution.py:113
  60.5 1.9 %collective-permute-start.1 = (bf16[256,1280]{1,0:T(8,128)(2,1)S(1)}, bf16[256,1280]{1,0:T(8,128)(2,1)S(1)}, u32[]{:S(2)}, u32[]{:S(2)}) collective-permute-start(bf16[256,1280]{1,0:T(8,128)(2,1)S(1)} %bitcast.59), channel_id=1, source_target_pairs={{0,1},{1,2},{2,3},{3,4},{4,5},{5,6},{6,7},{7,0},{8,9},{9,10},{10,1... | collective-permute-start | bytes 1966088 | tf_op jit(solution)/shard_map/ppermute | solution.py:19
  63.9 1.9 %collective-permute-start = (bf16[32,1280]{1,0:T(8,128)(2,1)}, bf16[32,1280]{1,0:T(8,128)(2,1)S(1)}, u32[]{:S(2)}, u32[]{:S(2)}) collective-permute-start(bf16[32,1280]{1,0:T(8,128)(2,1)} %get-tuple-element.11), channel_id=1, source_target_pairs={{0,9},{1,10},{2,11},{3,12},{4,13},{5,14},{6,15},{7,8},{8,17},{9,18... | collective-permute-start | bytes 245768 | tf_op jit(solution)/shard_map/ppermute | solution.py:97
  65.8 3.9 %collective-permute-start.3 = (s32[16,256]{1,0:T(8,128)}, s32[16,256]{1,0:T(8,128)S(1)}, u32[]{:S(2)}, u32[]{:S(2)}) collective-permute-start(s32[16,256]{1,0:T(8,128)} %get-tuple-element.12), channel_id=1, source_target_pairs={{0,1},{1,2},{2,3},{3,4},{4,5},{5,6},{6,7},{7,0},{8,9},{9,10},{10,1... | collective-permute-start | bytes 49160 | tf_op jit(solution)/shard_map/ppermute | solution.py:19
  69.8 5.3 %collective-permute-start.2 = (f32[4,1280]{1,0:T(4,128)S(1)}, f32[4,1280]{1,0:T(4,128)S(1)}, u32[]{:S(2)}, u32[]{:S(2)}) collective-permute-start(f32[4,1280]{1,0:T(4,128)S(1)} %bitcast.66), channel_id=1, source_target_pairs={{0,1},{1,2},{2,3},{3,4},{4,5},{5,6},{6,7},{7,0},{8,9},{9,10},{10,1... | collective-permute-start | bytes 61448 | tf_op jit(solution)/shard_map/ppermute | solution.py:19
  75.1 1.9 %collective-permute-start.13 = (bf16[640,1280]{1,0:T(8,128)(2,1)}, bf16[640,1280]{1,0:T(8,128)(2,1)}, u32[]{:S(2)}, u32[]{:S(2)}) collective-permute-start(bf16[640,1280]{1,0:T(8,128)(2,1)} %collective-permute-done.12), channel_id=1, source_target_pairs={{0,8},{8,0},{1,9},{9,1},{2,10},{10,2},{3,11},{11,3},{4,12},{12,4},... | collective-permute-start | bytes 4915208 | tf_op jit(solution)/shard_map/ppermute | solution.py:19
  77.1 6.1 %collective-permute-done = bf16[32,1280]{1,0:T(8,128)(2,1)S(1)} collective-permute-done((bf16[32,1280]{1,0:T(8,128)(2,1)}, bf16[32,1280]{1,0:T(8,128)(2,1)S(1)}, u32[]{:S(2)}, u32[]{:S(2)}) %collective-permute-start) | collective-permute-done | bytes 81952 | tf_op jit(solution)/shard_map/ppermute | solution.py:97
  83.7 2.1 %collective-permute-start.4 = (s32[16,272]{1,0:T(8,128)S(1)}, s32[16,272]{1,0:T(8,128)S(1)}, u32[]{:S(2)}, u32[]{:S(2)}) collective-permute-start(s32[16,272]{1,0:T(8,128)S(1)} %get-tuple-element.42), channel_id=1, source_target_pairs={{0,128},{128,256},{256,384},{384,0},{1,129},{129,257},{257,385},{3... | collective-permute-start | bytes 52232 | tf_op jit(solution)/shard_map/ppermute | solution.py:19
  85.8 4.0 %collective-permute-start.5 = (s32[16,272]{1,0:T(8,128)S(1)}, s32[16,272]{1,0:T(8,128)S(1)}, u32[]{:S(2)}, u32[]{:S(2)}) collective-permute-start(s32[16,272]{1,0:T(8,128)S(1)} %get-tuple-element.41), channel_id=1, source_target_pairs={{0,256},{128,384},{256,0},{384,128},{1,257},{129,385},{257,1},{385... | collective-permute-start | bytes 52232 | tf_op jit(solution)/shard_map/ppermute | solution.py:19
  89.9 1.9 %collective-permute-start.6 = (s32[16,272]{1,0:T(8,128)S(1)}, s32[16,272]{1,0:T(8,128)S(1)}, u32[]{:S(2)}, u32[]{:S(2)}) collective-permute-start(s32[16,272]{1,0:T(8,128)S(1)} %get-tuple-element.40), channel_id=1, source_target_pairs={{0,384},{128,0},{256,128},{384,256},{1,385},{129,1},{257,129},{385... | collective-permute-start | bytes 52232 | tf_op jit(solution)/shard_map/ppermute | solution.py:19
  92.2 3.5 %collective-permute-done.6 = s32[16,272]{1,0:T(8,128)S(1)} collective-permute-done((s32[16,272]{1,0:T(8,128)S(1)}, s32[16,272]{1,0:T(8,128)S(1)}, u32[]{:S(2)}, u32[]{:S(2)}) %collective-permute-start.6) | collective-permute-done | bytes 17440 | tf_op jit(solution)/shard_map/ppermute | solution.py:19
  96.7 5.2 %pick_matrices.1 = (bf16[4,272,1024]{2,1,0:T(8,128)(2,1)}, bf16[4,272,1024]{2,1,0:T(8,128)(2,1)}) custom-call(s32[4,272,16]{2,1,0:T(8,128)} %bitcast.56), custom_call_target="tpu_custom_call" | custom-call | tf_op jit(solution)/shard_map/pick_matrices/pallas_call | solution.py:39
  101.9 2.8 %slice.159 = bf16[3,272,1024]{2,1,0:T(8,128)(2,1)} slice(bf16[4,272,1024]{2,1,0:T(8,128)(2,1)} %get-tuple-element.13), slice={[1:4], [0:272], [0:1024]} | slice | bytes 3342336 | tf_op jit(solution)/shard_map/slice | solution.py:135
  104.8 13.8 %collective-permute-start.8 = (bf16[1024,640]{1,0:T(8,128)(2,1)S(1)}, bf16[1024,640]{1,0:T(8,128)(2,1)S(1)}, u32[]{:S(2)}, u32[]{:S(2)}) collective-permute-start(bf16[1024,640]{1,0:T(8,128)(2,1)S(1)} %bitcast.53), channel_id=1, source_target_pairs={{0,8},{8,0},{1,9},{9,1},{2,10},{10,2},{3,11},{11,3},{4,12},{12,4},... | collective-permute-start | bytes 3932168 | tf_op jit(solution)/shard_map/ppermute | solution.py:19
  118.9 2.9 %fusion.69 = f32[816,640]{1,0:T(8,128)S(1)} fusion(bf16[816,1024]{1,0:T(8,128)(2,1)} %bitcast.57, bf16[1024,640]{1,0:T(8,128)(2,1)S(1)} %bitcast.54), kind=kOutput, calls=%fused_computation.139 | convolution fusion | flops 1069547520 | bytes 5070848 | tf_op jit(solution)/shard_map/dot_general | solution.py:136
  121.9 2.3 %broadcast_select_fusion = (bf16[640,1280]{1,0:T(8,128)(2,1)S(1)}, bf16[640,1280]{1,0:T(8,128)(2,1)S(1)}) fusion(bf16[640,1280]{1,0:T(8,128)(2,1)} %collective-permute-done.13, bf16[640,1280]{1,0:T(8,128)(2,1)} %collective-permute-done.12, pred[]{:T(512)S(6)} %eq.62), kind=kLoop, calls=%fused_computation.2 | loop fusion | flops 1638400 | bytes 6553601 | tf_op jit(solution)/shard_map/jit(_where)/select_n | solution.py:146
  125.0 1.9 %collective-permute-start.9 = (bf16[272,640]{1,0:T(8,128)(2,1)S(1)}, bf16[272,640]{1,0:T(8,128)(2,1)S(1)}, u32[]{:S(2)}, u32[]{:S(2)}) collective-permute-start(bf16[272,640]{1,0:T(8,128)(2,1)S(1)} %fusion.7), channel_id=1, source_target_pairs={{0,256},{128,384},{256,0},{384,128},{1,257},{129,385},{257,1},{385... | collective-permute-start | bytes 1044488 | tf_op jit(solution)/shard_map/ppermute | solution.py:19
  127.6 2.8 %collective-permute-start.10 = (bf16[272,640]{1,0:T(8,128)(2,1)S(1)}, bf16[272,640]{1,0:T(8,128)(2,1)S(1)}, u32[]{:S(2)}, u32[]{:S(2)}) collective-permute-start(bf16[272,640]{1,0:T(8,128)(2,1)S(1)} %fusion.6), channel_id=1, source_target_pairs={{0,384},{128,0},{256,128},{384,256},{1,385},{129,1},{257,129},{385... | collective-permute-start | bytes 1044488 | tf_op jit(solution)/shard_map/ppermute | solution.py:19
  131.0 3.7 %collective-permute-start.11 = (bf16[272,640]{1,0:T(8,128)(2,1)S(1)}, bf16[272,640]{1,0:T(8,128)(2,1)S(1)}, u32[]{:S(2)}, u32[]{:S(2)}) collective-permute-start(bf16[272,640]{1,0:T(8,128)(2,1)S(1)} %fusion.5), channel_id=1, source_target_pairs={{0,128},{128,256},{256,384},{384,0},{1,129},{129,257},{257,385},{3... | collective-permute-start | bytes 1044488 | tf_op jit(solution)/shard_map/ppermute | solution.py:19
  138.2 7.9 %collective-permute-done.10 = bf16[272,640]{1,0:T(8,128)(2,1)S(1)} collective-permute-done((bf16[272,640]{1,0:T(8,128)(2,1)S(1)}, bf16[272,640]{1,0:T(8,128)(2,1)S(1)}, u32[]{:S(2)}, u32[]{:S(2)}) %collective-permute-start.10) | collective-permute-done | bytes 348192 | tf_op jit(solution)/shard_map/ppermute | solution.py:19
  (49 shorter events, 14.6 us)
Async XLA Ops:
  0.0 6.8 %copy-start.2 = (bf16[1,128,640]{2,1,0:T(8,128)(2,1)S(1)}, bf16[1,128,640]{2,1,0:T(8,128)(2,1)}, u32[]{:S(2)}) copy-start(bf16[1,128,640]{2,1,0:T(8,128)(2,1)} %param.10) | copy-start | bytes 491524
  2.8 72.3 %collective-permute-start.12 = (bf16[640,1280]{1,0:T(8,128)(2,1)}, bf16[640,1280]{1,0:T(8,128)(2,1)}, u32[]{:S(2)}, u32[]{:S(2)}) collective-permute-start(bf16[640,1280]{1,0:T(8,128)(2,1)} %select_bitcast_fusion), channel_id=1, source_target_pairs={{0,1},{1,2},{2,3},{3,4},{4,5},{5,6},{6,7},{7,0},{8,9},{9,10},{10,1... | collective-permute-start | bytes 4915208 | tf_op jit(solution)/shard_map/ppermute | solution.py:19
  6.8 45.9 %collective-permute-start.7 = (bf16[128,640]{1,0:T(8,128)(2,1)S(1)}, bf16[128,640]{1,0:T(8,128)(2,1)S(1)}, u32[]{:S(2)}, u32[]{:S(2)}) collective-permute-start(bf16[128,640]{1,0:T(8,128)(2,1)S(1)} %bitcast.65), channel_id=1, source_target_pairs={{0,1},{1,2},{2,3},{3,4},{4,5},{5,6},{6,7},{7,0},{8,9},{9,10},{10,1... | collective-permute-start | bytes 491528 | tf_op jit(solution)/shard_map/ppermute | solution.py:19
  53.9 6.7 %copy-start.1 = (bf16[1,256,1280]{2,1,0:T(8,128)(2,1)S(1)}, bf16[1,256,1280]{2,1,0:T(8,128)(2,1)}, u32[]{:S(2)}) copy-start(bf16[1,256,1280]{2,1,0:T(8,128)(2,1)} %param.7) | copy-start | bytes 1966084
  53.9 15.9 %copy-start.3 = (f32[1,4,1280]{2,1,0:T(4,128)S(1)}, f32[1,4,1280]{2,1,0:T(4,128)}, u32[]{:S(2)}) copy-start(f32[1,4,1280]{2,1,0:T(4,128)} %param.13) | copy-start | bytes 61444
  53.9 51.0 %all-to-all-start = ((bf16[8,128,640]{2,1,0:T(8,128)(2,1)}), bf16[8,128,640]{2,1,0:T(8,128)(2,1)S(1)}, u32[]{:S(2)}, u32[]{:S(2)}) async-start(bf16[8,128,640]{2,1,0:T(8,128)(2,1)} %broadcast_in_dim.115), calls=%async_computation | async-start | bytes 2621440 | tf_op jit(solution)/shard_map/all_to_all | solution.py:113
  60.5 44.2 %collective-permute-start.1 = (bf16[256,1280]{1,0:T(8,128)(2,1)S(1)}, bf16[256,1280]{1,0:T(8,128)(2,1)S(1)}, u32[]{:S(2)}, u32[]{:S(2)}) collective-permute-start(bf16[256,1280]{1,0:T(8,128)(2,1)S(1)} %bitcast.59), channel_id=1, source_target_pairs={{0,1},{1,2},{2,3},{3,4},{4,5},{5,6},{6,7},{7,0},{8,9},{9,10},{10,1... | collective-permute-start | bytes 1966088 | tf_op jit(solution)/shard_map/ppermute | solution.py:19
  63.9 19.3 %collective-permute-start = (bf16[32,1280]{1,0:T(8,128)(2,1)}, bf16[32,1280]{1,0:T(8,128)(2,1)S(1)}, u32[]{:S(2)}, u32[]{:S(2)}) collective-permute-start(bf16[32,1280]{1,0:T(8,128)(2,1)} %get-tuple-element.11), channel_id=1, source_target_pairs={{0,9},{1,10},{2,11},{3,12},{4,13},{5,14},{6,15},{7,8},{8,17},{9,18... | collective-permute-start | bytes 245768 | tf_op jit(solution)/shard_map/ppermute | solution.py:97
  65.8 17.5 %collective-permute-start.3 = (s32[16,256]{1,0:T(8,128)}, s32[16,256]{1,0:T(8,128)S(1)}, u32[]{:S(2)}, u32[]{:S(2)}) collective-permute-start(s32[16,256]{1,0:T(8,128)} %get-tuple-element.12), channel_id=1, source_target_pairs={{0,1},{1,2},{2,3},{3,4},{4,5},{5,6},{6,7},{7,0},{8,9},{9,10},{10,1... | collective-permute-start | bytes 49160 | tf_op jit(solution)/shard_map/ppermute | solution.py:19
  69.8 20.1 %collective-permute-start.2 = (f32[4,1280]{1,0:T(4,128)S(1)}, f32[4,1280]{1,0:T(4,128)S(1)}, u32[]{:S(2)}, u32[]{:S(2)}) collective-permute-start(f32[4,1280]{1,0:T(4,128)S(1)} %bitcast.66), channel_id=1, source_target_pairs={{0,1},{1,2},{2,3},{3,4},{4,5},{5,6},{6,7},{7,0},{8,9},{9,10},{10,1... | collective-permute-start | bytes 61448 | tf_op jit(solution)/shard_map/ppermute | solution.py:19
  75.1 46.7 %collective-permute-start.13 = (bf16[640,1280]{1,0:T(8,128)(2,1)}, bf16[640,1280]{1,0:T(8,128)(2,1)}, u32[]{:S(2)}, u32[]{:S(2)}) collective-permute-start(bf16[640,1280]{1,0:T(8,128)(2,1)} %collective-permute-done.12), channel_id=1, source_target_pairs={{0,8},{8,0},{1,9},{9,1},{2,10},{10,2},{3,11},{11,3},{4,12},{12,4},... | collective-permute-start | bytes 4915208 | tf_op jit(solution)/shard_map/ppermute | solution.py:19
  83.7 8.2 %collective-permute-start.4 = (s32[16,272]{1,0:T(8,128)S(1)}, s32[16,272]{1,0:T(8,128)S(1)}, u32[]{:S(2)}, u32[]{:S(2)}) collective-permute-start(s32[16,272]{1,0:T(8,128)S(1)} %get-tuple-element.42), channel_id=1, source_target_pairs={{0,128},{128,256},{256,384},{384,0},{1,129},{129,257},{257,385},{3... | collective-permute-start | bytes 52232 | tf_op jit(solution)/shard_map/ppermute | solution.py:19
  85.8 6.4 %collective-permute-start.5 = (s32[16,272]{1,0:T(8,128)S(1)}, s32[16,272]{1,0:T(8,128)S(1)}, u32[]{:S(2)}, u32[]{:S(2)}) collective-permute-start(s32[16,272]{1,0:T(8,128)S(1)} %get-tuple-element.41), channel_id=1, source_target_pairs={{0,256},{128,384},{256,0},{384,128},{1,257},{129,385},{257,1},{385... | collective-permute-start | bytes 52232 | tf_op jit(solution)/shard_map/ppermute | solution.py:19
  89.9 5.8 %collective-permute-start.6 = (s32[16,272]{1,0:T(8,128)S(1)}, s32[16,272]{1,0:T(8,128)S(1)}, u32[]{:S(2)}, u32[]{:S(2)}) collective-permute-start(s32[16,272]{1,0:T(8,128)S(1)} %get-tuple-element.40), channel_id=1, source_target_pairs={{0,384},{128,0},{256,128},{384,256},{1,385},{129,1},{257,129},{385... | collective-permute-start | bytes 52232 | tf_op jit(solution)/shard_map/ppermute | solution.py:19
  104.8 19.3 %collective-permute-start.8 = (bf16[1024,640]{1,0:T(8,128)(2,1)S(1)}, bf16[1024,640]{1,0:T(8,128)(2,1)S(1)}, u32[]{:S(2)}, u32[]{:S(2)}) collective-permute-start(bf16[1024,640]{1,0:T(8,128)(2,1)S(1)} %bitcast.53), channel_id=1, source_target_pairs={{0,8},{8,0},{1,9},{9,1},{2,10},{10,2},{3,11},{11,3},{4,12},{12,4},... | collective-permute-start | bytes 3932168 | tf_op jit(solution)/shard_map/ppermute | solution.py:19
  121.8 2.6 %copy-start = (bf16[4,272,1024]{2,1,0:T(8,128)(2,1)S(1)}, bf16[4,272,1024]{2,1,0:T(8,128)(2,1)}, u32[]{:S(2)}) copy-start(bf16[4,272,1024]{2,1,0:T(8,128)(2,1)} %get-tuple-element.14) | copy-start | bytes 6684676
  125.0 13.1 %collective-permute-start.9 = (bf16[272,640]{1,0:T(8,128)(2,1)S(1)}, bf16[272,640]{1,0:T(8,128)(2,1)S(1)}, u32[]{:S(2)}, u32[]{:S(2)}) collective-permute-start(bf16[272,640]{1,0:T(8,128)(2,1)S(1)} %fusion.7), channel_id=1, source_target_pairs={{0,256},{128,384},{256,0},{384,128},{1,257},{129,385},{257,1},{385... | collective-permute-start | bytes 1044488 | tf_op jit(solution)/shard_map/ppermute | solution.py:19
  127.6 18.5 %collective-permute-start.10 = (bf16[272,640]{1,0:T(8,128)(2,1)S(1)}, bf16[272,640]{1,0:T(8,128)(2,1)S(1)}, u32[]{:S(2)}, u32[]{:S(2)}) collective-permute-start(bf16[272,640]{1,0:T(8,128)(2,1)S(1)} %fusion.6), channel_id=1, source_target_pairs={{0,384},{128,0},{256,128},{384,256},{1,385},{129,1},{257,129},{385... | collective-permute-start | bytes 1044488 | tf_op jit(solution)/shard_map/ppermute | solution.py:19
  131.0 15.1 %collective-permute-start.11 = (bf16[272,640]{1,0:T(8,128)(2,1)S(1)}, bf16[272,640]{1,0:T(8,128)(2,1)S(1)}, u32[]{:S(2)}, u32[]{:S(2)}) collective-permute-start(bf16[272,640]{1,0:T(8,128)(2,1)S(1)} %fusion.5), channel_id=1, source_target_pairs={{0,128},{128,256},{256,384},{384,0},{1,129},{129,257},{257,385},{3... | collective-permute-start | bytes 1044488 | tf_op jit(solution)/shard_map/ppermute | solution.py:19

commit v5 on v4

--- a/solution.py
+++ b/solution.py
@@ -25,22 +25,30 @@
 def pick_matrices(asked, rows_dev):
     groups, rows, _ = asked.shape
 
-    def body(asked_ref, own_ref, other_ref):
+    def body(asked_ref, sent_ref, mine_ref, other_ref):
         lane = lax.broadcasted_iota(jnp.int32, (rows, rows_dev), 1)
         for group in range(groups):
-            for swapped, out_ref in ((0, own_ref), (1, other_ref)):
-                for far in range(NY):
-                    column = swapped * NY + far
-                    hit = asked_ref[group, :, column : column + 1] == lane
-                    hit = hit.astype(jnp.float32).astype(jnp.bfloat16)
-                    out_ref[group, :, far * rows_dev : (far + 1) * rows_dev] = hit
+            for column in range(NC * NY):
+                hit = asked_ref[group, :, column : column + 1] == lane
+                hit = hit.astype(jnp.float32).astype(jnp.bfloat16)
+                at = column % NY * rows_dev
+                if column >= NY:
+                    other_ref[group, :, at : at + rows_dev] = hit
+                elif group == 0:
+                    mine_ref[:, at : at + rows_dev] = hit
+                else:
+                    sent_ref[(group - 1) * rows : group * rows, at : at + rows_dev] = hit
 
-    shape = jax.ShapeDtypeStruct((groups, rows, NY * rows_dev), jnp.bfloat16)
+    wide = NY * rows_dev
     return pl.pallas_call(
         body,
         in_specs=[VMEM],
-        out_specs=[VMEM, VMEM],
-        out_shape=[shape, shape],
+        out_specs=[VMEM] * 3,
+        out_shape=[
+            jax.ShapeDtypeStruct(((groups - 1) * rows, wide), jnp.bfloat16),
+            jax.ShapeDtypeStruct((rows, wide), jnp.bfloat16),
+            jax.ShapeDtypeStruct((groups, rows, wide), jnp.bfloat16),
+        ],
         name="pick_matrices",
     )(asked)
 
@@ -129,22 +137,20 @@
     for ahead in range(1, NX):
         received.append(rotated(asked[ahead], "x", ahead))
     asked = jnp.stack(received).transpose(0, 2, 1)
-    pick_own, pick_other = pick_matrices(asked, rows_dev)
+    pick_sent, pick_mine, pick_other = pick_matrices(asked, rows_dev)
 
     rows = tok_rows + HALO
-    pick_sent = pick_own[1:].reshape((NX - 1) * rows, -1)
     own_part = jnp.dot(pick_sent, own_rows, preferred_element_type=jnp.float32).reshape(NX - 1, rows, -1)
     sums = []
     for back in (2, 1, 3):
         part = own_part[back - 1] + jnp.dot(pick_other[back], other_rows, preferred_element_type=jnp.float32)
         sums.append(rotated(part.astype(bf16), "x", -back))
-    total = jnp.dot(pick_own[0], own_rows, preferred_element_type=jnp.float32) + jnp.dot(
+    total = jnp.dot(pick_mine, own_rows, preferred_element_type=jnp.float32) + jnp.dot(
         pick_other[0], other_rows, preferred_element_type=jnp.float32
     )
-    total = lax.optimization_barrier(total)
     key_here = jnp.where(core == 0, weight_one, weight_two)
     value_here = jnp.where(core == 0, weight_two, weight_one)
-    key_here, value_here = lax.optimization_barrier((key_here, value_here))
+    key_here, value_here, total, states = lax.optimization_barrier((key_here, value_here, total, states))
     for part in sums:
         total = total + part.astype(jnp.float32)
     packed = total.astype(bf16)

time: 151 us -> 124 us (0.82)
  the two profiles are of different devices: /device:TPU:47 before, /device:TPU:1 now
where the time goes in v5:
time: 124 us; the launch traced here: 121 us
  starting transfers between devices  55.2 us (45%)
  waiting for transfers between devices  41.9 us (34%)
  matrix products  7.56 us (6%)
  other arithmetic  7.27 us (6%)
  Pallas kernels  6.54 us (5%)
  local copies, waits for them, and re-layouts  2.56 us (2%)
    ppermute x13, starting transfers between devices, rotated(): lax.ppermute(value, axis, [(i, (i + by) % count) for i in range(count)])  42.8 us
    ppermute x13, waiting for transfers between devices, rotated(): lax.ppermute(value, axis, [(i, (i + by) % count) for i in range(count)])  40.2 us
    all_to_all x1, starting transfers between devices, local(): lax.all_to_all(copies, 'y', split_axis=0, concat_axis=0, tiled=True)  6.95 us
    ppermute x1, starting transfers between devices, local(): lax.ppermute(tail, TABLE + ('segment',), [(i * sections + s, (i + 1) * se...  5.45 us
    pallas_call x1, Pallas kernels, pick_matrices(): pl.pallas_call(body, in_specs=[VMEM], out_specs=[VMEM] * 3, out_shape=[ja...  5.1 us
    dot_general x1, matrix products, local(): jnp.dot(pick_sent, own_rows, preferred_element_type=jnp.float32)  2.89 us
  transfers between devices with their start and end apart: 15, of which 6 were waited for; matrix products, arithmetic and copies ran while one was open for 11% of the time, Pallas kernels for 5%

profile of v5, /device:TPU:1, one launch (start us, length us, event | category | flops | bytes accessed | tf_op | source)
XLA Modules:
  0.0 121.4 jit_solution(14045284662840280898)
XLA Ops:
  0.0 4.8 %collective-permute-start.7 = (bf16[128,640]{1,0:T(8,128)(2,1)}, bf16[128,640]{1,0:T(8,128)(2,1)S(1)}, u32[]{:S(2)}, u32[]{:S(2)}) collective-permute-start(bf16[128,640]{1,0:T(8,128)(2,1)} %bitcast.61), channel_id=1, source_target_pairs={{0,1},{1,2},{2,3},{3,4},{4,5},{5,6},{6,7},{7,0},{8,9},{9,10},{10,1... | collective-permute-start | bytes 491528 | tf_op jit(solution)/shard_map/ppermute | solution.py:19
  4.8 1.6 %select_bitcast_fusion = bf16[640,1280]{1,0:T(8,128)(2,1)S(1)} fusion(bf16[1,640,1280]{2,1,0:T(8,128)(2,1)} %param.11, bf16[1,640,1280]{2,1,0:T(8,128)(2,1)} %param.12, pred[]{:T(512)S(6)} %eq.60), kind=kLoop, calls=%fused_computation.1 | loop fusion | flops 819200 | bytes 4915201 | tf_op jit(solution)/shard_map/jit(_where)/select_n | solution.py:115
  6.4 4.0 %collective-permute-start.1 = (bf16[640,1280]{1,0:T(8,128)(2,1)S(1)}, bf16[640,1280]{1,0:T(8,128)(2,1)}, u32[]{:S(2)}, u32[]{:S(2)}) collective-permute-start(bf16[640,1280]{1,0:T(8,128)(2,1)S(1)} %select_bitcast_fusion), channel_id=1, source_target_pairs={{0,1},{1,2},{2,3},{3,4},{4,5},{5,6},{6,7},{7,0},{8,9},{9,10},{10,1... | collective-permute-start | bytes 4915208 | tf_op jit(solution)/shard_map/ppermute | solution.py:19
  10.4 5.1 %collective-permute-done.7 = bf16[128,640]{1,0:T(8,128)(2,1)S(1)} collective-permute-done((bf16[128,640]{1,0:T(8,128)(2,1)}, bf16[128,640]{1,0:T(8,128)(2,1)S(1)}, u32[]{:S(2)}, u32[]{:S(2)}) %collective-permute-start.7) | collective-permute-done | bytes 163872 | tf_op jit(solution)/shard_map/ppermute | solution.py:19
  16.8 7.0 %all-to-all-start = ((bf16[8,128,640]{2,1,0:T(8,128)(2,1)}), bf16[8,128,640]{2,1,0:T(8,128)(2,1)S(1)}, u32[]{:S(2)}, u32[]{:S(2)}) async-start(bf16[8,128,640]{2,1,0:T(8,128)(2,1)} %broadcast_in_dim.113), calls=%async_computation | async-start | bytes 2621440 | tf_op jit(solution)/shard_map/all_to_all | solution.py:121
  23.7 27.3 %collective-permute-done.1 = bf16[640,1280]{1,0:T(8,128)(2,1)} collective-permute-done((bf16[640,1280]{1,0:T(8,128)(2,1)S(1)}, bf16[640,1280]{1,0:T(8,128)(2,1)}, u32[]{:S(2)}, u32[]{:S(2)}) %collective-permute-start.1) | collective-permute-done | bytes 1638432 | tf_op jit(solution)/shard_map/ppermute | solution.py:19
  51.0 3.0 %collective-permute-start.2 = (bf16[640,1280]{1,0:T(8,128)(2,1)}, bf16[640,1280]{1,0:T(8,128)(2,1)}, u32[]{:S(2)}, u32[]{:S(2)}) collective-permute-start(bf16[640,1280]{1,0:T(8,128)(2,1)} %collective-permute-done.1), channel_id=1, source_target_pairs={{0,8},{8,0},{1,9},{9,1},{2,10},{10,2},{3,11},{11,3},{4,12},{12,4},... | collective-permute-start | bytes 4915208 | tf_op jit(solution)/shard_map/ppermute | solution.py:19
  54.0 1.9 %collective-permute-start.10 = (f32[4,1280]{1,0:T(4,128)S(1)}, f32[4,1280]{1,0:T(4,128)S(1)}, u32[]{:S(2)}, u32[]{:S(2)}) collective-permute-start(f32[4,1280]{1,0:T(4,128)S(1)} %bitcast.62), channel_id=1, source_target_pairs={{0,1},{1,2},{2,3},{3,4},{4,5},{5,6},{6,7},{7,0},{8,9},{9,10},{10,1... | collective-permute-start | bytes 61448 | tf_op jit(solution)/shard_map/ppermute | solution.py:19
  57.3 1.9 %collective-permute-start.3 = (s32[16,256]{1,0:T(8,128)}, s32[16,256]{1,0:T(8,128)S(1)}, u32[]{:S(2)}, u32[]{:S(2)}) collective-permute-start(s32[16,256]{1,0:T(8,128)} %get-tuple-element.15), channel_id=1, source_target_pairs={{0,1},{1,2},{2,3},{3,4},{4,5},{5,6},{6,7},{7,0},{8,9},{9,10},{10,1... | collective-permute-start | bytes 49160 | tf_op jit(solution)/shard_map/ppermute | solution.py:19
  59.3 5.4 %collective-permute-start = (bf16[32,1280]{1,0:T(8,128)(2,1)}, bf16[32,1280]{1,0:T(8,128)(2,1)S(1)}, u32[]{:S(2)}, u32[]{:S(2)}) collective-permute-start(bf16[32,1280]{1,0:T(8,128)(2,1)} %get-tuple-element.14), channel_id=1, source_target_pairs={{0,9},{1,10},{2,11},{3,12},{4,13},{5,14},{6,15},{7,8},{8,17},{9,18... | collective-permute-start | bytes 245768 | tf_op jit(solution)/shard_map/ppermute | solution.py:105
  64.8 1.7 %collective-permute-done = bf16[32,1280]{1,0:T(8,128)(2,1)S(1)} collective-permute-done((bf16[32,1280]{1,0:T(8,128)(2,1)}, bf16[32,1280]{1,0:T(8,128)(2,1)S(1)}, u32[]{:S(2)}, u32[]{:S(2)}) %collective-permute-start) | collective-permute-done | bytes 81952 | tf_op jit(solution)/shard_map/ppermute | solution.py:105
  67.0 1.9 %collective-permute-start.8 = (bf16[1024,640]{1,0:T(8,128)(2,1)S(1)}, bf16[1024,640]{1,0:T(8,128)(2,1)S(1)}, u32[]{:S(2)}, u32[]{:S(2)}) collective-permute-start(bf16[1024,640]{1,0:T(8,128)(2,1)S(1)} %bitcast.50), channel_id=1, source_target_pairs={{0,8},{8,0},{1,9},{9,1},{2,10},{10,2},{3,11},{11,3},{4,12},{12,4},... | collective-permute-start | bytes 3932168 | tf_op jit(solution)/shard_map/ppermute | solution.py:19
  68.9 7.7 %collective-permute-start.6 = (s32[16,272]{1,0:T(8,128)S(1)}, s32[16,272]{1,0:T(8,128)S(1)}, u32[]{:S(2)}, u32[]{:S(2)}) collective-permute-start(s32[16,272]{1,0:T(8,128)S(1)} %get-tuple-element.46), channel_id=1, source_target_pairs={{0,384},{128,0},{256,128},{384,256},{1,385},{129,1},{257,129},{385... | collective-permute-start | bytes 52232 | tf_op jit(solution)/shard_map/ppermute | solution.py:19
  76.6 2.4 %collective-permute-start.5 = (s32[16,272]{1,0:T(8,128)S(1)}, s32[16,272]{1,0:T(8,128)S(1)}, u32[]{:S(2)}, u32[]{:S(2)}) collective-permute-start(s32[16,272]{1,0:T(8,128)S(1)} %get-tuple-element.47), channel_id=1, source_target_pairs={{0,256},{128,384},{256,0},{384,128},{1,257},{129,385},{257,1},{385... | collective-permute-start | bytes 52232 | tf_op jit(solution)/shard_map/ppermute | solution.py:19
  79.1 2.5 %collective-permute-start.4 = (s32[16,272]{1,0:T(8,128)S(1)}, s32[16,272]{1,0:T(8,128)S(1)}, u32[]{:S(2)}, u32[]{:S(2)}) collective-permute-start(s32[16,272]{1,0:T(8,128)S(1)} %get-tuple-element.48), channel_id=1, source_target_pairs={{0,128},{128,256},{256,384},{384,0},{1,129},{129,257},{257,385},{3... | collective-permute-start | bytes 52232 | tf_op jit(solution)/shard_map/ppermute | solution.py:19
  81.7 3.0 %collective-permute-start.9 = (bf16[256,1280]{1,0:T(8,128)(2,1)}, bf16[256,1280]{1,0:T(8,128)(2,1)S(1)}, u32[]{:S(2)}, u32[]{:S(2)}) collective-permute-start(bf16[256,1280]{1,0:T(8,128)(2,1)} %bitcast.55), channel_id=1, source_target_pairs={{0,1},{1,2},{2,3},{3,4},{4,5},{5,6},{6,7},{7,0},{8,9},{9,10},{10,1... | collective-permute-start | bytes 1966088 | tf_op jit(solution)/shard_map/ppermute | solution.py:19
  85.9 5.1 %pick_matrices.1 = (bf16[816,1024]{1,0:T(8,128)(2,1)}, bf16[272,1024]{1,0:T(8,128)(2,1)}, bf16[4,272,1024]{2,1,0:T(8,128)(2,1)}) custom-call(s32[4,272,16]{2,1,0:T(8,128)} %bitcast.53), custom_call_target="tpu_custom_call" | custom-call | tf_op jit(solution)/shard_map/pick_matrices/pallas_call | solution.py:43
  91.0 2.9 %fusion.67 = f32[816,640]{1,0:T(8,128)S(1)} fusion(bf16[816,1024]{1,0:T(8,128)(2,1)} %get-tuple-element.20, bf16[1024,640]{1,0:T(8,128)(2,1)S(1)} %bitcast.51), kind=kOutput, calls=%fused_computation.137 | convolution fusion | flops 1069547520 | bytes 5070848 | tf_op jit(solution)/shard_map/dot_general | solution.py:143
  93.9 2.3 %broadcast_select_fusion = (bf16[640,1280]{1,0:T(8,128)(2,1)S(1)}, bf16[640,1280]{1,0:T(8,128)(2,1)S(1)}) fusion(bf16[640,1280]{1,0:T(8,128)(2,1)} %collective-permute-done.2, bf16[640,1280]{1,0:T(8,128)(2,1)} %collective-permute-done.1, pred[]{:T(512)S(6)} %eq.60), kind=kLoop, calls=%fused_computation.2 | loop fusion | flops 1638400 | bytes 6553601 | tf_op jit(solution)/shard_map/jit(_where)/select_n | solution.py:152
  97.1 3.6 %collective-permute-start.11 = (bf16[272,640]{1,0:T(8,128)(2,1)S(1)}, bf16[272,640]{1,0:T(8,128)(2,1)S(1)}, u32[]{:S(2)}, u32[]{:S(2)}) collective-permute-start(bf16[272,640]{1,0:T(8,128)(2,1)S(1)} %fusion.7), channel_id=1, source_target_pairs={{0,256},{128,384},{256,0},{384,128},{1,257},{129,385},{257,1},{385... | collective-permute-start | bytes 1044488 | tf_op jit(solution)/shard_map/ppermute | solution.py:19
  101.3 4.0 %collective-permute-start.12 = (bf16[272,640]{1,0:T(8,128)(2,1)S(1)}, bf16[272,640]{1,0:T(8,128)(2,1)S(1)}, u32[]{:S(2)}, u32[]{:S(2)}) collective-permute-start(bf16[272,640]{1,0:T(8,128)(2,1)S(1)} %fusion.6), channel_id=1, source_target_pairs={{0,384},{128,0},{256,128},{384,256},{1,385},{129,1},{257,129},{385... | collective-permute-start | bytes 1044488 | tf_op jit(solution)/shard_map/ppermute | solution.py:19
  105.9 2.1 %collective-permute-start.13 = (bf16[272,640]{1,0:T(8,128)(2,1)S(1)}, bf16[272,640]{1,0:T(8,128)(2,1)S(1)}, u32[]{:S(2)}, u32[]{:S(2)}) collective-permute-start(bf16[272,640]{1,0:T(8,128)(2,1)S(1)} %fusion.5), channel_id=1, source_target_pairs={{0,128},{128,256},{256,384},{384,0},{1,129},{129,257},{257,385},{3... | collective-permute-start | bytes 1044488 | tf_op jit(solution)/shard_map/ppermute | solution.py:19
  109.5 7.0 %collective-permute-done.12 = bf16[272,640]{1,0:T(8,128)(2,1)S(1)} collective-permute-done((bf16[272,640]{1,0:T(8,128)(2,1)S(1)}, bf16[272,640]{1,0:T(8,128)(2,1)S(1)}, u32[]{:S(2)}, u32[]{:S(2)}) %collective-permute-start.12) | collective-permute-done | bytes 348192 | tf_op jit(solution)/shard_map/ppermute | solution.py:19
  119.7 1.7 %fusion.8 = bf16[1,256,1280]{2,1,0:T(8,128)(2,1)} fusion(f32[272,1280]{1,0:T(8,128)S(1)} %get-tuple-element.52, f32[272,1280]{1,0:T(8,128)S(1)} %multiply_select_fusion, f32[1280]{0:T(1024)S(1)} %get-tuple-element.40, f32[1280]{0:T(1024)S(1)} %get-tuple-element.41, f32[1280]{0:T(1024)S(1)} %get-tuple-element.42, f32[1280]{0:T(1024)S(1)} %get-tuple-element.39, ...), kind=kLoop, calls=%fused_computation.28 | loop fusion | flops 4587520 | bytes 8540160 | tf_op jit(solution)/shard_map/broadcast_in_dim | solution.py:171
  (45 shorter events, 11.1 us)
Async XLA Ops:
  0.0 15.6 %collective-permute-start.7 = (bf16[128,640]{1,0:T(8,128)(2,1)}, bf16[128,640]{1,0:T(8,128)(2,1)S(1)}, u32[]{:S(2)}, u32[]{:S(2)}) collective-permute-start(bf16[128,640]{1,0:T(8,128)(2,1)} %bitcast.61), channel_id=1, source_target_pairs={{0,1},{1,2},{2,3},{3,4},{4,5},{5,6},{6,7},{7,0},{8,9},{9,10},{10,1... | collective-permute-start | bytes 491528 | tf_op jit(solution)/shard_map/ppermute | solution.py:19
  6.4 44.5 %collective-permute-start.1 = (bf16[640,1280]{1,0:T(8,128)(2,1)S(1)}, bf16[640,1280]{1,0:T(8,128)(2,1)}, u32[]{:S(2)}, u32[]{:S(2)}) collective-permute-start(bf16[640,1280]{1,0:T(8,128)(2,1)S(1)} %select_bitcast_fusion), channel_id=1, source_target_pairs={{0,1},{1,2},{2,3},{3,4},{4,5},{5,6},{6,7},{7,0},{8,9},{9,10},{10,1... | collective-permute-start | bytes 4915208 | tf_op jit(solution)/shard_map/ppermute | solution.py:19
  16.7 37.2 %copy-start.2 = (f32[1,4,1280]{2,1,0:T(4,128)S(1)}, f32[1,4,1280]{2,1,0:T(4,128)}, u32[]{:S(2)}) copy-start(f32[1,4,1280]{2,1,0:T(4,128)} %param.13) | copy-start | bytes 61444
  16.8 50.2 %all-to-all-start = ((bf16[8,128,640]{2,1,0:T(8,128)(2,1)}), bf16[8,128,640]{2,1,0:T(8,128)(2,1)S(1)}, u32[]{:S(2)}, u32[]{:S(2)}) async-start(bf16[8,128,640]{2,1,0:T(8,128)(2,1)} %broadcast_in_dim.113), calls=%async_computation | async-start | bytes 2621440 | tf_op jit(solution)/shard_map/all_to_all | solution.py:121
  51.0 42.9 %collective-permute-start.2 = (bf16[640,1280]{1,0:T(8,128)(2,1)}, bf16[640,1280]{1,0:T(8,128)(2,1)}, u32[]{:S(2)}, u32[]{:S(2)}) collective-permute-start(bf16[640,1280]{1,0:T(8,128)(2,1)} %collective-permute-done.1), channel_id=1, source_target_pairs={{0,8},{8,0},{1,9},{9,1},{2,10},{10,2},{3,11},{11,3},{4,12},{12,4},... | collective-permute-start | bytes 4915208 | tf_op jit(solution)/shard_map/ppermute | solution.py:19
  54.0 25.1 %collective-permute-start.10 = (f32[4,1280]{1,0:T(4,128)S(1)}, f32[4,1280]{1,0:T(4,128)S(1)}, u32[]{:S(2)}, u32[]{:S(2)}) collective-permute-start(f32[4,1280]{1,0:T(4,128)S(1)} %bitcast.62), channel_id=1, source_target_pairs={{0,1},{1,2},{2,3},{3,4},{4,5},{5,6},{6,7},{7,0},{8,9},{9,10},{10,1... | collective-permute-start | bytes 61448 | tf_op jit(solution)/shard_map/ppermute | solution.py:19
  57.3 9.2 %collective-permute-start.3 = (s32[16,256]{1,0:T(8,128)}, s32[16,256]{1,0:T(8,128)S(1)}, u32[]{:S(2)}, u32[]{:S(2)}) collective-permute-start(s32[16,256]{1,0:T(8,128)} %get-tuple-element.15), channel_id=1, source_target_pairs={{0,1},{1,2},{2,3},{3,4},{4,5},{5,6},{6,7},{7,0},{8,9},{9,10},{10,1... | collective-permute-start | bytes 49160 | tf_op jit(solution)/shard_map/ppermute | solution.py:19
  59.3 7.2 %collective-permute-start = (bf16[32,1280]{1,0:T(8,128)(2,1)}, bf16[32,1280]{1,0:T(8,128)(2,1)S(1)}, u32[]{:S(2)}, u32[]{:S(2)}) collective-permute-start(bf16[32,1280]{1,0:T(8,128)(2,1)} %get-tuple-element.14), channel_id=1, source_target_pairs={{0,9},{1,10},{2,11},{3,12},{4,13},{5,14},{6,15},{7,8},{8,17},{9,18... | collective-permute-start | bytes 245768 | tf_op jit(solution)/shard_map/ppermute | solution.py:105
  67.0 29.2 %collective-permute-start.8 = (bf16[1024,640]{1,0:T(8,128)(2,1)S(1)}, bf16[1024,640]{1,0:T(8,128)(2,1)S(1)}, u32[]{:S(2)}, u32[]{:S(2)}) collective-permute-start(bf16[1024,640]{1,0:T(8,128)(2,1)S(1)} %bitcast.50), channel_id=1, source_target_pairs={{0,8},{8,0},{1,9},{9,1},{2,10},{10,2},{3,11},{11,3},{4,12},{12,4},... | collective-permute-start | bytes 3932168 | tf_op jit(solution)/shard_map/ppermute | solution.py:19
  68.9 12.7 %collective-permute-start.6 = (s32[16,272]{1,0:T(8,128)S(1)}, s32[16,272]{1,0:T(8,128)S(1)}, u32[]{:S(2)}, u32[]{:S(2)}) collective-permute-start(s32[16,272]{1,0:T(8,128)S(1)} %get-tuple-element.46), channel_id=1, source_target_pairs={{0,384},{128,0},{256,128},{384,256},{1,385},{129,1},{257,129},{385... | collective-permute-start | bytes 52232 | tf_op jit(solution)/shard_map/ppermute | solution.py:19
  76.6 8.1 %collective-permute-start.5 = (s32[16,272]{1,0:T(8,128)S(1)}, s32[16,272]{1,0:T(8,128)S(1)}, u32[]{:S(2)}, u32[]{:S(2)}) collective-permute-start(s32[16,272]{1,0:T(8,128)S(1)} %get-tuple-element.47), channel_id=1, source_target_pairs={{0,256},{128,384},{256,0},{384,128},{1,257},{129,385},{257,1},{385... | collective-permute-start | bytes 52232 | tf_op jit(solution)/shard_map/ppermute | solution.py:19
  79.1 5.8 %collective-permute-start.4 = (s32[16,272]{1,0:T(8,128)S(1)}, s32[16,272]{1,0:T(8,128)S(1)}, u32[]{:S(2)}, u32[]{:S(2)}) collective-permute-start(s32[16,272]{1,0:T(8,128)S(1)} %get-tuple-element.48), channel_id=1, source_target_pairs={{0,128},{128,256},{256,384},{384,0},{1,129},{129,257},{257,385},{3... | collective-permute-start | bytes 52232 | tf_op jit(solution)/shard_map/ppermute | solution.py:19
  81.7 27.5 %collective-permute-start.9 = (bf16[256,1280]{1,0:T(8,128)(2,1)}, bf16[256,1280]{1,0:T(8,128)(2,1)S(1)}, u32[]{:S(2)}, u32[]{:S(2)}) collective-permute-start(bf16[256,1280]{1,0:T(8,128)(2,1)} %bitcast.55), channel_id=1, source_target_pairs={{0,1},{1,2},{2,3},{3,4},{4,5},{5,6},{6,7},{7,0},{8,9},{9,10},{10,1... | collective-permute-start | bytes 1966088 | tf_op jit(solution)/shard_map/ppermute | solution.py:19
  93.9 2.6 %copy-start = (bf16[4,272,1024]{2,1,0:T(8,128)(2,1)S(1)}, bf16[4,272,1024]{2,1,0:T(8,128)(2,1)}, u32[]{:S(2)}) copy-start(bf16[4,272,1024]{2,1,0:T(8,128)(2,1)} %get-tuple-element.17) | copy-start | bytes 6684676
  97.1 12.5 %collective-permute-start.11 = (bf16[272,640]{1,0:T(8,128)(2,1)S(1)}, bf16[272,640]{1,0:T(8,128)(2,1)S(1)}, u32[]{:S(2)}, u32[]{:S(2)}) collective-permute-start(bf16[272,640]{1,0:T(8,128)(2,1)S(1)} %fusion.7), channel_id=1, source_target_pairs={{0,256},{128,384},{256,0},{384,128},{1,257},{129,385},{257,1},{385... | collective-permute-start | bytes 1044488 | tf_op jit(solution)/shard_map/ppermute | solution.py:19
  101.3 15.2 %collective-permute-start.12 = (bf16[272,640]{1,0:T(8,128)(2,1)S(1)}, bf16[272,640]{1,0:T(8,128)(2,1)S(1)}, u32[]{:S(2)}, u32[]{:S(2)}) collective-permute-start(bf16[272,640]{1,0:T(8,128)(2,1)S(1)} %fusion.6), channel_id=1, source_target_pairs={{0,384},{128,0},{256,128},{384,256},{1,385},{129,1},{257,129},{385... | collective-permute-start | bytes 1044488 | tf_op jit(solution)/shard_map/ppermute | solution.py:19
  105.9 2.7 %copy-start.1 = (bf16[272,1024]{1,0:T(8,128)(2,1)S(1)}, bf16[272,1024]{1,0:T(8,128)(2,1)}, u32[]{:S(2)}) copy-start(bf16[272,1024]{1,0:T(8,128)(2,1)} %get-tuple-element.16) | copy-start | bytes 1671172
  105.9 11.2 %collective-permute-start.13 = (bf16[272,640]{1,0:T(8,128)(2,1)S(1)}, bf16[272,640]{1,0:T(8,128)(2,1)S(1)}, u32[]{:S(2)}, u32[]{:S(2)}) collective-permute-start(bf16[272,640]{1,0:T(8,128)(2,1)S(1)} %fusion.5), channel_id=1, source_target_pairs={{0,128},{128,256},{256,384},{384,0},{1,129},{129,257},{257,385},{3... | collective-permute-start | bytes 1044488 | tf_op jit(solution)/shard_map/ppermute | solution.py:19

commit v6 on v5

--- a/solution.py
+++ b/solution.py
@@ -12,6 +12,7 @@
 NX, NY, NC = 4, 8, 2
 HALO = 16
 TABLE = ("x", "y", "core")
+GROUPS = ((0, 1, 2, 3), (0, 3, 2, 1))
 
 
 def rotated(value, axis, by):
@@ -51,6 +52,14 @@
         ],
         name="pick_matrices",
     )(asked)
+
+
+def along_x(value, steps):
+    pairs = []
+    for place in range(NX):
+        for core in range(NC):
+            pairs.append((place * NC + core, (place + steps[core]) % NX * NC + core))
+    return lax.ppermute(value, ("x", "core"), pairs)
 
 
 def rms_scale(values):
@@ -125,7 +134,8 @@
     head_numbers = tail[HALO:, 128 - HALO : 128].astype(jnp.int32)
     numbers = jnp.concatenate([head_numbers, numbers], axis=1)
     place = lax.broadcasted_iota(jnp.int32, (shards, 1), 0)
-    ahead, swapped, far = place // (NY * NC), place // NY % NC, place % NY
+    group, swapped, far = place // (NY * NC), place // NY % NC, place % NY
+    ahead = jnp.where(group % 2 == 1, (group + 2 * core) % NX, group)
     shard = (x + ahead) % NX * (NY * NC) + far * NC + (core ^ swapped)
     asked = jnp.full((shards, tok_rows + HALO), -1, jnp.int32)
     for h in range(head_count):
@@ -134,8 +144,8 @@
         )
     asked = asked.reshape(NX, NY * NC, tok_rows + HALO)
     received = [asked[0]]
-    for ahead in range(1, NX):
-        received.append(rotated(asked[ahead], "x", ahead))
+    for group in range(1, NX):
+        received.append(along_x(asked[group], (GROUPS[0][group], GROUPS[1][group])))
     asked = jnp.stack(received).transpose(0, 2, 1)
     pick_sent, pick_mine, pick_other = pick_matrices(asked, rows_dev)
 
@@ -144,16 +154,15 @@
     sums = []
     for back in (2, 1, 3):
         part = own_part[back - 1] + jnp.dot(pick_other[back], other_rows, preferred_element_type=jnp.float32)
-        sums.append(rotated(part.astype(bf16), "x", -back))
+        sums.append(along_x(part.astype(bf16), (-GROUPS[0][back], -GROUPS[1][back])))
     total = jnp.dot(pick_mine, own_rows, preferred_element_type=jnp.float32) + jnp.dot(
         pick_other[0], other_rows, preferred_element_type=jnp.float32
     )
     key_here = jnp.where(core == 0, weight_one, weight_two)
     value_here = jnp.where(core == 0, weight_two, weight_one)
     key_here, value_here, total, states = lax.optimization_barrier((key_here, value_here, total, states))
-    for part in sums:
-        total = total + part.astype(jnp.float32)
-    packed = total.astype(bf16)
+    total = lax.optimization_barrier(total + sums[0].astype(jnp.float32) + sums[1].astype(jnp.float32))
+    packed = (total + sums[2].astype(jnp.float32)).astype(bf16)
 
     states_float = jnp.concatenate([tail[:HALO], states], axis=0).astype(jnp.float32)
     keys_out = jnp.dot(packed, key_here, preferred_element_type=jnp.float32)

time: 124 us -> 122 us (0.984); the launches traced: 121 us -> 121 us
  starting transfers between devices: 55.2 us -> 52 us
  waiting for transfers between devices: 41.9 us -> 44.3 us
    ppermute x0 -> x6, starting transfers between devices: none -> 19.5 us  [along_x(): return lax.ppermute(value, ('x', 'core'), pairs)]
    ppermute x13 -> x7, starting transfers between devices: 42.8 us -> 23.6 us  [rotated(): lax.ppermute(value, axis, [(i, (i + by) % count) for i in range(count)])]
    ppermute x0 -> x6, waiting for transfers between devices: none -> 11.9 us  [along_x(): return lax.ppermute(value, ('x', 'core'), pairs)]
    ppermute x13 -> x7, waiting for transfers between devices: 40.2 us -> 32.4 us  [rotated(): lax.ppermute(value, axis, [(i, (i + by) % count) for i in range(count)])]
    ppermute x1, starting transfers between devices: 5.45 us -> 1.91 us  [local(): lax.ppermute(tail, TABLE + ('segment',), [(i * sections + s, (i + 1) * se...]
    ppermute x1, waiting for transfers between devices: 1.73 us -> 0.01 us  [local(): lax.ppermute(tail, TABLE + ('segment',), [(i * sections + s, (i + 1) * se...]
  transfers between devices with their start and end apart: 15 -> 15, of which waited for: 6 -> 5; matrix products, arithmetic and copies ran while one was open for 11% -> 11% of each run, Pallas kernels for 5% -> 5%
where the time goes in v6:
time: 122 us; the launch traced here: 121 us
  starting transfers between devices  52 us (43%)
  waiting for transfers between devices  44.3 us (36%)
  matrix products  7.62 us (6%)
  other arithmetic  7.24 us (6%)
  Pallas kernels  6.54 us (5%)
  local copies, waits for them, and re-layouts  2.56 us (2%)
    ppermute x7, waiting for transfers between devices, rotated(): lax.ppermute(value, axis, [(i, (i + by) % count) for i in range(count)])  32.4 us
    ppermute x7, starting transfers between devices, rotated(): lax.ppermute(value, axis, [(i, (i + by) % count) for i in range(count)])  23.6 us
    ppermute x6, starting transfers between devices, along_x(): return lax.ppermute(value, ('x', 'core'), pairs)  19.5 us
    ppermute x6, waiting for transfers between devices, along_x(): return lax.ppermute(value, ('x', 'core'), pairs)  11.9 us
    all_to_all x1, starting transfers between devices, local(): lax.all_to_all(copies, 'y', split_axis=0, concat_axis=0, tiled=True)  6.95 us
    pallas_call x1, Pallas kernels, pick_matrices(): pl.pallas_call(body, in_specs=[VMEM], out_specs=[VMEM] * 3, out_shape=[ja...  5.1 us
    dot_general x1, matrix products, local(): jnp.dot(pick_sent, own_rows, preferred_element_type=jnp.float32)  2.89 us
  transfers between devices with their start and end apart: 15, of which 5 were waited for; matrix products, arithmetic and copies ran while one was open for 11% of the time, Pallas kernels for 5%

profile of v6, /device:TPU:1, one launch (start us, length us, event | category | flops | bytes accessed | tf_op | source)
XLA Modules:
  0.0 120.6 jit_solution(2635391582151991378)
XLA Ops:
  0.0 4.8 %collective-permute-start.7 = (bf16[128,640]{1,0:T(8,128)(2,1)}, bf16[128,640]{1,0:T(8,128)(2,1)S(1)}, u32[]{:S(2)}, u32[]{:S(2)}) collective-permute-start(bf16[128,640]{1,0:T(8,128)(2,1)} %bitcast.59), channel_id=1, source_target_pairs={{0,1},{1,2},{2,3},{3,4},{4,5},{5,6},{6,7},{7,0},{8,9},{9,10},{10,1... | collective-permute-start | bytes 491528 | tf_op jit(solution)/shard_map/ppermute | solution.py:20
  4.8 1.6 %select_bitcast_fusion = bf16[640,1280]{1,0:T(8,128)(2,1)S(1)} fusion(bf16[1,640,1280]{2,1,0:T(8,128)(2,1)} %param.11, bf16[1,640,1280]{2,1,0:T(8,128)(2,1)} %param.12, pred[]{:T(512)S(6)} %eq.133), kind=kLoop, calls=%fused_computation.1 | loop fusion | flops 819200 | bytes 4915201 | tf_op jit(solution)/shard_map/jit(_where)/select_n | solution.py:124
  6.4 4.0 %collective-permute-start.1 = (bf16[640,1280]{1,0:T(8,128)(2,1)S(1)}, bf16[640,1280]{1,0:T(8,128)(2,1)}, u32[]{:S(2)}, u32[]{:S(2)}) collective-permute-start(bf16[640,1280]{1,0:T(8,128)(2,1)S(1)} %select_bitcast_fusion), channel_id=1, source_target_pairs={{0,1},{1,2},{2,3},{3,4},{4,5},{5,6},{6,7},{7,0},{8,9},{9,10},{10,1... | collective-permute-start | bytes 4915208 | tf_op jit(solution)/shard_map/ppermute | solution.py:20
  10.4 5.1 %collective-permute-done.7 = bf16[128,640]{1,0:T(8,128)(2,1)S(1)} collective-permute-done((bf16[128,640]{1,0:T(8,128)(2,1)}, bf16[128,640]{1,0:T(8,128)(2,1)S(1)}, u32[]{:S(2)}, u32[]{:S(2)}) %collective-permute-start.7) | collective-permute-done | bytes 163872 | tf_op jit(solution)/shard_map/ppermute | solution.py:20
  16.8 7.0 %all-to-all-start = ((bf16[8,128,640]{2,1,0:T(8,128)(2,1)}), bf16[8,128,640]{2,1,0:T(8,128)(2,1)S(1)}, u32[]{:S(2)}, u32[]{:S(2)}) async-start(bf16[8,128,640]{2,1,0:T(8,128)(2,1)} %broadcast_in_dim.113), calls=%async_computation | async-start | bytes 2621440 | tf_op jit(solution)/shard_map/all_to_all | solution.py:130
  23.7 27.3 %collective-permute-done.1 = bf16[640,1280]{1,0:T(8,128)(2,1)} collective-permute-done((bf16[640,1280]{1,0:T(8,128)(2,1)S(1)}, bf16[640,1280]{1,0:T(8,128)(2,1)}, u32[]{:S(2)}, u32[]{:S(2)}) %collective-permute-start.1) | collective-permute-done | bytes 1638432 | tf_op jit(solution)/shard_map/ppermute | solution.py:20
  51.0 3.0 %collective-permute-start.2 = (bf16[640,1280]{1,0:T(8,128)(2,1)}, bf16[640,1280]{1,0:T(8,128)(2,1)}, u32[]{:S(2)}, u32[]{:S(2)}) collective-permute-start(bf16[640,1280]{1,0:T(8,128)(2,1)} %collective-permute-done.1), channel_id=1, source_target_pairs={{0,8},{8,0},{1,9},{9,1},{2,10},{10,2},{3,11},{11,3},{4,12},{12,4},... | collective-permute-start | bytes 4915208 | tf_op jit(solution)/shard_map/ppermute | solution.py:20
  55.4 1.9 %collective-permute-start = (bf16[32,1280]{1,0:T(8,128)(2,1)}, bf16[32,1280]{1,0:T(8,128)(2,1)S(1)}, u32[]{:S(2)}, u32[]{:S(2)}) collective-permute-start(bf16[32,1280]{1,0:T(8,128)(2,1)} %get-tuple-element.14), channel_id=1, source_target_pairs={{0,9},{1,10},{2,11},{3,12},{4,13},{5,14},{6,15},{7,8},{8,17},{9,18... | collective-permute-start | bytes 245768 | tf_op jit(solution)/shard_map/ppermute | solution.py:114
  57.3 2.6 %collective-permute-start.3 = (s32[16,256]{1,0:T(8,128)}, s32[16,256]{1,0:T(8,128)S(1)}, u32[]{:S(2)}, u32[]{:S(2)}) collective-permute-start(s32[16,256]{1,0:T(8,128)} %get-tuple-element.15), channel_id=1, source_target_pairs={{0,1},{1,2},{2,3},{3,4},{4,5},{5,6},{6,7},{7,0},{8,9},{9,10},{10,1... | collective-permute-start | bytes 49160 | tf_op jit(solution)/shard_map/ppermute | solution.py:20
  59.9 4.2 %collective-permute-start.10 = (f32[4,1280]{1,0:T(4,128)S(1)}, f32[4,1280]{1,0:T(4,128)S(1)}, u32[]{:S(2)}, u32[]{:S(2)}) collective-permute-start(f32[4,1280]{1,0:T(4,128)S(1)} %bitcast.60), channel_id=1, source_target_pairs={{0,1},{1,2},{2,3},{3,4},{4,5},{5,6},{6,7},{7,0},{8,9},{9,10},{10,1... | collective-permute-start | bytes 61448 | tf_op jit(solution)/shard_map/ppermute | solution.py:20
  64.7 2.1 %collective-permute-start.8 = (bf16[1024,640]{1,0:T(8,128)(2,1)S(1)}, bf16[1024,640]{1,0:T(8,128)(2,1)S(1)}, u32[]{:S(2)}, u32[]{:S(2)}) collective-permute-start(bf16[1024,640]{1,0:T(8,128)(2,1)S(1)} %bitcast.48), channel_id=1, source_target_pairs={{0,8},{8,0},{1,9},{9,1},{2,10},{10,2},{3,11},{11,3},{4,12},{12,4},... | collective-permute-start | bytes 3932168 | tf_op jit(solution)/shard_map/ppermute | solution.py:20
  66.8 5.7 %collective-permute-start.4 = (s32[16,272]{1,0:T(8,128)S(1)}, s32[16,272]{1,0:T(8,128)S(1)}, u32[]{:S(2)}, u32[]{:S(2)}) collective-permute-start(s32[16,272]{1,0:T(8,128)S(1)} %get-tuple-element.48), channel_id=1, source_target_pairs={{0,128},{8,392},{128,256},{136,8},{256,384},{264,136},{384,0},{392... | collective-permute-start | bytes 52232 | tf_op jit(solution)/shard_map/ppermute | solution.py:62
  72.5 2.4 %collective-permute-start.5 = (s32[16,272]{1,0:T(8,128)S(1)}, s32[16,272]{1,0:T(8,128)S(1)}, u32[]{:S(2)}, u32[]{:S(2)}) collective-permute-start(s32[16,272]{1,0:T(8,128)S(1)} %get-tuple-element.47), channel_id=1, source_target_pairs={{0,256},{8,264},{128,384},{136,392},{256,0},{264,8},{384,128},{392... | collective-permute-start | bytes 52232 | tf_op jit(solution)/shard_map/ppermute | solution.py:62
  74.9 2.5 %collective-permute-start.6 = (s32[16,272]{1,0:T(8,128)S(1)}, s32[16,272]{1,0:T(8,128)S(1)}, u32[]{:S(2)}, u32[]{:S(2)}) collective-permute-start(s32[16,272]{1,0:T(8,128)S(1)} %get-tuple-element.46), channel_id=1, source_target_pairs={{0,384},{8,136},{128,0},{136,264},{256,128},{264,392},{384,256},{3... | collective-permute-start | bytes 52232 | tf_op jit(solution)/shard_map/ppermute | solution.py:62
  77.6 2.9 %collective-permute-start.9 = (bf16[256,1280]{1,0:T(8,128)(2,1)}, bf16[256,1280]{1,0:T(8,128)(2,1)S(1)}, u32[]{:S(2)}, u32[]{:S(2)}) collective-permute-start(bf16[256,1280]{1,0:T(8,128)(2,1)} %bitcast.53), channel_id=1, source_target_pairs={{0,1},{1,2},{2,3},{3,4},{4,5},{5,6},{6,7},{7,0},{8,9},{9,10},{10,1... | collective-permute-start | bytes 1966088 | tf_op jit(solution)/shard_map/ppermute | solution.py:20
  81.8 5.1 %pick_matrices.1 = (bf16[816,1024]{1,0:T(8,128)(2,1)}, bf16[272,1024]{1,0:T(8,128)(2,1)}, bf16[4,272,1024]{2,1,0:T(8,128)(2,1)}) custom-call(s32[4,272,16]{2,1,0:T(8,128)} %bitcast.51), custom_call_target="tpu_custom_call" | custom-call | tf_op jit(solution)/shard_map/pick_matrices/pallas_call | solution.py:44
  86.9 2.9 %fusion.69 = f32[816,640]{1,0:T(8,128)S(1)} fusion(bf16[816,1024]{1,0:T(8,128)(2,1)} %get-tuple-element.20, bf16[1024,640]{1,0:T(8,128)(2,1)S(1)} %bitcast.49), kind=kOutput, calls=%fused_computation.147 | convolution fusion | flops 1069547520 | bytes 5070848 | tf_op jit(solution)/shard_map/dot_general | solution.py:153
  89.8 2.3 %broadcast_select_fusion = (bf16[640,1280]{1,0:T(8,128)(2,1)S(1)}, bf16[640,1280]{1,0:T(8,128)(2,1)S(1)}) fusion(bf16[640,1280]{1,0:T(8,128)(2,1)} %collective-permute-done.2, bf16[640,1280]{1,0:T(8,128)(2,1)} %collective-permute-done.1, pred[]{:T(512)S(6)} %eq.133), kind=kLoop, calls=%fused_computation.2 | loop fusion | flops 1638400 | bytes 6553601 | tf_op jit(solution)/shard_map/jit(_where)/select_n | solution.py:162
  93.0 3.8 %collective-permute-start.13 = (bf16[272,640]{1,0:T(8,128)(2,1)S(1)}, bf16[272,640]{1,0:T(8,128)(2,1)S(1)}, u32[]{:S(2)}, u32[]{:S(2)}) collective-permute-start(bf16[272,640]{1,0:T(8,128)(2,1)S(1)} %fusion.5), channel_id=1, source_target_pairs={{0,128},{8,392},{128,256},{136,8},{256,384},{264,136},{384,0},{392... | collective-permute-start | bytes 1044488 | tf_op jit(solution)/shard_map/ppermute | solution.py:62
  97.4 3.1 %collective-permute-start.11 = (bf16[272,640]{1,0:T(8,128)(2,1)S(1)}, bf16[272,640]{1,0:T(8,128)(2,1)S(1)}, u32[]{:S(2)}, u32[]{:S(2)}) collective-permute-start(bf16[272,640]{1,0:T(8,128)(2,1)S(1)} %fusion.7), channel_id=1, source_target_pairs={{0,256},{8,264},{128,384},{136,392},{256,0},{264,8},{384,128},{392... | collective-permute-start | bytes 1044488 | tf_op jit(solution)/shard_map/ppermute | solution.py:62
  101.1 2.1 %collective-permute-start.12 = (bf16[272,640]{1,0:T(8,128)(2,1)S(1)}, bf16[272,640]{1,0:T(8,128)(2,1)S(1)}, u32[]{:S(2)}, u32[]{:S(2)}) collective-permute-start(bf16[272,640]{1,0:T(8,128)(2,1)S(1)} %fusion.6), channel_id=1, source_target_pairs={{0,384},{8,136},{128,0},{136,264},{256,128},{264,392},{384,256},{3... | collective-permute-start | bytes 1044488 | tf_op jit(solution)/shard_map/ppermute | solution.py:62
  104.8 6.2 %collective-permute-done.11 = bf16[272,640]{1,0:T(8,128)(2,1)S(1)} collective-permute-done((bf16[272,640]{1,0:T(8,128)(2,1)S(1)}, bf16[272,640]{1,0:T(8,128)(2,1)S(1)}, u32[]{:S(2)}, u32[]{:S(2)}) %collective-permute-start.11) | collective-permute-done | bytes 348192 | tf_op jit(solution)/shard_map/ppermute | solution.py:62
  111.0 5.5 %collective-permute-done.12 = bf16[272,640]{1,0:T(8,128)(2,1)S(1)} collective-permute-done((bf16[272,640]{1,0:T(8,128)(2,1)S(1)}, bf16[272,640]{1,0:T(8,128)(2,1)S(1)}, u32[]{:S(2)}, u32[]{:S(2)}) %collective-permute-start.12) | collective-permute-done | bytes 348192 | tf_op jit(solution)/shard_map/ppermute | solution.py:62
  118.9 1.7 %fusion.8 = bf16[1,256,1280]{2,1,0:T(8,128)(2,1)} fusion(f32[272,1280]{1,0:T(8,128)S(1)} %get-tuple-element.52, f32[272,1280]{1,0:T(8,128)S(1)} %multiply_select_fusion, f32[1280]{0:T(1024)S(1)} %get-tuple-element.40, f32[1280]{0:T(1024)S(1)} %get-tuple-element.41, f32[1280]{0:T(1024)S(1)} %get-tuple-element.42, f32[1280]{0:T(1024)S(1)} %get-tuple-element.39, ...), kind=kLoop, calls=%fused_computation.29 | loop fusion | flops 4587520 | bytes 8540160 | tf_op jit(solution)/shard_map/broadcast_in_dim | solution.py:180
  (46 shorter events, 10.6 us)
Async XLA Ops:
  0.0 15.6 %collective-permute-start.7 = (bf16[128,640]{1,0:T(8,128)(2,1)}, bf16[128,640]{1,0:T(8,128)(2,1)S(1)}, u32[]{:S(2)}, u32[]{:S(2)}) collective-permute-start(bf16[128,640]{1,0:T(8,128)(2,1)} %bitcast.59), channel_id=1, source_target_pairs={{0,1},{1,2},{2,3},{3,4},{4,5},{5,6},{6,7},{7,0},{8,9},{9,10},{10,1... | collective-permute-start | bytes 491528 | tf_op jit(solution)/shard_map/ppermute | solution.py:20
  6.4 44.5 %collective-permute-start.1 = (bf16[640,1280]{1,0:T(8,128)(2,1)S(1)}, bf16[640,1280]{1,0:T(8,128)(2,1)}, u32[]{:S(2)}, u32[]{:S(2)}) collective-permute-start(bf16[640,1280]{1,0:T(8,128)(2,1)S(1)} %select_bitcast_fusion), channel_id=1, source_target_pairs={{0,1},{1,2},{2,3},{3,4},{4,5},{5,6},{6,7},{7,0},{8,9},{9,10},{10,1... | collective-permute-start | bytes 4915208 | tf_op jit(solution)/shard_map/ppermute | solution.py:20
  16.7 43.2 %copy-start.2 = (f32[1,4,1280]{2,1,0:T(4,128)S(1)}, f32[1,4,1280]{2,1,0:T(4,128)}, u32[]{:S(2)}) copy-start(f32[1,4,1280]{2,1,0:T(4,128)} %param.13) | copy-start | bytes 61444
  16.8 48.0 %all-to-all-start = ((bf16[8,128,640]{2,1,0:T(8,128)(2,1)}), bf16[8,128,640]{2,1,0:T(8,128)(2,1)S(1)}, u32[]{:S(2)}, u32[]{:S(2)}) async-start(bf16[8,128,640]{2,1,0:T(8,128)(2,1)} %broadcast_in_dim.113), calls=%async_computation | async-start | bytes 2621440 | tf_op jit(solution)/shard_map/all_to_all | solution.py:130
  51.0 38.8 %collective-permute-start.2 = (bf16[640,1280]{1,0:T(8,128)(2,1)}, bf16[640,1280]{1,0:T(8,128)(2,1)}, u32[]{:S(2)}, u32[]{:S(2)}) collective-permute-start(bf16[640,1280]{1,0:T(8,128)(2,1)} %collective-permute-done.1), channel_id=1, source_target_pairs={{0,8},{8,0},{1,9},{9,1},{2,10},{10,2},{3,11},{11,3},{4,12},{12,4},... | collective-permute-start | bytes 4915208 | tf_op jit(solution)/shard_map/ppermute | solution.py:20
  55.4 8.8 %collective-permute-start = (bf16[32,1280]{1,0:T(8,128)(2,1)}, bf16[32,1280]{1,0:T(8,128)(2,1)S(1)}, u32[]{:S(2)}, u32[]{:S(2)}) collective-permute-start(bf16[32,1280]{1,0:T(8,128)(2,1)} %get-tuple-element.14), channel_id=1, source_target_pairs={{0,9},{1,10},{2,11},{3,12},{4,13},{5,14},{6,15},{7,8},{8,17},{9,18... | collective-permute-start | bytes 245768 | tf_op jit(solution)/shard_map/ppermute | solution.py:114
  57.3 7.0 %collective-permute-start.3 = (s32[16,256]{1,0:T(8,128)}, s32[16,256]{1,0:T(8,128)S(1)}, u32[]{:S(2)}, u32[]{:S(2)}) collective-permute-start(s32[16,256]{1,0:T(8,128)} %get-tuple-element.15), channel_id=1, source_target_pairs={{0,1},{1,2},{2,3},{3,4},{4,5},{5,6},{6,7},{7,0},{8,9},{9,10},{10,1... | collective-permute-start | bytes 49160 | tf_op jit(solution)/shard_map/ppermute | solution.py:20
  59.9 15.0 %collective-permute-start.10 = (f32[4,1280]{1,0:T(4,128)S(1)}, f32[4,1280]{1,0:T(4,128)S(1)}, u32[]{:S(2)}, u32[]{:S(2)}) collective-permute-start(f32[4,1280]{1,0:T(4,128)S(1)} %bitcast.60), channel_id=1, source_target_pairs={{0,1},{1,2},{2,3},{3,4},{4,5},{5,6},{6,7},{7,0},{8,9},{9,10},{10,1... | collective-permute-start | bytes 61448 | tf_op jit(solution)/shard_map/ppermute | solution.py:20
  64.7 27.4 %collective-permute-start.8 = (bf16[1024,640]{1,0:T(8,128)(2,1)S(1)}, bf16[1024,640]{1,0:T(8,128)(2,1)S(1)}, u32[]{:S(2)}, u32[]{:S(2)}) collective-permute-start(bf16[1024,640]{1,0:T(8,128)(2,1)S(1)} %bitcast.48), channel_id=1, source_target_pairs={{0,8},{8,0},{1,9},{9,1},{2,10},{10,2},{3,11},{11,3},{4,12},{12,4},... | collective-permute-start | bytes 3932168 | tf_op jit(solution)/shard_map/ppermute | solution.py:20
  66.8 10.7 %collective-permute-start.4 = (s32[16,272]{1,0:T(8,128)S(1)}, s32[16,272]{1,0:T(8,128)S(1)}, u32[]{:S(2)}, u32[]{:S(2)}) collective-permute-start(s32[16,272]{1,0:T(8,128)S(1)} %get-tuple-element.48), channel_id=1, source_target_pairs={{0,128},{8,392},{128,256},{136,8},{256,384},{264,136},{384,0},{392... | collective-permute-start | bytes 52232 | tf_op jit(solution)/shard_map/ppermute | solution.py:62
  72.5 8.0 %collective-permute-start.5 = (s32[16,272]{1,0:T(8,128)S(1)}, s32[16,272]{1,0:T(8,128)S(1)}, u32[]{:S(2)}, u32[]{:S(2)}) collective-permute-start(s32[16,272]{1,0:T(8,128)S(1)} %get-tuple-element.47), channel_id=1, source_target_pairs={{0,256},{8,264},{128,384},{136,392},{256,0},{264,8},{384,128},{392... | collective-permute-start | bytes 52232 | tf_op jit(solution)/shard_map/ppermute | solution.py:62
  74.9 5.8 %collective-permute-start.6 = (s32[16,272]{1,0:T(8,128)S(1)}, s32[16,272]{1,0:T(8,128)S(1)}, u32[]{:S(2)}, u32[]{:S(2)}) collective-permute-start(s32[16,272]{1,0:T(8,128)S(1)} %get-tuple-element.46), channel_id=1, source_target_pairs={{0,384},{8,136},{128,0},{136,264},{256,128},{264,392},{384,256},{3... | collective-permute-start | bytes 52232 | tf_op jit(solution)/shard_map/ppermute | solution.py:62
  77.6 26.9 %collective-permute-start.9 = (bf16[256,1280]{1,0:T(8,128)(2,1)}, bf16[256,1280]{1,0:T(8,128)(2,1)S(1)}, u32[]{:S(2)}, u32[]{:S(2)}) collective-permute-start(bf16[256,1280]{1,0:T(8,128)(2,1)} %bitcast.53), channel_id=1, source_target_pairs={{0,1},{1,2},{2,3},{3,4},{4,5},{5,6},{6,7},{7,0},{8,9},{9,10},{10,1... | collective-permute-start | bytes 1966088 | tf_op jit(solution)/shard_map/ppermute | solution.py:20
  89.8 2.6 %copy-start = (bf16[4,272,1024]{2,1,0:T(8,128)(2,1)S(1)}, bf16[4,272,1024]{2,1,0:T(8,128)(2,1)}, u32[]{:S(2)}) copy-start(bf16[4,272,1024]{2,1,0:T(8,128)(2,1)} %get-tuple-element.17) | copy-start | bytes 6684676
  93.0 23.6 %collective-permute-start.13 = (bf16[272,640]{1,0:T(8,128)(2,1)S(1)}, bf16[272,640]{1,0:T(8,128)(2,1)S(1)}, u32[]{:S(2)}, u32[]{:S(2)}) collective-permute-start(bf16[272,640]{1,0:T(8,128)(2,1)S(1)} %fusion.5), channel_id=1, source_target_pairs={{0,128},{8,392},{128,256},{136,8},{256,384},{264,136},{384,0},{392... | collective-permute-start | bytes 1044488 | tf_op jit(solution)/shard_map/ppermute | solution.py:62
  97.4 13.6 %collective-permute-start.11 = (bf16[272,640]{1,0:T(8,128)(2,1)S(1)}, bf16[272,640]{1,0:T(8,128)(2,1)S(1)}, u32[]{:S(2)}, u32[]{:S(2)}) collective-permute-start(bf16[272,640]{1,0:T(8,128)(2,1)S(1)} %fusion.7), channel_id=1, source_target_pairs={{0,256},{8,264},{128,384},{136,392},{256,0},{264,8},{384,128},{392... | collective-permute-start | bytes 1044488 | tf_op jit(solution)/shard_map/ppermute | solution.py:62
  101.1 2.7 %copy-start.1 = (bf16[272,1024]{1,0:T(8,128)(2,1)S(1)}, bf16[272,1024]{1,0:T(8,128)(2,1)}, u32[]{:S(2)}) copy-start(bf16[272,1024]{1,0:T(8,128)(2,1)} %get-tuple-element.16) | copy-start | bytes 1671172
  101.1 15.3 %collective-permute-start.12 = (bf16[272,640]{1,0:T(8,128)(2,1)S(1)}, bf16[272,640]{1,0:T(8,128)(2,1)S(1)}, u32[]{:S(2)}, u32[]{:S(2)}) collective-permute-start(bf16[272,640]{1,0:T(8,128)(2,1)S(1)} %fusion.6), channel_id=1, source_target_pairs={{0,384},{8,136},{128,0},{136,264},{256,128},{264,392},{384,256},{3... | collective-permute-start | bytes 1044488 | tf_op jit(solution)/shard_map/ppermute | solution.py:62

commit v7 on v6

--- a/solution.py
+++ b/solution.py
@@ -123,7 +123,6 @@
     states = rotated(hidden[0], "segment", 1)
     weight_one = jnp.where(core == 0, key_weight[0], value_weight[0])
     weight_one = rotated(weight_one, "segment", 1)
-    weight_two = rotated(weight_one, "core", 1)
     taps = rotated(conv_weight[0], "segment", 1)
 
     copies = jnp.broadcast_to(table[None], (NY, rows_dev, row_features))
@@ -148,6 +147,8 @@
         received.append(along_x(asked[group], (GROUPS[0][group], GROUPS[1][group])))
     asked = jnp.stack(received).transpose(0, 2, 1)
     pick_sent, pick_mine, pick_other = pick_matrices(asked, rows_dev)
+    pick_sent, weight_one = lax.optimization_barrier((pick_sent, weight_one))
+    weight_two = rotated(weight_one, "core", 1)
 
     rows = tok_rows + HALO
     own_part = jnp.dot(pick_sent, own_rows, preferred_element_type=jnp.float32).reshape(NX - 1, rows, -1)
@@ -161,8 +162,9 @@
     key_here = jnp.where(core == 0, weight_one, weight_two)
     value_here = jnp.where(core == 0, weight_two, weight_one)
     key_here, value_here, total, states = lax.optimization_barrier((key_here, value_here, total, states))
-    total = lax.optimization_barrier(total + sums[0].astype(jnp.float32) + sums[1].astype(jnp.float32))
-    packed = (total + sums[2].astype(jnp.float32)).astype(bf16)
+    for part in sums:
+        total = total + part.astype(jnp.float32)
+    packed = total.astype(bf16)
 
     states_float = jnp.concatenate([tail[:HALO], states], axis=0).astype(jnp.float32)
     keys_out = jnp.dot(packed, key_here, preferred_element_type=jnp.float32)

time: 122 us -> 168 us (1.38)
  the two profiles are of different devices: /device:TPU:1 before, /device:TPU:40 now
where the time goes in v7:
time: 168 us; the launch traced here: 167 us
  waiting for transfers between devices  95.3 us (57%)
  starting transfers between devices  47.8 us (28%)
  matrix products  7.59 us (5%)
  other arithmetic  7.31 us (4%)
  Pallas kernels  6.55 us (4%)
  local copies, waits for them, and re-layouts  2.58 us (2%)
    ppermute x7, waiting for transfers between devices, rotated(): lax.ppermute(value, axis, [(i, (i + by) % count) for i in range(count)])  57.6 us
    ppermute x1, waiting for transfers between devices, local(): lax.ppermute(tail, TABLE + ('segment',), [(i * sections + s, (i + 1) * se...  25.7 us
    ppermute x6, starting transfers between devices, along_x(): return lax.ppermute(value, ('x', 'core'), pairs)  19.6 us
    ppermute x7, starting transfers between devices, rotated(): lax.ppermute(value, axis, [(i, (i + by) % count) for i in range(count)])  19.2 us
    ppermute x6, waiting for transfers between devices, along_x(): return lax.ppermute(value, ('x', 'core'), pairs)  12 us
    all_to_all x1, starting transfers between devices, local(): lax.all_to_all(copies, 'y', split_axis=0, concat_axis=0, tiled=True)  7.09 us
    pallas_call x1, Pallas kernels, pick_matrices(): pl.pallas_call(body, in_specs=[VMEM], out_specs=[VMEM] * 3, out_shape=[ja...  5.1 us
  transfers between devices with their start and end apart: 15, of which 8 were waited for; matrix products, arithmetic and copies ran while one was open for 7% of the time, Pallas kernels for 4%

profile of v7, /device:TPU:40, one launch (start us, length us, event | category | flops | bytes accessed | tf_op | source)
XLA Modules:
  0.0 167.5 jit_solution(12968404438354819845)
XLA Ops:
  1.6 4.3 %collective-permute-start.5 = (bf16[640,1280]{1,0:T(8,128)(2,1)S(1)}, bf16[640,1280]{1,0:T(8,128)(2,1)}, u32[]{:S(2)}, u32[]{:S(2)}) collective-permute-start(bf16[640,1280]{1,0:T(8,128)(2,1)S(1)} %select_bitcast_fusion), channel_id=1, source_target_pairs={{0,1},{1,2},{2,3},{3,4},{4,5},{5,6},{6,7},{7,0},{8,9},{9,10},{10,1... | collective-permute-start | bytes 4915208 | tf_op jit(solution)/shard_map/ppermute | solution.py:20
  5.9 4.3 %collective-permute-start.7 = (bf16[128,640]{1,0:T(8,128)(2,1)S(1)}, bf16[128,640]{1,0:T(8,128)(2,1)S(1)}, u32[]{:S(2)}, u32[]{:S(2)}) collective-permute-start(bf16[128,640]{1,0:T(8,128)(2,1)S(1)} %bitcast.61), channel_id=1, source_target_pairs={{0,1},{1,2},{2,3},{3,4},{4,5},{5,6},{6,7},{7,0},{8,9},{9,10},{10,1... | collective-permute-start | bytes 491528 | tf_op jit(solution)/shard_map/ppermute | solution.py:20
  10.2 41.7 %collective-permute-done.7 = bf16[128,640]{1,0:T(8,128)(2,1)S(1)} collective-permute-done((bf16[128,640]{1,0:T(8,128)(2,1)S(1)}, bf16[128,640]{1,0:T(8,128)(2,1)S(1)}, u32[]{:S(2)}, u32[]{:S(2)}) %collective-permute-start.7) | collective-permute-done | bytes 163872 | tf_op jit(solution)/shard_map/ppermute | solution.py:20
  53.1 7.1 %all-to-all-start = ((bf16[8,128,640]{2,1,0:T(8,128)(2,1)}), bf16[8,128,640]{2,1,0:T(8,128)(2,1)S(1)}, u32[]{:S(2)}, u32[]{:S(2)}) async-start(bf16[8,128,640]{2,1,0:T(8,128)(2,1)} %broadcast_in_dim.113), calls=%async_computation | async-start | bytes 2621440 | tf_op jit(solution)/shard_map/all_to_all | solution.py:129
  63.6 1.9 %collective-permute-start = (bf16[32,1280]{1,0:T(8,128)(2,1)}, bf16[32,1280]{1,0:T(8,128)(2,1)S(1)}, u32[]{:S(2)}, u32[]{:S(2)}) collective-permute-start(bf16[32,1280]{1,0:T(8,128)(2,1)} %get-tuple-element.16), channel_id=1, source_target_pairs={{0,9},{1,10},{2,11},{3,12},{4,13},{5,14},{6,15},{7,8},{8,17},{9,18... | collective-permute-start | bytes 245768 | tf_op jit(solution)/shard_map/ppermute | solution.py:114
  65.5 25.7 %collective-permute-done = bf16[32,1280]{1,0:T(8,128)(2,1)S(1)} collective-permute-done((bf16[32,1280]{1,0:T(8,128)(2,1)}, bf16[32,1280]{1,0:T(8,128)(2,1)S(1)}, u32[]{:S(2)}, u32[]{:S(2)}) %collective-permute-start) | collective-permute-done | bytes 81952 | tf_op jit(solution)/shard_map/ppermute | solution.py:114
  91.8 4.7 %collective-permute-start.4 = (s32[16,272]{1,0:T(8,128)S(1)}, s32[16,272]{1,0:T(8,128)S(1)}, u32[]{:S(2)}, u32[]{:S(2)}) collective-permute-start(s32[16,272]{1,0:T(8,128)S(1)} %get-tuple-element.50), channel_id=1, source_target_pairs={{0,384},{8,136},{128,0},{136,264},{256,128},{264,392},{384,256},{3... | collective-permute-start | bytes 52232 | tf_op jit(solution)/shard_map/ppermute | solution.py:62
  96.4 2.7 %collective-permute-start.3 = (s32[16,272]{1,0:T(8,128)S(1)}, s32[16,272]{1,0:T(8,128)S(1)}, u32[]{:S(2)}, u32[]{:S(2)}) collective-permute-start(s32[16,272]{1,0:T(8,128)S(1)} %get-tuple-element.51), channel_id=1, source_target_pairs={{0,256},{8,264},{128,384},{136,392},{256,0},{264,8},{384,128},{392... | collective-permute-start | bytes 52232 | tf_op jit(solution)/shard_map/ppermute | solution.py:62
  99.2 2.8 %collective-permute-start.2 = (s32[16,272]{1,0:T(8,128)S(1)}, s32[16,272]{1,0:T(8,128)S(1)}, u32[]{:S(2)}, u32[]{:S(2)}) collective-permute-start(s32[16,272]{1,0:T(8,128)S(1)} %get-tuple-element.52), channel_id=1, source_target_pairs={{0,128},{8,392},{128,256},{136,8},{256,384},{264,136},{384,0},{392... | collective-permute-start | bytes 52232 | tf_op jit(solution)/shard_map/ppermute | solution.py:62
  103.7 2.4 %collective-permute-done.2 = s32[16,272]{1,0:T(8,128)S(1)} collective-permute-done((s32[16,272]{1,0:T(8,128)S(1)}, s32[16,272]{1,0:T(8,128)S(1)}, u32[]{:S(2)}, u32[]{:S(2)}) %collective-permute-start.2) | collective-permute-done | bytes 17440 | tf_op jit(solution)/shard_map/ppermute | solution.py:62
  107.1 5.1 %pick_matrices.1 = (bf16[816,1024]{1,0:T(8,128)(2,1)}, bf16[272,1024]{1,0:T(8,128)(2,1)}, bf16[4,272,1024]{2,1,0:T(8,128)(2,1)}) custom-call(s32[4,272,16]{2,1,0:T(8,128)} %bitcast.53), custom_call_target="tpu_custom_call" | custom-call | tf_op jit(solution)/shard_map/pick_matrices/pallas_call | solution.py:44
  112.2 1.9 %collective-permute-start.6 = (bf16[640,1280]{1,0:T(8,128)(2,1)}, bf16[640,1280]{1,0:T(8,128)(2,1)}, u32[]{:S(2)}, u32[]{:S(2)}) collective-permute-start(bf16[640,1280]{1,0:T(8,128)(2,1)} %collective-permute-done.5), channel_id=1, source_target_pairs={{0,8},{8,0},{1,9},{9,1},{2,10},{10,2},{3,11},{11,3},{4,12},{12,4},... | collective-permute-start | bytes 4915208 | tf_op jit(solution)/shard_map/ppermute | solution.py:20
  114.1 2.4 %collective-permute-start.8 = (bf16[1024,640]{1,0:T(8,128)(2,1)S(1)}, bf16[1024,640]{1,0:T(8,128)(2,1)S(1)}, u32[]{:S(2)}, u32[]{:S(2)}) collective-permute-start(bf16[1024,640]{1,0:T(8,128)(2,1)S(1)} %bitcast.50), channel_id=1, source_target_pairs={{0,8},{8,0},{1,9},{9,1},{2,10},{10,2},{3,11},{11,3},{4,12},{12,4},... | collective-permute-start | bytes 3932168 | tf_op jit(solution)/shard_map/ppermute | solution.py:20
  116.6 2.5 %collective-permute-start.9 = (bf16[256,1280]{1,0:T(8,128)(2,1)}, bf16[256,1280]{1,0:T(8,128)(2,1)S(1)}, u32[]{:S(2)}, u32[]{:S(2)}) collective-permute-start(bf16[256,1280]{1,0:T(8,128)(2,1)} %bitcast.55), channel_id=1, source_target_pairs={{0,1},{1,2},{2,3},{3,4},{4,5},{5,6},{6,7},{7,0},{8,9},{9,10},{10,1... | collective-permute-start | bytes 1966088 | tf_op jit(solution)/shard_map/ppermute | solution.py:20
  119.1 1.9 %collective-permute-start.10 = (f32[4,1280]{1,0:T(4,128)S(1)}, f32[4,1280]{1,0:T(4,128)S(1)}, u32[]{:S(2)}, u32[]{:S(2)}) collective-permute-start(f32[4,1280]{1,0:T(4,128)S(1)} %bitcast.62), channel_id=1, source_target_pairs={{0,1},{1,2},{2,3},{3,4},{4,5},{5,6},{6,7},{7,0},{8,9},{9,10},{10,1... | collective-permute-start | bytes 61448 | tf_op jit(solution)/shard_map/ppermute | solution.py:20
  121.0 15.9 %collective-permute-done.10 = f32[4,1280]{1,0:T(4,128)S(1)} collective-permute-done((f32[4,1280]{1,0:T(4,128)S(1)}, f32[4,1280]{1,0:T(4,128)S(1)}, u32[]{:S(2)}, u32[]{:S(2)}) %collective-permute-start.10) | collective-permute-done | bytes 20512 | tf_op jit(solution)/shard_map/ppermute | solution.py:20
  137.0 2.9 %fusion.68 = f32[816,640]{1,0:T(8,128)S(1)} fusion(bf16[816,1024]{1,0:T(8,128)(2,1)} %get-tuple-element.24, bf16[1024,640]{1,0:T(8,128)(2,1)S(1)} %bitcast.51), kind=kOutput, calls=%fused_computation.145 | convolution fusion | flops 1069547520 | bytes 5070848 | tf_op jit(solution)/shard_map/dot_general | solution.py:154
  140.0 2.3 %broadcast_select_fusion = (bf16[640,1280]{1,0:T(8,128)(2,1)S(1)}, bf16[640,1280]{1,0:T(8,128)(2,1)S(1)}) fusion(bf16[640,1280]{1,0:T(8,128)(2,1)} %collective-permute-done.6, bf16[640,1280]{1,0:T(8,128)(2,1)} %collective-permute-done.5, pred[]{:T(512)S(6)} %eq.133), kind=kLoop, calls=%fused_computation.2 | loop fusion | flops 1638400 | bytes 6553601 | tf_op jit(solution)/shard_map/jit(_where)/select_n | solution.py:163
  143.2 3.4 %collective-permute-start.11 = (bf16[272,640]{1,0:T(8,128)(2,1)S(1)}, bf16[272,640]{1,0:T(8,128)(2,1)S(1)}, u32[]{:S(2)}, u32[]{:S(2)}) collective-permute-start(bf16[272,640]{1,0:T(8,128)(2,1)S(1)} %fusion.7), channel_id=1, source_target_pairs={{0,256},{8,264},{128,384},{136,392},{256,0},{264,8},{384,128},{392... | collective-permute-start | bytes 1044488 | tf_op jit(solution)/shard_map/ppermute | solution.py:62
  147.2 2.7 %collective-permute-start.12 = (bf16[272,640]{1,0:T(8,128)(2,1)S(1)}, bf16[272,640]{1,0:T(8,128)(2,1)S(1)}, u32[]{:S(2)}, u32[]{:S(2)}) collective-permute-start(bf16[272,640]{1,0:T(8,128)(2,1)S(1)} %fusion.6), channel_id=1, source_target_pairs={{0,384},{8,136},{128,0},{136,264},{256,128},{264,392},{384,256},{3... | collective-permute-start | bytes 1044488 | tf_op jit(solution)/shard_map/ppermute | solution.py:62
  150.6 3.2 %collective-permute-start.13 = (bf16[272,640]{1,0:T(8,128)(2,1)S(1)}, bf16[272,640]{1,0:T(8,128)(2,1)S(1)}, u32[]{:S(2)}, u32[]{:S(2)}) collective-permute-start(bf16[272,640]{1,0:T(8,128)(2,1)S(1)} %fusion.5), channel_id=1, source_target_pairs={{0,128},{8,392},{128,256},{136,8},{256,384},{264,136},{384,0},{392... | collective-permute-start | bytes 1044488 | tf_op jit(solution)/shard_map/ppermute | solution.py:62
  155.4 2.2 %collective-permute-done.11 = bf16[272,640]{1,0:T(8,128)(2,1)S(1)} collective-permute-done((bf16[272,640]{1,0:T(8,128)(2,1)S(1)}, bf16[272,640]{1,0:T(8,128)(2,1)S(1)}, u32[]{:S(2)}, u32[]{:S(2)}) %collective-permute-start.11) | collective-permute-done | bytes 348192 | tf_op jit(solution)/shard_map/ppermute | solution.py:62
  157.6 2.9 %collective-permute-done.12 = bf16[272,640]{1,0:T(8,128)(2,1)S(1)} collective-permute-done((bf16[272,640]{1,0:T(8,128)(2,1)S(1)}, bf16[272,640]{1,0:T(8,128)(2,1)S(1)}, u32[]{:S(2)}, u32[]{:S(2)}) %collective-permute-start.12) | collective-permute-done | bytes 348192 | tf_op jit(solution)/shard_map/ppermute | solution.py:62
  160.5 2.7 %collective-permute-done.13 = bf16[272,640]{1,0:T(8,128)(2,1)S(1)} collective-permute-done((bf16[272,640]{1,0:T(8,128)(2,1)S(1)}, bf16[272,640]{1,0:T(8,128)(2,1)S(1)}, u32[]{:S(2)}, u32[]{:S(2)}) %collective-permute-start.13) | collective-permute-done | bytes 348192 | tf_op jit(solution)/shard_map/ppermute | solution.py:62
  (47 shorter events, 17.4 us)
Async XLA Ops:
  0.0 5.9 %copy-start.2 = (bf16[1,128,640]{2,1,0:T(8,128)(2,1)S(1)}, bf16[1,128,640]{2,1,0:T(8,128)(2,1)}, u32[]{:S(2)}) copy-start(bf16[1,128,640]{2,1,0:T(8,128)(2,1)} %param.10) | copy-start | bytes 491524
  1.6 110.6 %collective-permute-start.5 = (bf16[640,1280]{1,0:T(8,128)(2,1)S(1)}, bf16[640,1280]{1,0:T(8,128)(2,1)}, u32[]{:S(2)}, u32[]{:S(2)}) collective-permute-start(bf16[640,1280]{1,0:T(8,128)(2,1)S(1)} %select_bitcast_fusion), channel_id=1, source_target_pairs={{0,1},{1,2},{2,3},{3,4},{4,5},{5,6},{6,7},{7,0},{8,9},{9,10},{10,1... | collective-permute-start | bytes 4915208 | tf_op jit(solution)/shard_map/ppermute | solution.py:20
  5.9 45.9 %collective-permute-start.7 = (bf16[128,640]{1,0:T(8,128)(2,1)S(1)}, bf16[128,640]{1,0:T(8,128)(2,1)S(1)}, u32[]{:S(2)}, u32[]{:S(2)}) collective-permute-start(bf16[128,640]{1,0:T(8,128)(2,1)S(1)} %bitcast.61), channel_id=1, source_target_pairs={{0,1},{1,2},{2,3},{3,4},{4,5},{5,6},{6,7},{7,0},{8,9},{9,10},{10,1... | collective-permute-start | bytes 491528 | tf_op jit(solution)/shard_map/ppermute | solution.py:20
  53.1 61.0 %all-to-all-start = ((bf16[8,128,640]{2,1,0:T(8,128)(2,1)}), bf16[8,128,640]{2,1,0:T(8,128)(2,1)S(1)}, u32[]{:S(2)}, u32[]{:S(2)}) async-start(bf16[8,128,640]{2,1,0:T(8,128)(2,1)} %broadcast_in_dim.113), calls=%async_computation | async-start | bytes 2621440 | tf_op jit(solution)/shard_map/all_to_all | solution.py:129
  60.2 58.9 %copy-start.3 = (f32[1,4,1280]{2,1,0:T(4,128)S(1)}, f32[1,4,1280]{2,1,0:T(4,128)}, u32[]{:S(2)}) copy-start(f32[1,4,1280]{2,1,0:T(4,128)} %param.13) | copy-start | bytes 61444
  61.6 29.7 %collective-permute-start.1 = (s32[16,256]{1,0:T(8,128)}, s32[16,256]{1,0:T(8,128)S(1)}, u32[]{:S(2)}, u32[]{:S(2)}) collective-permute-start(s32[16,256]{1,0:T(8,128)} %get-tuple-element.17), channel_id=1, source_target_pairs={{0,1},{1,2},{2,3},{3,4},{4,5},{5,6},{6,7},{7,0},{8,9},{9,10},{10,1... | collective-permute-start | bytes 49160 | tf_op jit(solution)/shard_map/ppermute | solution.py:20
  63.6 27.7 %collective-permute-start = (bf16[32,1280]{1,0:T(8,128)(2,1)}, bf16[32,1280]{1,0:T(8,128)(2,1)S(1)}, u32[]{:S(2)}, u32[]{:S(2)}) collective-permute-start(bf16[32,1280]{1,0:T(8,128)(2,1)} %get-tuple-element.16), channel_id=1, source_target_pairs={{0,9},{1,10},{2,11},{3,12},{4,13},{5,14},{6,15},{7,8},{8,17},{9,18... | collective-permute-start | bytes 245768 | tf_op jit(solution)/shard_map/ppermute | solution.py:114
  91.8 10.2 %collective-permute-start.4 = (s32[16,272]{1,0:T(8,128)S(1)}, s32[16,272]{1,0:T(8,128)S(1)}, u32[]{:S(2)}, u32[]{:S(2)}) collective-permute-start(s32[16,272]{1,0:T(8,128)S(1)} %get-tuple-element.50), channel_id=1, source_target_pairs={{0,384},{8,136},{128,0},{136,264},{256,128},{264,392},{384,256},{3... | collective-permute-start | bytes 52232 | tf_op jit(solution)/shard_map/ppermute | solution.py:62
  96.4 7.2 %collective-permute-start.3 = (s32[16,272]{1,0:T(8,128)S(1)}, s32[16,272]{1,0:T(8,128)S(1)}, u32[]{:S(2)}, u32[]{:S(2)}) collective-permute-start(s32[16,272]{1,0:T(8,128)S(1)} %get-tuple-element.51), channel_id=1, source_target_pairs={{0,256},{8,264},{128,384},{136,392},{256,0},{264,8},{384,128},{392... | collective-permute-start | bytes 52232 | tf_op jit(solution)/shard_map/ppermute | solution.py:62
  99.2 6.9 %collective-permute-start.2 = (s32[16,272]{1,0:T(8,128)S(1)}, s32[16,272]{1,0:T(8,128)S(1)}, u32[]{:S(2)}, u32[]{:S(2)}) collective-permute-start(s32[16,272]{1,0:T(8,128)S(1)} %get-tuple-element.52), channel_id=1, source_target_pairs={{0,128},{8,392},{128,256},{136,8},{256,384},{264,136},{384,0},{392... | collective-permute-start | bytes 52232 | tf_op jit(solution)/shard_map/ppermute | solution.py:62
  112.2 27.7 %collective-permute-start.6 = (bf16[640,1280]{1,0:T(8,128)(2,1)}, bf16[640,1280]{1,0:T(8,128)(2,1)}, u32[]{:S(2)}, u32[]{:S(2)}) collective-permute-start(bf16[640,1280]{1,0:T(8,128)(2,1)} %collective-permute-done.5), channel_id=1, source_target_pairs={{0,8},{8,0},{1,9},{9,1},{2,10},{10,2},{3,11},{11,3},{4,12},{12,4},... | collective-permute-start | bytes 4915208 | tf_op jit(solution)/shard_map/ppermute | solution.py:20
  114.1 28.1 %collective-permute-start.8 = (bf16[1024,640]{1,0:T(8,128)(2,1)S(1)}, bf16[1024,640]{1,0:T(8,128)(2,1)S(1)}, u32[]{:S(2)}, u32[]{:S(2)}) collective-permute-start(bf16[1024,640]{1,0:T(8,128)(2,1)S(1)} %bitcast.50), channel_id=1, source_target_pairs={{0,8},{8,0},{1,9},{9,1},{2,10},{10,2},{3,11},{11,3},{4,12},{12,4},... | collective-permute-start | bytes 3932168 | tf_op jit(solution)/shard_map/ppermute | solution.py:20
  116.6 38.5 %collective-permute-start.9 = (bf16[256,1280]{1,0:T(8,128)(2,1)}, bf16[256,1280]{1,0:T(8,128)(2,1)S(1)}, u32[]{:S(2)}, u32[]{:S(2)}) collective-permute-start(bf16[256,1280]{1,0:T(8,128)(2,1)} %bitcast.55), channel_id=1, source_target_pairs={{0,1},{1,2},{2,3},{3,4},{4,5},{5,6},{6,7},{7,0},{8,9},{9,10},{10,1... | collective-permute-start | bytes 1966088 | tf_op jit(solution)/shard_map/ppermute | solution.py:20
  119.1 17.9 %collective-permute-start.10 = (f32[4,1280]{1,0:T(4,128)S(1)}, f32[4,1280]{1,0:T(4,128)S(1)}, u32[]{:S(2)}, u32[]{:S(2)}) collective-permute-start(f32[4,1280]{1,0:T(4,128)S(1)} %bitcast.62), channel_id=1, source_target_pairs={{0,1},{1,2},{2,3},{3,4},{4,5},{5,6},{6,7},{7,0},{8,9},{9,10},{10,1... | collective-permute-start | bytes 61448 | tf_op jit(solution)/shard_map/ppermute | solution.py:20
  139.9 2.6 %copy-start = (bf16[4,272,1024]{2,1,0:T(8,128)(2,1)S(1)}, bf16[4,272,1024]{2,1,0:T(8,128)(2,1)}, u32[]{:S(2)}) copy-start(bf16[4,272,1024]{2,1,0:T(8,128)(2,1)} %get-tuple-element.21) | copy-start | bytes 6684676
  143.2 14.5 %collective-permute-start.11 = (bf16[272,640]{1,0:T(8,128)(2,1)S(1)}, bf16[272,640]{1,0:T(8,128)(2,1)S(1)}, u32[]{:S(2)}, u32[]{:S(2)}) collective-permute-start(bf16[272,640]{1,0:T(8,128)(2,1)S(1)} %fusion.7), channel_id=1, source_target_pairs={{0,256},{8,264},{128,384},{136,392},{256,0},{264,8},{384,128},{392... | collective-permute-start | bytes 1044488 | tf_op jit(solution)/shard_map/ppermute | solution.py:62
  147.2 13.3 %collective-permute-start.12 = (bf16[272,640]{1,0:T(8,128)(2,1)S(1)}, bf16[272,640]{1,0:T(8,128)(2,1)S(1)}, u32[]{:S(2)}, u32[]{:S(2)}) collective-permute-start(bf16[272,640]{1,0:T(8,128)(2,1)S(1)} %fusion.6), channel_id=1, source_target_pairs={{0,384},{8,136},{128,0},{136,264},{256,128},{264,392},{384,256},{3... | collective-permute-start | bytes 1044488 | tf_op jit(solution)/shard_map/ppermute | solution.py:62
  150.5 3.9 %copy-start.1 = (bf16[272,1024]{1,0:T(8,128)(2,1)S(1)}, bf16[272,1024]{1,0:T(8,128)(2,1)}, u32[]{:S(2)}) copy-start(bf16[272,1024]{1,0:T(8,128)(2,1)} %get-tuple-element.20) | copy-start | bytes 1671172
  150.6 12.7 %collective-permute-start.13 = (bf16[272,640]{1,0:T(8,128)(2,1)S(1)}, bf16[272,640]{1,0:T(8,128)(2,1)S(1)}, u32[]{:S(2)}, u32[]{:S(2)}) collective-permute-start(bf16[272,640]{1,0:T(8,128)(2,1)S(1)} %fusion.5), channel_id=1, source_target_pairs={{0,128},{8,392},{128,256},{136,8},{256,384},{264,136},{384,0},{392... | collective-permute-start | bytes 1044488 | tf_op jit(solution)/shard_map/ppermute | solution.py:62
